TPU v7x, 512 devices: a whole 4x8x8 slice. The times are simulated.
512 devices in a mesh: space: 32 (over y, z_hi), tensor: 16 (over x, z_lo, core).
Axes of the slice: x: 4, y: 8, z: 8 (z_hi: 4, z_lo: 2; z = z_hi * 2 + z_lo), core: 2. Of those that a mesh axis runs over, the one named last changes fastest.
Arguments:
- features: bfloat16 [128, 128, 1024], P('space', None, 'tensor'), may hold values from -6 to 6
- depth_kernel: bfloat16 [2, 7, 7, 1024], P(None, None, None, 'tensor'), may hold values from -5 to 5
- norm_gain: float32 [2, 1024], replicated, may hold values from 0.5 to 1.5
- norm_bias: float32 [2, 1024], replicated, may hold values from -3 to 3
- w_expand: bfloat16 [2, 1024, 4096], P(None, None, 'tensor'), may hold values from -0.1875 to 0.1875
- b_expand: float32 [2, 4096], P(None, 'tensor'), may hold values from -3 to 3
- w_reduce: bfloat16 [2, 4096, 1024], P(None, 'tensor'), may hold values from -0.125 to 0.125
- b_reduce: float32 [2, 1024], P(None, 'tensor'), may hold values from -3 to 3
- layer_scale: float32 [2, 1024], P(None, 'tensor'), may hold values from 0.5 to 1.5
Outputs:
- output: bfloat16 [128, 128, 1024], P('space', None, 'tensor')
All inputs are finite; a program needn't handle non-finite values.
Results may differ from a plain program's by a relative error of at most 0.023.
Values may be sent and summed in bfloat16 or wider, within the bound.
No kernel may reach another device: no remote copies, remote signals or barrier semaphores. Data moves between devices by JAX's collectives and lax.ppermute only.
A program may use at most 64 MiB of HBM per device.

v0:
```python
import jax
import jax.numpy as jnp
from jax import lax
from jax.sharding import PartitionSpec as P

D = 1024
TAPS = 7
BLOCKS = 2


def with_halo(x, sides, width):
    for axis, dim in sides:
        devices, length = (lax.axis_size(axis), x.shape[dim])
        up = [(i, (i + 1) % devices) for i in range(devices - 1)]
        down = [(j, i) for i, j in up]
        last = lax.slice_in_dim(x, length - width, length, axis=dim)
        leading = lax.slice_in_dim(x, 0, width, axis=dim)
        before = lax.ppermute(last, axis, up)
        after = lax.ppermute(leading, axis, down)
        x = jnp.concatenate([before, x, after], axis=dim)
    return x


def one_block(stream, kernel, gain, bias, expand, bias_expand, reduce_w, bias_reduce, scale):
    half = TAPS // 2
    height, width, share = stream.shape
    positions = height * width
    padded = with_halo(stream, (("space", 0),), half)
    padded = jnp.pad(padded.astype(jnp.float32), ((0, 0), (half, half), (0, 0)))
    filtered = jnp.zeros(stream.shape, jnp.float32)
    for row_tap in range(TAPS):
        for col_tap in range(TAPS):
            filtered = filtered + padded[
                row_tap : row_tap + height, col_tap : col_tap + width
            ] * kernel[row_tap, col_tap].astype(jnp.float32)
    filtered = filtered.reshape(positions, share)
    offset = lax.axis_index("tensor") * share
    gain_part = lax.dynamic_slice_in_dim(gain, offset, share, 0)
    bias_part = lax.dynamic_slice_in_dim(bias, offset, share, 0)
    sums, squares = lax.psum(
        (jnp.sum(filtered, axis=-1), jnp.sum(filtered * filtered, axis=-1)), "tensor"
    )
    mean = (sums / D)[:, None]
    var = jnp.maximum(squares[:, None] / D - mean * mean, 0.0)
    normed_part = ((filtered - mean) / jnp.sqrt(var + 1e-06) * gain_part + bias_part).astype(
        jnp.bfloat16
    )
    preact = jnp.dot(
        lax.all_gather(normed_part, "tensor", axis=1, tiled=True),
        expand,
        preferred_element_type=jnp.float32,
    )
    hidden = jax.nn.gelu(preact + bias_expand, approximate=False).astype(jnp.bfloat16)
    partial_value = jnp.dot(hidden, reduce_w, preferred_element_type=jnp.float32)
    mixed = lax.psum_scatter(
        partial_value.astype(jnp.bfloat16), "tensor", scatter_dimension=1, tiled=True
    ).astype(jnp.float32)
    updated = stream.reshape(positions, share).astype(jnp.float32) + scale * (mixed + bias_reduce)
    return updated.astype(jnp.bfloat16).reshape(height, width, share)


def per_device(
    features,
    depth_kernel,
    norm_gain,
    norm_bias,
    w_expand,
    b_expand,
    w_reduce,
    b_reduce,
    layer_scale,
):
    stream = features
    for block_id in range(BLOCKS):
        stream = one_block(
            stream,
            depth_kernel[block_id],
            norm_gain[block_id],
            norm_bias[block_id],
            w_expand[block_id],
            b_expand[block_id],
            w_reduce[block_id],
            b_reduce[block_id],
            layer_scale[block_id],
        )
    return stream


def solution(mesh):
    return jax.shard_map(
        per_device,
        mesh=mesh,
        in_specs=(
            P("space", None, "tensor"),
            P(None, None, None, "tensor"),
            P(),
            P(),
            P(None, None, "tensor"),
            P(None, "tensor"),
            P(None, "tensor", None),
            P(None, "tensor"),
            P(None, "tensor"),
        ),
        out_specs=P("space", None, "tensor"),
        check_vma=False,
    )
```

profile of v0, /device:TPU:56, one launch (start us, length us, event | category | flops | bytes accessed | tf_op | source)
XLA Modules:
  0.0 326.5 jit_solution(3460924509859641475)
XLA Ops:
  6.5 0.0 all-gather.3.cloned.1.call-start
  6.5 0.9 fusion.455
  7.4 6.1 %collective-permute-start = (bf16[3,128,64]{1,2,0:T(8,128)(2,1)S(1)}, bf16[3,128,64]{1,2,0:T(8,128)(2,1)S(1)}, u32[]{:S(2)}, u32[]{:S(2)}) collective-permute-start(bf16[3,128,64]{1,2,0:T(8,128)(2,1)S(1)} %get-tuple-element.17), channel_id=1, source_target_pairs={{0,16},{16,32},{32,48},{48,64},{64,80},{80,96},{96,112},{112,128},... | collective-permute-start | bytes 147464 | tf_op jit(solution)/shard_map/ppermute | solution.py:18
  13.5 7.6 %collective-permute-start.1 = (bf16[3,128,64]{1,2,0:T(8,128)(2,1)S(1)}, bf16[3,128,64]{1,2,0:T(8,128)(2,1)S(1)}, u32[]{:S(2)}, u32[]{:S(2)}) collective-permute-start(bf16[3,128,64]{1,2,0:T(8,128)(2,1)S(1)} %get-tuple-element.18), channel_id=1, source_target_pairs={{16,0},{32,16},{48,32},{64,48},{80,64},{96,80},{112,96},{128,112},... | collective-permute-start | bytes 147464 | tf_op jit(solution)/shard_map/ppermute | solution.py:19
  21.1 0.9 fusion.456
  22.0 0.8 fusion.457
  22.8 0.8 fusion.458
  23.6 0.1 fusion.288
  23.7 0.0 copy-start.1
  23.7 0.0 copy-start.4
  23.7 0.0 copy-start.5
  23.7 0.0 collective-permute-done
  23.7 0.0 collective-permute-done.1
  23.7 1.0 maximum_convert_fusion.1
  24.7 2.2 fusion.451
  26.9 30.0 %all-reduce.3 = (f32[512]{0:T(512)S(1)}, f32[512]{0:T(512)S(1)}) all-reduce(f32[512]{0:T(512)S(1)} %bitcast.584, f32[512]{0:T(512)S(1)} %bitcast.583), channel_id=1, replica_groups=mesh['space'=32,'tensor'=16] {'tensor'}, use_global_device_ids=true, to_apply=%region_3.4 | all-reduce | flops 1024 | bytes 8192 | tf_op jit(solution)/shard_map/psum | solution.py:40
  56.9 0.7 fusion.285
  57.6 0.0 all-gather.3.cloned.1.call-update
  57.6 0.0 reduce-scatter.3.cloned.1.call-start
  57.7 0.0 copy-done.1
  57.7 33.6 %all-gather.3.cloned.1.call-done = bf16[512,1024]{0,1:T(8,128)(2,1)} async-done(((bf16[512,64]{0,1:T(8,128)(2,1)}), bf16[512,1024]{0,1:T(8,128)(2,1)}) %all-gather.3.cloned.1.call-update) | async-done | bytes 1048592 | tf_op jit(solution)/shard_map/all_gather | solution.py:49
  91.3 0.0 copy-done.4
  91.3 0.0 copy-done.5
  91.3 4.6 %convolution_convert_fusion.1 = bf16[512,1024]{0,1:T(8,128)(2,1)} fusion(bf16[2,256,1024]{2,1,0:T(8,128)(2,1)S(1)} %copy-done.4, bf16[512,1024]{0,1:T(8,128)(2,1)} %all-gather.3.cloned.1.call-done, bf16[2,1024,256]{2,1,0:T(8,128)(2,1)S(1)} %copy-done.5, f32[256]{0:T(256)S(1)} %bitcast.588), kind=kOutput, calls=%fused_computation.85 | convolution fusion | flops 546045952 | bytes 3146752 | tf_op jit(solution)/shard_map/dot_general | solution.py:54
  95.9 0.0 copy-start.2
  95.9 0.0 copy-start.3
  95.9 0.0 copy-start
  95.9 0.0 reduce-scatter.3.cloned.1.call-update
  95.9 0.0 all-gather.5.cloned.1.call-start
  96.0 0.6 copy-done.2
  96.6 0.0 copy-done.3
  96.6 66.4 %reduce-scatter.3.cloned.1.call-done = bf16[512,64]{0,1:T(8,128)(2,1)} async-done(((bf16[512,1024]{0,1:T(8,128)(2,1)}), bf16[512,64]{0,1:T(8,128)(2,1)}) %reduce-scatter.3.cloned.1.call-update) | async-done | bytes 65552 | tf_op jit(solution)/shard_map/reduce_scatter | solution.py:55
  163.1 0.0 copy-done
  163.1 0.9 fusion.284
  164.1 6.4 %collective-permute-start.3 = (bf16[3,128,64]{1,0,2:T(4,128)(2,1)S(1)}, bf16[3,128,64]{1,0,2:T(4,128)(2,1)S(1)}, u32[]{:S(2)}, u32[]{:S(2)}) collective-permute-start(bf16[3,128,64]{1,0,2:T(4,128)(2,1)S(1)} %slice.780), channel_id=1, source_target_pairs={{16,0},{32,16},{48,32},{64,48},{80,64},{96,80},{112,96},{128,112},... | collective-permute-start | bytes 147464 | tf_op jit(solution)/shard_map/ppermute | solution.py:19
  170.5 1.9 collective-permute-start.2
  172.4 0.1 fusion.290
  172.5 0.0 collective-permute-done.3
  172.5 7.1 %collective-permute-done.2 = bf16[3,128,64]{1,0,2:T(4,128)(2,1)S(1)} collective-permute-done((bf16[3,128,64]{1,0,2:T(4,128)(2,1)S(1)}, bf16[3,128,64]{1,0,2:T(4,128)(2,1)S(1)}, u32[]{:S(2)}, u32[]{:S(2)}) %collective-permute-start.2) | collective-permute-done | bytes 49184 | tf_op jit(solution)/shard_map/ppermute | solution.py:18
  179.6 0.1 maximum_convert_fusion
  179.8 7.0 %fusion.450 = (f32[4,128]{1,0:T(4,128)S(1)}, f32[4,128]{1,0:T(4,128)S(1)}, f32[4,128,64]{1,0,2:T(4,128)S(1)}) fusion(f32[64]{0:T(128)S(1)} %get-tuple-element.22, f32[64]{0:T(128)S(1)} %get-tuple-element.23, f32[64]{0:T(128)S(1)} %get-tuple-element.24, f32[64]{0:T(128)S(1)} %get-tuple-element.25, f32[10,128,64]{1,0,2:T(8,128)S(1)} %maximum_convert_fusion, ...), kind=kLoop, calls=%fused_computation.684 | loop fusion | flops 3275776 | bytes 1602048 | tf_op jit(solution)/shard_map/reduce_sum | solution.py:41
  186.8 27.1 %all-reduce.2 = (f32[512]{0:T(512)S(1)}, f32[512]{0:T(512)S(1)}) all-reduce(f32[512]{0:T(512)S(1)} %bitcast.586, f32[512]{0:T(512)S(1)} %bitcast.585), channel_id=1, replica_groups=mesh['space'=32,'tensor'=16] {'tensor'}, use_global_device_ids=true, to_apply=%region_8.9 | all-reduce | flops 1024 | bytes 8192 | tf_op jit(solution)/shard_map/psum | solution.py:40
  214.0 0.7 fusion.286
  214.7 0.0 all-gather.5.cloned.1.call-update
  214.7 0.0 reduce-scatter.5.cloned.1.call-start
  214.8 31.8 %all-gather.5.cloned.1.call-done = bf16[512,1024]{0,1:T(8,128)(2,1)} async-done(((bf16[512,64]{0,1:T(8,128)(2,1)}), bf16[512,1024]{0,1:T(8,128)(2,1)}) %all-gather.5.cloned.1.call-update) | async-done | bytes 1048592 | tf_op jit(solution)/shard_map/all_gather | solution.py:49
  246.6 4.6 %convolution_convert_fusion = bf16[512,1024]{0,1:T(8,128)(2,1)} fusion(bf16[2,256,1024]{2,1,0:T(8,128)(2,1)S(1)} %copy-done.4, bf16[512,1024]{0,1:T(8,128)(2,1)} %all-gather.5.cloned.1.call-done, bf16[2,1024,256]{2,1,0:T(8,128)(2,1)S(1)} %copy-done.5, f32[256]{0:T(256)S(1)} %bitcast.587), kind=kOutput, calls=%fused_computation.84 | convolution fusion | flops 546045952 | bytes 3146752 | tf_op jit(solution)/shard_map/dot_general | solution.py:54
  251.2 0.0 reduce-scatter.5.cloned.1.call-update
  251.2 67.2 %reduce-scatter.5.cloned.1.call-done = bf16[512,64]{0,1:T(8,128)(2,1)} async-done(((bf16[512,1024]{0,1:T(8,128)(2,1)}), bf16[512,64]{0,1:T(8,128)(2,1)}) %reduce-scatter.5.cloned.1.call-update) | async-done | bytes 65552 | tf_op jit(solution)/shard_map/reduce_scatter | solution.py:55
  318.4 1.6 copy_bitcast_fusion
  (15 shorter events, 0.2 us)
Async XLA Ops:
  6.5 84.8 %all-gather.3.cloned.1.call-start = ((), (), s32[]{:S(2)}) async-start(), calls=%async_computation.2 | async-start | bytes 1114112 | tf_op jit(solution)/shard_map/all_gather | solution.py:49
  7.4 16.3 %collective-permute-start = (bf16[3,128,64]{1,2,0:T(8,128)(2,1)S(1)}, bf16[3,128,64]{1,2,0:T(8,128)(2,1)S(1)}, u32[]{:S(2)}, u32[]{:S(2)}) collective-permute-start(bf16[3,128,64]{1,2,0:T(8,128)(2,1)S(1)} %get-tuple-element.17), channel_id=1, source_target_pairs={{0,16},{16,32},{32,48},{48,64},{64,80},{80,96},{96,112},{112,128},... | collective-permute-start | bytes 147464 | tf_op jit(solution)/shard_map/ppermute | solution.py:18
  13.5 10.2 %collective-permute-start.1 = (bf16[3,128,64]{1,2,0:T(8,128)(2,1)S(1)}, bf16[3,128,64]{1,2,0:T(8,128)(2,1)S(1)}, u32[]{:S(2)}, u32[]{:S(2)}) collective-permute-start(bf16[3,128,64]{1,2,0:T(8,128)(2,1)S(1)} %get-tuple-element.18), channel_id=1, source_target_pairs={{16,0},{32,16},{48,32},{64,48},{80,64},{96,80},{112,96},{128,112},... | collective-permute-start | bytes 147464 | tf_op jit(solution)/shard_map/ppermute | solution.py:19
  23.7 34.0 %copy-start.1 = (f32[2,256]{1,0:T(2,128)S(1)}, f32[2,256]{1,0:T(2,128)}, u32[]{:S(2)}) copy-start(f32[2,256]{1,0:T(2,128)} %param.14) | copy-start | bytes 6148
  23.7 67.6 %copy-start.4 = (bf16[2,256,1024]{2,1,0:T(8,128)(2,1)S(1)}, bf16[2,256,1024]{2,1,0:T(8,128)(2,1)}, u32[]{:S(2)}) copy-start(bf16[2,256,1024]{2,1,0:T(8,128)(2,1)} %param.15) | copy-start | bytes 3145732
  23.7 67.6 %copy-start.5 = (bf16[2,1024,256]{2,1,0:T(8,128)(2,1)S(1)}, bf16[2,1024,256]{2,1,0:T(8,128)(2,1)}, u32[]{:S(2)}) copy-start(bf16[2,1024,256]{2,1,0:T(8,128)(2,1)} %param.13) | copy-start | bytes 3145732
  57.6 105.5 %reduce-scatter.3.cloned.1.call-start = ((), (), s32[]{:S(2)}) async-start(), calls=%async_computation.3 | async-start | bytes 1114112 | tf_op jit(solution)/shard_map/reduce_scatter | solution.py:55
  95.9 0.7 copy-start.2
  95.9 0.7 copy-start.3
  95.9 67.2 %copy-start = (bf16[4,128,64]{1,2,0:T(8,128)(2,1)S(1)}, bf16[4,128,64]{1,2,0:T(8,128)(2,1)}, u32[]{:S(2)}) copy-start(bf16[4,128,64]{1,2,0:T(8,128)(2,1)} %param.9) | copy-start | bytes 196612
  95.9 150.7 %all-gather.5.cloned.1.call-start = ((), (), s32[]{:S(2)}) async-start(), calls=%async_computation.4 | async-start | bytes 1114112 | tf_op jit(solution)/shard_map/all_gather | solution.py:49
  164.1 8.4 %collective-permute-start.3 = (bf16[3,128,64]{1,0,2:T(4,128)(2,1)S(1)}, bf16[3,128,64]{1,0,2:T(4,128)(2,1)S(1)}, u32[]{:S(2)}, u32[]{:S(2)}) collective-permute-start(bf16[3,128,64]{1,0,2:T(4,128)(2,1)S(1)} %slice.780), channel_id=1, source_target_pairs={{16,0},{32,16},{48,32},{64,48},{80,64},{96,80},{112,96},{128,112},... | collective-permute-start | bytes 147464 | tf_op jit(solution)/shard_map/ppermute | solution.py:19
  170.5 9.2 %collective-permute-start.2 = (bf16[3,128,64]{1,0,2:T(4,128)(2,1)S(1)}, bf16[3,128,64]{1,0,2:T(4,128)(2,1)S(1)}, u32[]{:S(2)}, u32[]{:S(2)}) collective-permute-start(bf16[3,128,64]{1,0,2:T(4,128)(2,1)S(1)} %slice.778), channel_id=1, source_target_pairs={{0,16},{16,32},{32,48},{48,64},{64,80},{80,96},{96,112},{112,128},... | collective-permute-start | bytes 147464 | tf_op jit(solution)/shard_map/ppermute | solution.py:18
  214.7 103.7 %reduce-scatter.5.cloned.1.call-start = ((), (), s32[]{:S(2)}) async-start(), calls=%async_computation.5 | async-start | bytes 1114112 | tf_op jit(solution)/shard_map/reduce_scatter | solution.py:55
Sparse Core Ops, SparseCore 0:
  57.7 33.5 all-gather.2
  96.0 66.9 reduce-scatter.2
  214.8 31.7 all-gather.4
  251.3 67.0 reduce-scatter.4
where the time goes:
time: 328 us; the launch traced here: 326 us
  waiting for transfers between devices  206 us (63%)
  blocking collectives  57.1 us (17%)
  starting transfers between devices  22.1 us (7%)
  other arithmetic  14.4 us (4%)
  between operations  13.3 us (4%)
  matrix products  9.2 us (3%)
  local copies, waits for them, and re-layouts  4.19 us (1%)
    reduce_scatter x2, waiting for transfers between devices, one_block(): lax.psum_scatter(partial_value.astype(jnp.bfloat16), 'tensor', scatter_di...  134 us
    all_gather x2, waiting for transfers between devices, one_block(): lax.all_gather(normed_part, 'tensor', axis=1, tiled=True)  65.4 us
    psum x2, blocking collectives, one_block(): lax.psum((jnp.sum(filtered, axis=-1), jnp.sum(filtered * filtered, axis=-...  57.1 us
    ppermute x2, starting transfers between devices, with_halo(): after = lax.ppermute(leading, axis, down)  13.9 us
    dot_general x2, matrix products, one_block(): jnp.dot(hidden, reduce_w, preferred_element_type=jnp.float32)  9.2 us
    reduce_sum x2, other arithmetic, one_block(): jnp.sum(filtered, axis=-1)  9.17 us
    ppermute x2, starting transfers between devices, with_halo(): before = lax.ppermute(last, axis, up)  8 us
    ppermute x2, waiting for transfers between devices, with_halo(): before = lax.ppermute(last, axis, up)  7.13 us
  transfers between devices with their start and end apart: 8, of which 5 were waited for; matrix products, arithmetic and copies ran while one was open for 1% of the time, Pallas kernels for 0%

commit v1 on v0

v1 whole, which is shorter than its diff:
```python
import jax
import jax.numpy as jnp
from jax import lax
from jax.experimental import pallas as pl
from jax.experimental.pallas import tpu as pltpu
from jax.sharding import PartitionSpec as P

D = 1024
TAPS = 7
HALF = TAPS // 2
BLOCKS = 2
CORES = 2

VMEM = pl.BlockSpec(memory_space=pltpu.VMEM)


def call(body, outs, *args):
    single = not isinstance(outs, (list, tuple))
    return pl.pallas_call(
        body,
        out_shape=outs,
        in_specs=[VMEM] * len(args),
        out_specs=VMEM if single else [VMEM] * len(outs),
        compiler_params=pltpu.CompilerParams(vmem_limit_bytes=48 << 20),
    )(*args)


def conv_kernel(before_ref, rows_ref, after_ref, taps_ref, out_ref):
    height, share, width = rows_ref.shape
    copies = out_ref.shape[0]
    column = lax.broadcasted_iota(jnp.int32, (8, width), 1)
    for group in range(share // 8):
        chans = slice(8 * group, 8 * group + 8)
        rows = [before_ref[r, chans, :] for r in range(HALF)]
        rows += [rows_ref[r, chans, :] for r in range(height)]
        rows += [after_ref[r, chans, :] for r in range(HALF)]
        rows = [row.astype(jnp.float32) for row in rows]
        totals = [jnp.zeros((8, width), jnp.float32)] * height
        for j in range(TAPS):
            taps = [
                jnp.broadcast_to(taps_ref[chans, i * TAPS + j : i * TAPS + j + 1], (8, width))
                for i in range(TAPS)
            ]
            shift = j - HALF
            for r in range(height):
                acc = rows[r] * taps[0]
                for i in range(1, TAPS):
                    acc = acc + rows[r + i] * taps[i]
                if shift:
                    acc = pltpu.roll(acc, (-shift) % width, 1)
                    inside = (column + shift >= 0) & (column + shift < width)
                    acc = jnp.where(inside, acc, 0.0)
                totals[r] = totals[r] + acc
        for r in range(height):
            half, at = divmod(r, height // CORES)
            value = totals[r].astype(jnp.bfloat16)
            for copy in range(copies):
                out_ref[copy, half, chans, width * at : width * (at + 1)] = value


def mlp_kernel(block, x_ref, gain_ref, bias_ref, ea_ref, eb_ref, ba_ref, bb_ref, ra_ref, rb_ref, out_ref):
    x = x_ref[...].reshape(D, x_ref.shape[-1])
    x = jnp.transpose(x).astype(jnp.float32)
    mean = jnp.mean(x, axis=-1, keepdims=True)
    centered = x - mean
    var = jnp.mean(centered * centered, axis=-1, keepdims=True)
    gain = gain_ref[block : block + 1, :]
    bias = bias_ref[block : block + 1, :]
    normed = (centered * lax.rsqrt(var + 1e-06) * gain + bias).astype(jnp.bfloat16)
    total = None
    for e_ref, b_ref, r_ref in ((ea_ref, ba_ref, ra_ref), (eb_ref, bb_ref, rb_ref)):
        preact = jnp.dot(normed, e_ref[block], preferred_element_type=jnp.float32)
        preact = preact + b_ref[block : block + 1, :]
        hidden = 0.5 * preact * (1.0 + lax.erf(preact * (0.5**0.5)))
        partial = jnp.dot(hidden.astype(jnp.bfloat16), r_ref[block], preferred_element_type=jnp.float32)
        total = partial if total is None else total + partial
    out_ref[...] = jnp.transpose(total.astype(jnp.bfloat16)).reshape(out_ref.shape)


def mix_rows(block, parts_ref, stream_ref, cols_ref):
    height, share, width = stream_ref.shape
    scale = jnp.broadcast_to(cols_ref[:, 2 * block : 2 * block + 1], (share, width))
    shift = jnp.broadcast_to(cols_ref[:, 2 * block + 1 : 2 * block + 2], (share, width))
    rows = []
    for r in range(height):
        half, at = divmod(r, height // CORES)
        lanes = slice(width * at, width * (at + 1))
        mixed = parts_ref[0, half, :, lanes].astype(jnp.float32)
        for copy in range(1, parts_ref.shape[0]):
            mixed = mixed + parts_ref[copy, half, :, lanes].astype(jnp.float32)
        updated = stream_ref[r].astype(jnp.float32) + scale * (mixed + shift)
        rows.append(updated.astype(jnp.bfloat16))
    return rows


def mix_kernel(block, parts_ref, stream_ref, cols_ref, out_ref, first_ref, last_ref):
    rows = mix_rows(block, parts_ref, stream_ref, cols_ref)
    for r, row in enumerate(rows):
        out_ref[r] = row
        if r < HALF:
            first_ref[r] = row
        if r >= len(rows) - HALF:
            last_ref[r - (len(rows) - HALF)] = row


def last_kernel(block, parts_ref, stream_ref, cols_ref, out_ref):
    for r, row in enumerate(mix_rows(block, parts_ref, stream_ref, cols_ref)):
        out_ref[r] = row


def per_device(features, depth_kernel, norm_gain, norm_bias, w_expand, b_expand, w_reduce, b_reduce, layer_scale):
    height, width, share = features.shape
    bands, members = lax.axis_size("space"), lax.axis_size("tensor")
    copies = members // CORES
    half = height // CORES * width
    down = [(i, i + 1) for i in range(bands - 1)]
    up = [(j, i) for i, j in down]
    sibling = [(i, i ^ 1) for i in range(members)]

    stream = jnp.transpose(features, (0, 2, 1))
    first, last = stream[:HALF], stream[height - HALF :]
    before = lax.ppermute(last, "space", down)
    after = lax.ppermute(first, "space", up)
    other_expand = lax.ppermute(w_expand, "tensor", sibling)
    other_reduce = lax.ppermute(w_reduce, "tensor", sibling)
    other_bias = lax.ppermute(b_expand, "tensor", sibling)
    taps = jnp.transpose(depth_kernel.reshape(BLOCKS, TAPS * TAPS, share), (0, 2, 1)).astype(jnp.float32)
    cols = jnp.stack([layer_scale[0], b_reduce[0], layer_scale[1], b_reduce[1]], axis=-1)

    for block in range(BLOCKS):
        filtered = call(
            conv_kernel,
            jax.ShapeDtypeStruct((copies, CORES, share, half), jnp.bfloat16),
            before, stream, after, taps[block],
        )
        filtered = lax.all_to_all(filtered.reshape(members, share, half), "tensor", 0, 0, tiled=True)
        partial = call(
            lambda *refs: mlp_kernel(block, *refs),
            jax.ShapeDtypeStruct((members, share, half), jnp.bfloat16),
            filtered, norm_gain, norm_bias, w_expand, other_expand, b_expand, other_bias, w_reduce, other_reduce,
        )
        partial = lax.all_to_all(partial, "tensor", 0, 0, tiled=True).reshape(copies, CORES, share, half)
        whole = jax.ShapeDtypeStruct((height, share, width), jnp.bfloat16)
        if block == BLOCKS - 1:
            stream = call(lambda *refs: last_kernel(block, *refs), whole, partial, stream, cols)
        else:
            edge = jax.ShapeDtypeStruct((HALF, share, width), jnp.bfloat16)
            stream, first, last = call(
                lambda *refs: mix_kernel(block, *refs), (whole, edge, edge), partial, stream, cols
            )
            before = lax.ppermute(last, "space", down)
            after = lax.ppermute(first, "space", up)
    return jnp.transpose(stream, (0, 2, 1))


def solution(mesh):
    return jax.shard_map(
        per_device,
        mesh=mesh,
        in_specs=(
            P("space", None, "tensor"),
            P(None, None, None, "tensor"),
            P(),
            P(),
            P(None, None, "tensor"),
            P(None, "tensor"),
            P(None, "tensor", None),
            P(None, "tensor"),
            P(None, "tensor"),
        ),
        out_specs=P("space", None, "tensor"),
        check_vma=False,
    )
```

time: 328 us -> 111 us (0.34)
  the two profiles are of different devices: /device:TPU:56 before, /device:TPU:32 now
where the time goes in v1:
time: 111 us; the launch traced here: 110 us
  starting transfers between devices  39.3 us (35%)
  blocking collectives  27 us (24%)
  waiting for transfers between devices  25.4 us (23%)
  Pallas kernels  14.7 us (13%)
  local copies, waits for them, and re-layouts  3.37 us (3%)
    ppermute x2, starting transfers between devices, per_device(): after = lax.ppermute(first, 'space', up)  19 us
    pallas_call x6, Pallas kernels, call(): pl.pallas_call(body, out_shape=outs, in_specs=[VMEM] * len(args), out_spe...  14.7 us
    all_to_all x1, blocking collectives, per_device(): lax.all_to_all(filtered.reshape(members, share, half), 'tensor', 0, 0, ti...  13.5 us
    all_to_all x1, blocking collectives, per_device(): lax.all_to_all(partial, 'tensor', 0, 0, tiled=True)  13.5 us
    all_to_all x1, waiting for transfers between devices, per_device(): lax.all_to_all(partial, 'tensor', 0, 0, tiled=True)  10.7 us
    all_to_all x1, waiting for transfers between devices, per_device(): lax.all_to_all(filtered.reshape(members, share, half), 'tensor', 0, 0, ti...  7.84 us
    all_to_all x1, starting transfers between devices, per_device(): lax.all_to_all(filtered.reshape(members, share, half), 'tensor', 0, 0, ti...  5.37 us
    ppermute x2, waiting for transfers between devices, per_device(): before = lax.ppermute(last, 'space', down)  4.42 us
  transfers between devices with their start and end apart: 9, of which 6 were waited for; matrix products, arithmetic and copies ran while one was open for 0% of the time, Pallas kernels for 3%

profile of v1, /device:TPU:32, one launch (start us, length us, event | category | flops | bytes accessed | tf_op | source)
XLA Modules:
  0.0 110.0 jit_solution(16738316278509464814)
XLA Ops:
  0.0 0.0 copy-start.8
  0.0 0.0 copy-start.4
  0.0 0.0 copy-start.7
  0.0 0.0 copy-start.5
  0.0 0.0 copy-start.6
  0.0 1.5 %fusion = (bf16[3,64,128]{2,1,0:T(8,128)(2,1)}, bf16[3,64,128]{2,1,0:T(8,128)(2,1)S(1)}) fusion(bf16[4,64,128]{2,1,0:T(8,128)(2,1)} %bitcast.25), kind=kLoop, calls=%fused_computation.8 | loop fusion | bytes 196608 | tf_op jit(solution)/shard_map/slice | solution.py:121
  1.6 10.8 %collective-permute-start.1 = (bf16[3,64,128]{2,1,0:T(8,128)(2,1)}, bf16[3,64,128]{2,1,0:T(8,128)(2,1)S(1)}, u32[]{:S(2)}, u32[]{:S(2)}) collective-permute-start(bf16[3,64,128]{2,1,0:T(8,128)(2,1)} %get-tuple-element.13), channel_id=1, source_target_pairs={{16,0},{32,16},{48,32},{64,48},{80,64},{96,80},{112,96},{128,112},... | collective-permute-start | bytes 147464 | tf_op jit(solution)/shard_map/ppermute | solution.py:123
  12.4 0.0 copy-start
  12.4 0.0 copy-start.1
  12.4 2.1 %collective-permute-start = (bf16[3,64,128]{2,1,0:T(8,128)(2,1)S(1)}, bf16[3,64,128]{2,1,0:T(8,128)(2,1)S(1)}, u32[]{:S(2)}, u32[]{:S(2)}) collective-permute-start(bf16[3,64,128]{2,1,0:T(8,128)(2,1)S(1)} %get-tuple-element.14), channel_id=1, source_target_pairs={{0,16},{16,32},{32,48},{48,64},{64,80},{80,96},{96,112},{112,128},... | collective-permute-start | bytes 147464 | tf_op jit(solution)/shard_map/ppermute | solution.py:122
  14.5 1.9 %collective-permute-start.2 = (bf16[2,1024,256]{2,1,0:T(8,128)(2,1)}, bf16[2,1024,256]{2,1,0:T(8,128)(2,1)S(1)}, u32[]{:S(2)}, u32[]{:S(2)}) collective-permute-start(bf16[2,1024,256]{2,1,0:T(8,128)(2,1)} %refs_3_.3), channel_id=1, source_target_pairs={{0,1},{1,0},{2,3},{3,2},{4,5},{5,4},{6,7},{7,6},{8,9},{9,8},{10,11... | collective-permute-start | bytes 3145736 | tf_op jit(solution)/shard_map/ppermute | solution.py:124
  16.4 2.4 %collective-permute-start.4 = (bf16[2,256,1024]{2,1,0:T(8,128)(2,1)}, bf16[2,256,1024]{2,1,0:T(8,128)(2,1)}, u32[]{:S(2)}, u32[]{:S(2)}) collective-permute-start(bf16[2,256,1024]{2,1,0:T(8,128)(2,1)} %refs_7_.3), channel_id=1, source_target_pairs={{0,1},{1,0},{2,3},{3,2},{4,5},{5,4},{6,7},{7,6},{8,9},{9,8},{10,11... | collective-permute-start | bytes 3145736 | tf_op jit(solution)/shard_map/ppermute | solution.py:125
  18.8 0.0 copy-done.8
  18.9 0.1 copy.20
  19.0 0.0 collective-permute-done.1.after_ref
  19.0 4.3 %collective-permute-done.before_ref = bf16[3,64,128]{2,1,0:T(8,128)(2,1)S(1)} collective-permute-done((bf16[3,64,128]{2,1,0:T(8,128)(2,1)S(1)}, bf16[3,64,128]{2,1,0:T(8,128)(2,1)S(1)}, u32[]{:S(2)}, u32[]{:S(2)}) %collective-permute-start) | collective-permute-done | bytes 49184 | tf_op jit(solution)/shard_map/ppermute | solution.py:122
  23.3 0.0 copy-done.4
  23.3 3.8 %shard_map.91 = bf16[8,2,64,256]{3,2,1,0:T(8,128)(2,1)S(1)} custom-call(bf16[3,64,128]{2,1,0:T(8,128)(2,1)S(1)} %collective-permute-done.before_ref, bf16[4,64,128]{2,1,0:T(8,128)(2,1)S(1)} %bitcast.26, bf16[3,64,128]{2,1,0:T(8,128)(2,1)S(1)} %collective-permute-done.1.after_ref, f32[64,49]{1,0:T(8,128)S(1)} %get-tuple-element.12.taps_ref), custom_call_target="tpu_custom_call" | custom-call | tf_op jit(solution)/shard_map/pallas_call | solution.py:19
  27.0 0.0 copy-start.3
  27.1 0.8 copy-done.3
  27.8 5.4 %all-to-all-start = ((bf16[16,64,256]{2,1,0:T(8,128)(2,1)}), bf16[16,64,256]{2,1,0:T(8,128)(2,1)}, u32[]{:S(2)}, u32[]{:S(2)}) async-start(bf16[16,64,256]{2,1,0:T(8,128)(2,1)} %bitcast.22), calls=%async_computation | async-start | bytes 1048576 | tf_op jit(solution)/shard_map/all_to_all | solution.py:136
  33.2 0.0 copy-done.7
  33.2 2.3 %collective-permute-start.3 = (f32[2,256]{1,0:T(2,128)S(1)}, f32[2,256]{1,0:T(2,128)S(1)}, u32[]{:S(2)}, u32[]{:S(2)}) collective-permute-start(f32[2,256]{1,0:T(2,128)S(1)} %copy-done.7), channel_id=1, source_target_pairs={{0,1},{1,0},{2,3},{3,2},{4,5},{5,4},{6,7},{7,6},{8,9},{9,8},{10,11... | collective-permute-start | bytes 6152 | tf_op jit(solution)/shard_map/ppermute | solution.py:126
  35.5 0.8 collective-permute-done.3.refs_6_
  36.3 7.8 %all-to-all-done.refs_0_ = bf16[16,64,256]{2,1,0:T(8,128)(2,1)} async-done(((bf16[16,64,256]{2,1,0:T(8,128)(2,1)}), bf16[16,64,256]{2,1,0:T(8,128)(2,1)}, u32[]{:S(2)}, u32[]{:S(2)}) %all-to-all-start) | async-done | bytes 524320 | tf_op jit(solution)/shard_map/all_to_all | solution.py:136
  44.1 0.0 collective-permute-done.2.refs_4_
  44.1 0.0 collective-permute-done.4.refs_8_
  44.1 0.0 copy-done.5
  44.1 0.0 copy-done.6
  44.2 0.0 copy-done
  44.2 0.0 copy-done.1
  44.2 2.7 %shard_map.92 = bf16[16,64,256]{2,1,0:T(8,128)(2,1)S(1)} custom-call(bf16[16,64,256]{2,1,0:T(8,128)(2,1)} %all-to-all-done.refs_0_, f32[2,1024]{1,0:T(2,128)S(1)} %copy-done.5, f32[2,1024]{1,0:T(2,128)S(1)} %copy-done.6, bf16[2,1024,256]{2,1,0:T(8,128)(2,1)S(1)} %copy-done, bf16[2,1024,256]{2,1,0:T(8,128)(2,1)S(1)} %collective-permute-done.2.refs_4_, ...), custom_call_target="tpu_custom_call" | custom-call | tf_op jit(solution)/shard_map/pallas_call | solution.py:19
  46.9 0.0 copy-start.2
  46.9 0.8 copy-done.2
  47.7 0.0 copy-start.9
  47.7 0.0 copy-start.10
  47.7 4.4 %all-to-all-start.1 = ((bf16[16,64,256]{2,1,0:T(8,128)(2,1)}), bf16[16,64,256]{2,1,0:T(8,128)(2,1)}, u32[]{:S(2)}, u32[]{:S(2)}) async-start(bf16[16,64,256]{2,1,0:T(8,128)(2,1)} %copy-done.2), calls=%async_computation.1 | async-start | bytes 1048576 | tf_op jit(solution)/shard_map/all_to_all | solution.py:142
  52.1 0.0 copy-done.9
  52.1 0.0 copy-done.10
  52.2 0.1 copy.21.refs_2_
  52.3 10.7 %all-to-all-done.1 = bf16[16,64,256]{2,1,0:T(8,128)(2,1)} async-done(((bf16[16,64,256]{2,1,0:T(8,128)(2,1)}), bf16[16,64,256]{2,1,0:T(8,128)(2,1)}, u32[]{:S(2)}, u32[]{:S(2)}) %all-to-all-start.1) | async-done | bytes 524320 | tf_op jit(solution)/shard_map/all_to_all | solution.py:142
  63.0 1.1 %shard_map.93 = (bf16[4,64,128]{2,1,0:T(8,128)(2,1)S(1)}, bf16[3,64,128]{2,1,0:T(8,128)(2,1)S(1)}, bf16[3,64,128]{2,1,0:T(8,128)(2,1)S(1)}) custom-call(bf16[8,2,64,256]{3,2,1,0:T(8,128)(2,1)} %bitcast.5.refs_0_, bf16[4,64,128]{2,1,0:T(8,128)(2,1)S(1)} %bitcast.27, f32[64,4]{1,0:T(8,128)S(1)} %copy.21.refs_2_), custom_call_target="tpu_custom_call" | custom-call | tf_op jit(solution)/shard_map/pallas_call | solution.py:19
  64.1 1.9 %collective-permute-start.5 = (bf16[3,64,128]{2,1,0:T(8,128)(2,1)S(1)}, bf16[3,64,128]{2,1,0:T(8,128)(2,1)S(1)}, u32[]{:S(2)}, u32[]{:S(2)}) collective-permute-start(bf16[3,64,128]{2,1,0:T(8,128)(2,1)S(1)} %get-tuple-element.8), channel_id=1, source_target_pairs={{0,16},{16,32},{32,48},{48,64},{64,80},{80,96},{96,112},{112,128},... | collective-permute-start | bytes 147464 | tf_op jit(solution)/shard_map/ppermute | solution.py:151
  66.1 8.1 %collective-permute-start.6 = (bf16[3,64,128]{2,1,0:T(8,128)(2,1)S(1)}, bf16[3,64,128]{2,1,0:T(8,128)(2,1)S(1)}, u32[]{:S(2)}, u32[]{:S(2)}) collective-permute-start(bf16[3,64,128]{2,1,0:T(8,128)(2,1)S(1)} %get-tuple-element.10), channel_id=1, source_target_pairs={{16,0},{32,16},{48,32},{64,48},{80,64},{96,80},{112,96},{128,112},... | collective-permute-start | bytes 147464 | tf_op jit(solution)/shard_map/ppermute | solution.py:152
  74.2 0.1 collective-permute-done.5.before_ref
  74.3 1.6 %collective-permute-done.6.after_ref = bf16[3,64,128]{2,1,0:T(8,128)(2,1)S(1)} collective-permute-done((bf16[3,64,128]{2,1,0:T(8,128)(2,1)S(1)}, bf16[3,64,128]{2,1,0:T(8,128)(2,1)S(1)}, u32[]{:S(2)}, u32[]{:S(2)}) %collective-permute-start.6) | collective-permute-done | bytes 49184 | tf_op jit(solution)/shard_map/ppermute | solution.py:152
  75.9 3.8 %shard_map.94 = bf16[8,2,64,256]{3,2,1,0:T(8,128)(2,1)S(1)} custom-call(bf16[3,64,128]{2,1,0:T(8,128)(2,1)S(1)} %collective-permute-done.5.before_ref, bf16[4,64,128]{2,1,0:T(8,128)(2,1)S(1)} %get-tuple-element.9.rows_ref.refs_1_, bf16[3,64,128]{2,1,0:T(8,128)(2,1)S(1)} %collective-permute-done.6.after_ref, f32[64,49]{1,0:T(8,128)S(1)} %get-tuple-element.11.taps_ref), custom_call_target="tpu_custom_call" | custom-call | tf_op jit(solution)/shard_map/pallas_call | solution.py:19
  79.7 13.5 %all_to_all.20.refs_0_ = bf16[16,64,256]{2,1,0:T(8,128)(2,1)S(1)} all-to-all(bf16[16,64,256]{2,1,0:T(8,128)(2,1)S(1)} %bitcast.23), channel_id=1, replica_groups=mesh['space'=32,'tensor'=16] {'tensor'}, dimensions={0} | all-to-all | bytes 1048576 | tf_op jit(solution)/shard_map/all_to_all | solution.py:136
  93.2 2.6 %shard_map.95 = bf16[16,64,256]{2,1,0:T(8,128)(2,1)S(1)} custom-call(bf16[16,64,256]{2,1,0:T(8,128)(2,1)S(1)} %all_to_all.20.refs_0_, f32[2,1024]{1,0:T(2,128)S(1)} %copy-done.5, f32[2,1024]{1,0:T(2,128)S(1)} %copy-done.6, bf16[2,1024,256]{2,1,0:T(8,128)(2,1)S(1)} %copy-done, bf16[2,1024,256]{2,1,0:T(8,128)(2,1)S(1)} %collective-permute-done.2.refs_4_, ...), custom_call_target="tpu_custom_call" | custom-call | tf_op jit(solution)/shard_map/pallas_call | solution.py:19
  95.8 13.5 %all_to_all.21 = bf16[16,64,256]{2,1,0:T(8,128)(2,1)S(1)} all-to-all(bf16[16,64,256]{2,1,0:T(8,128)(2,1)S(1)} %shard_map.95), channel_id=1, replica_groups=mesh['space'=32,'tensor'=16] {'tensor'}, dimensions={0} | all-to-all | bytes 1048576 | tf_op jit(solution)/shard_map/all_to_all | solution.py:142
  109.3 0.7 shard_map.96
  (4 shorter events, 0.0 us)
Async XLA Ops:
  0.0 18.8 %copy-start.8 = (bf16[2,7,7,64]{3,0,2,1:T(2,128)(2,1)S(1)}, bf16[2,7,7,64]{3,0,2,1:T(2,128)(2,1)}, u32[]{:S(2)}) copy-start(bf16[2,7,7,64]{3,0,2,1:T(2,128)(2,1)} %param.10) | copy-start | bytes 37636
  0.0 23.3 %copy-start.4 = (bf16[4,128,64]{1,2,0:T(8,128)(2,1)S(1)}, bf16[4,128,64]{1,2,0:T(8,128)(2,1)}, u32[]{:S(2)}) copy-start(bf16[4,128,64]{1,2,0:T(8,128)(2,1)} %param.9) | copy-start | bytes 196612
  0.0 33.2 %copy-start.7 = (f32[2,256]{1,0:T(2,128)S(1)}, f32[2,256]{1,0:T(2,128)}, u32[]{:S(2)}) copy-start(f32[2,256]{1,0:T(2,128)} %refs_5_.3) | copy-start | bytes 6148
  0.0 44.1 %copy-start.5 = (f32[2,1024]{1,0:T(2,128)S(1)}, f32[2,1024]{1,0:T(2,128)}, u32[]{:S(2)}) copy-start(f32[2,1024]{1,0:T(2,128)} %refs_1_.3) | copy-start | bytes 24580
  0.0 44.1 %copy-start.6 = (f32[2,1024]{1,0:T(2,128)S(1)}, f32[2,1024]{1,0:T(2,128)}, u32[]{:S(2)}) copy-start(f32[2,1024]{1,0:T(2,128)} %refs_2_.3) | copy-start | bytes 24580
  1.6 17.4 %collective-permute-start.1 = (bf16[3,64,128]{2,1,0:T(8,128)(2,1)}, bf16[3,64,128]{2,1,0:T(8,128)(2,1)S(1)}, u32[]{:S(2)}, u32[]{:S(2)}) collective-permute-start(bf16[3,64,128]{2,1,0:T(8,128)(2,1)} %get-tuple-element.13), channel_id=1, source_target_pairs={{16,0},{32,16},{48,32},{64,48},{80,64},{96,80},{112,96},{128,112},... | collective-permute-start | bytes 147464 | tf_op jit(solution)/shard_map/ppermute | solution.py:123
  12.4 31.8 %copy-start = (bf16[2,1024,256]{2,1,0:T(8,128)(2,1)S(1)}, bf16[2,1024,256]{2,1,0:T(8,128)(2,1)}, u32[]{:S(2)}) copy-start(bf16[2,1024,256]{2,1,0:T(8,128)(2,1)} %refs_3_.3) | copy-start | bytes 3145732
  12.4 31.8 %copy-start.1 = (bf16[2,256,1024]{2,1,0:T(8,128)(2,1)S(1)}, bf16[2,256,1024]{2,1,0:T(8,128)(2,1)}, u32[]{:S(2)}) copy-start(bf16[2,256,1024]{2,1,0:T(8,128)(2,1)} %refs_7_.3) | copy-start | bytes 3145732
  12.4 10.8 %collective-permute-start = (bf16[3,64,128]{2,1,0:T(8,128)(2,1)S(1)}, bf16[3,64,128]{2,1,0:T(8,128)(2,1)S(1)}, u32[]{:S(2)}, u32[]{:S(2)}) collective-permute-start(bf16[3,64,128]{2,1,0:T(8,128)(2,1)S(1)} %get-tuple-element.14), channel_id=1, source_target_pairs={{0,16},{16,32},{32,48},{48,64},{64,80},{80,96},{96,112},{112,128},... | collective-permute-start | bytes 147464 | tf_op jit(solution)/shard_map/ppermute | solution.py:122
  14.5 29.7 %collective-permute-start.2 = (bf16[2,1024,256]{2,1,0:T(8,128)(2,1)}, bf16[2,1024,256]{2,1,0:T(8,128)(2,1)S(1)}, u32[]{:S(2)}, u32[]{:S(2)}) collective-permute-start(bf16[2,1024,256]{2,1,0:T(8,128)(2,1)} %refs_3_.3), channel_id=1, source_target_pairs={{0,1},{1,0},{2,3},{3,2},{4,5},{5,4},{6,7},{7,6},{8,9},{9,8},{10,11... | collective-permute-start | bytes 3145736 | tf_op jit(solution)/shard_map/ppermute | solution.py:124
  16.4 27.7 %collective-permute-start.4 = (bf16[2,256,1024]{2,1,0:T(8,128)(2,1)}, bf16[2,256,1024]{2,1,0:T(8,128)(2,1)}, u32[]{:S(2)}, u32[]{:S(2)}) collective-permute-start(bf16[2,256,1024]{2,1,0:T(8,128)(2,1)} %refs_7_.3), channel_id=1, source_target_pairs={{0,1},{1,0},{2,3},{3,2},{4,5},{5,4},{6,7},{7,6},{8,9},{9,8},{10,11... | collective-permute-start | bytes 3145736 | tf_op jit(solution)/shard_map/ppermute | solution.py:125
  27.0 0.8 copy-start.3
  27.8 16.3 %all-to-all-start = ((bf16[16,64,256]{2,1,0:T(8,128)(2,1)}), bf16[16,64,256]{2,1,0:T(8,128)(2,1)}, u32[]{:S(2)}, u32[]{:S(2)}) async-start(bf16[16,64,256]{2,1,0:T(8,128)(2,1)} %bitcast.22), calls=%async_computation | async-start | bytes 1048576 | tf_op jit(solution)/shard_map/all_to_all | solution.py:136
  33.2 3.1 %collective-permute-start.3 = (f32[2,256]{1,0:T(2,128)S(1)}, f32[2,256]{1,0:T(2,128)S(1)}, u32[]{:S(2)}, u32[]{:S(2)}) collective-permute-start(f32[2,256]{1,0:T(2,128)S(1)} %copy-done.7), channel_id=1, source_target_pairs={{0,1},{1,0},{2,3},{3,2},{4,5},{5,4},{6,7},{7,6},{8,9},{9,8},{10,11... | collective-permute-start | bytes 6152 | tf_op jit(solution)/shard_map/ppermute | solution.py:126
  46.9 0.8 copy-start.2
  47.7 4.4 %copy-start.9 = (f32[2,64]{1,0:T(2,128)S(1)}, f32[2,64]{1,0:T(2,128)}, u32[]{:S(2)}) copy-start(f32[2,64]{1,0:T(2,128)} %param.16) | copy-start | bytes 1540
  47.7 4.4 %copy-start.10 = (f32[2,64]{1,0:T(2,128)S(1)}, f32[2,64]{1,0:T(2,128)}, u32[]{:S(2)}) copy-start(f32[2,64]{1,0:T(2,128)} %param.17) | copy-start | bytes 1540
  47.7 15.3 %all-to-all-start.1 = ((bf16[16,64,256]{2,1,0:T(8,128)(2,1)}), bf16[16,64,256]{2,1,0:T(8,128)(2,1)}, u32[]{:S(2)}, u32[]{:S(2)}) async-start(bf16[16,64,256]{2,1,0:T(8,128)(2,1)} %copy-done.2), calls=%async_computation.1 | async-start | bytes 1048576 | tf_op jit(solution)/shard_map/all_to_all | solution.py:142
  64.1 10.2 %collective-permute-start.5 = (bf16[3,64,128]{2,1,0:T(8,128)(2,1)S(1)}, bf16[3,64,128]{2,1,0:T(8,128)(2,1)S(1)}, u32[]{:S(2)}, u32[]{:S(2)}) collective-permute-start(bf16[3,64,128]{2,1,0:T(8,128)(2,1)S(1)} %get-tuple-element.8), channel_id=1, source_target_pairs={{0,16},{16,32},{32,48},{48,64},{64,80},{80,96},{96,112},{112,128},... | collective-permute-start | bytes 147464 | tf_op jit(solution)/shard_map/ppermute | solution.py:151
  66.1 9.9 %collective-permute-start.6 = (bf16[3,64,128]{2,1,0:T(8,128)(2,1)S(1)}, bf16[3,64,128]{2,1,0:T(8,128)(2,1)S(1)}, u32[]{:S(2)}, u32[]{:S(2)}) collective-permute-start(bf16[3,64,128]{2,1,0:T(8,128)(2,1)S(1)} %get-tuple-element.10), channel_id=1, source_target_pairs={{16,0},{32,16},{48,32},{64,48},{80,64},{96,80},{112,96},{128,112},... | collective-permute-start | bytes 147464 | tf_op jit(solution)/shard_map/ppermute | solution.py:152

commit v2 on v1

v2 whole, which is shorter than its diff:
```python
import jax
import jax.numpy as jnp
from jax import lax
from jax.experimental import pallas as pl
from jax.experimental.pallas import tpu as pltpu
from jax.sharding import PartitionSpec as P

D = 1024
TAPS = 7
HALF = TAPS // 2
BLOCKS = 2
CORES = 2

VMEM = pl.BlockSpec(memory_space=pltpu.VMEM)


def call(body, outs, *args):
    single = not isinstance(outs, (list, tuple))
    return pl.pallas_call(
        body,
        out_shape=outs,
        in_specs=[VMEM] * len(args),
        out_specs=VMEM if single else [VMEM] * len(outs),
        compiler_params=pltpu.CompilerParams(vmem_limit_bytes=48 << 20),
    )(*args)


def spread_kernel(cols_ref, wide_ref):
    for at in range(cols_ref.shape[1]):
        wide_ref[at] = jnp.broadcast_to(cols_ref[:, at : at + 1], wide_ref.shape[1:])


def pack_kernel(expand_ref, reduce_ref, hidden_bias_ref, pack_ref, sems):
    units = pack_ref.shape[2]
    moves = []
    for block in range(BLOCKS):
        moves.append((expand_ref.at[block], pack_ref.at[block, pl.ds(0, D)]))
        for part in range(D // units):
            moves.append((
                reduce_ref.at[block, :, pl.ds(units * part, units)],
                pack_ref.at[block, pl.ds(D + units * part, units)],
            ))
    copies = [pltpu.make_async_copy(src, dst, sems.at[i]) for i, (src, dst) in enumerate(moves)]
    for copy in copies:
        copy.start()
    for block in range(BLOCKS):
        rest = hidden_bias_ref[block : block + 1, :]
        pieces = []
        for _ in range(3):
            pieces.append(rest.astype(jnp.bfloat16))
            rest = rest - pieces[-1].astype(jnp.float32)
        pieces = [piece.astype(jnp.float32) for piece in pieces] + [jnp.zeros((5, units), jnp.float32)]
        pack_ref[block, 2 * D :, :] = jnp.concatenate(pieces, axis=0).astype(jnp.bfloat16)
    for copy in copies:
        copy.wait()


def packed(w_expand, w_reduce, hidden_bias):
    units = w_expand.shape[2]
    raw = pl.BlockSpec(memory_space=pl.ANY)
    return pl.pallas_call(
        pack_kernel,
        out_shape=jax.ShapeDtypeStruct((BLOCKS, 2 * D + 8, units), jnp.bfloat16),
        in_specs=[raw, raw, VMEM],
        out_specs=VMEM,
        scratch_shapes=[pltpu.SemaphoreType.DMA((BLOCKS * (1 + D // units),))],
        compiler_params=pltpu.CompilerParams(vmem_limit_bytes=48 << 20),
    )(w_expand, w_reduce, hidden_bias)


def conv_kernel(before_ref, rows_ref, after_ref, wide_ref, out_ref):
    height, share, width = rows_ref.shape
    copies = out_ref.shape[0]
    size = 16
    column = lax.broadcasted_iota(jnp.int32, (size, width), 1)
    inside = {
        shift: ((column + shift >= 0) & (column + shift < width)).astype(jnp.float32)
        for shift in range(-HALF, HALF + 1)
    }
    for group in range(share // size):
        chans = slice(size * group, size * (group + 1))
        rows = [before_ref[r, chans, :] for r in range(height - HALF, height)]
        rows += [rows_ref[r, chans, :] for r in range(height)]
        rows += [after_ref[r, chans, :] for r in range(HALF)]
        rows = [row.astype(jnp.float32) for row in rows]
        totals = [None] * height
        for j in range(TAPS):
            taps = [wide_ref[i * TAPS + j, chans, :] for i in range(TAPS)]
            shift = j - HALF
            for r in range(height):
                acc = rows[r] * taps[0]
                for i in range(1, TAPS):
                    acc = acc + rows[r + i] * taps[i]
                if shift:
                    acc = pltpu.roll(acc, (-shift) % width, 1) * inside[shift]
                totals[r] = acc if totals[r] is None else totals[r] + acc
        for r in range(height):
            half, at = divmod(r, height // CORES)
            value = totals[r].astype(jnp.bfloat16)
            for copy in range(copies):
                out_ref[copy, half, chans, width * at : width * (at + 1)] = value


def mlp_kernel(block, x_ref, gain_ref, bias_ref, expand_ref, reduce_ref, hidden_bias_ref, pack_ref, out_ref):
    x = x_ref[...].reshape(D, x_ref.shape[-1])
    x = jnp.transpose(x).astype(jnp.float32)
    mean = jnp.mean(x, axis=-1, keepdims=True)
    centered = x - mean
    var = jnp.mean(centered * centered, axis=-1, keepdims=True)
    gain = gain_ref[block : block + 1, :]
    bias = bias_ref[block : block + 1, :]
    normed = (centered * lax.rsqrt(var + 1e-06) * gain + bias).astype(jnp.bfloat16)

    def units_of(weights, unit_bias):
        preact = jnp.dot(normed, weights, preferred_element_type=jnp.float32) + unit_bias
        return (0.5 * preact * (1.0 + lax.erf(preact * (0.5**0.5)))).astype(jnp.bfloat16)

    pieces = pack_ref[block, 2 * D :, :].astype(jnp.float32)
    own = units_of(expand_ref[block], hidden_bias_ref[block : block + 1, :])
    other = units_of(pack_ref[block, :D, :], pieces[0:1] + pieces[1:2] + pieces[2:3])
    units = own.shape[1]
    chips, cores, share, half = out_ref.shape
    for part in range(D // units):
        total = jnp.dot(
            own, reduce_ref[block, :, units * part : units * (part + 1)], preferred_element_type=jnp.float32
        ) + jnp.dot(
            other, pack_ref[block, D + units * part : D + units * (part + 1), :], preferred_element_type=jnp.float32
        )
        total = jnp.transpose(total.astype(jnp.bfloat16))
        for at in range(units // share):
            chip, core = divmod(part * (units // share) + at, cores)
            out_ref[chip, core] = total[share * at : share * (at + 1), :]


def mix_kernel(parts_ref, stream_ref, wide_ref, out_ref):
    height, share, width = stream_ref.shape
    scale, shift = wide_ref[TAPS * TAPS], wide_ref[TAPS * TAPS + 1]
    for r in range(height):
        half, at = divmod(r, height // CORES)
        lanes = slice(width * at, width * (at + 1))
        mixed = parts_ref[0, half, :, lanes].astype(jnp.float32)
        for copy in range(1, parts_ref.shape[0]):
            mixed = mixed + parts_ref[copy, half, :, lanes].astype(jnp.float32)
        updated = stream_ref[r].astype(jnp.float32) + scale * (mixed + shift)
        out_ref[r] = updated.astype(jnp.bfloat16)


def per_device(features, depth_kernel, norm_gain, norm_bias, w_expand, b_expand, w_reduce, b_reduce, layer_scale):
    height, width, share = features.shape
    bands, members = lax.axis_size("space"), lax.axis_size("tensor")
    copies = members // CORES
    half = height // CORES * width
    down = [(i, i + 1) for i in range(bands - 1)]
    up = [(j, i) for i, j in down]
    sibling = [(i, i ^ 1) for i in range(members)]

    stream = jnp.transpose(features, (0, 2, 1))
    cols = jnp.concatenate(
        [
            depth_kernel.reshape(BLOCKS, TAPS * TAPS, share).astype(jnp.float32),
            layer_scale[:, None, :],
            b_reduce[:, None, :],
        ],
        axis=1,
    )
    cols = jnp.transpose(cols, (0, 2, 1))

    for block in range(BLOCKS):
        after = lax.ppermute(stream, "space", up)
        before = lax.ppermute(stream, "space", down)
        if block == 0:
            after, cols, own_bias = lax.optimization_barrier((after, cols, b_expand))
            pack = packed(w_expand, w_reduce, own_bias)
        else:
            after, cols = lax.optimization_barrier((after, cols))
        wide = call(
            spread_kernel, jax.ShapeDtypeStruct((TAPS * TAPS + 2, share, width), jnp.float32), cols[block]
        )
        filtered = call(
            conv_kernel,
            jax.ShapeDtypeStruct((copies, CORES, share, half), jnp.bfloat16),
            before, stream, after, wide,
        )
        if block == 0:
            filtered, pack = lax.optimization_barrier((filtered, pack))
            pack = lax.ppermute(pack, "tensor", sibling)
        filtered = lax.all_to_all(filtered.reshape(members, share, half), "tensor", 0, 0, tiled=True)
        partial = call(
            lambda *refs: mlp_kernel(block, *refs),
            jax.ShapeDtypeStruct((copies, CORES, share, half), jnp.bfloat16),
            filtered, norm_gain, norm_bias, w_expand, w_reduce, b_expand, pack,
        )
        partial = lax.all_to_all(partial.reshape(members, share, half), "tensor", 0, 0, tiled=True)
        stream = call(
            mix_kernel,
            jax.ShapeDtypeStruct((height, share, width), jnp.bfloat16),
            partial.reshape(copies, CORES, share, half), stream, wide,
        )
    return jnp.transpose(stream, (0, 2, 1))


def solution(mesh):
    return jax.shard_map(
        per_device,
        mesh=mesh,
        in_specs=(
            P("space", None, "tensor"),
            P(None, None, None, "tensor"),
            P(),
            P(),
            P(None, None, "tensor"),
            P(None, "tensor"),
            P(None, "tensor", None),
            P(None, "tensor"),
            P(None, "tensor"),
        ),
        out_specs=P("space", None, "tensor"),
        check_vma=False,
    )
```

time: 111 us -> 99.2 us (0.89)
  blocking collectives: 27 us -> 56.5 us
  starting transfers between devices: 39.3 us -> 21.5 us
  waiting for transfers between devices: 25.4 us -> 11.8 us
  Pallas kernels: 14.7 us -> 6.08 us
  local copies, waits for them, and re-layouts: 3.37 us -> 1.68 us
    all_to_all x2 -> x0, waiting for transfers between devices: 18.6 us -> none  [the longest x1 10.7 us: per_device(): lax.all_to_all(partial, 'tensor', 0, 0, tiled=True)]
    all_to_all x1 -> x2, blocking collectives: 13.5 us -> 29.6 us  [per_device(): lax.all_to_all(filtered.reshape(members, share, half), 'tensor', 0, 0, ti...]
    all_to_all x1 -> x2, blocking collectives: 13.5 us -> 27 us  [per_device(): lax.all_to_all(partial.reshape(members, share, half), 'tensor', 0, 0, til...]
    all_to_all x2 -> x0, starting transfers between devices: 9.74 us -> none  [the longest x1 5.37 us: per_device(): lax.all_to_all(filtered.reshape(members, share, half), 'tensor', 0, 0, ti...]
    pallas_call x6 -> x8, Pallas kernels: 14.7 us -> 5.73 us  [call(): pl.pallas_call(body, out_shape=outs, in_specs=[VMEM] * len(args), out_spe...]
    ppermute x7 -> x5, starting transfers between devices: 29.5 us -> 21.5 us  [the longest x2 13.7 us: per_device(): after = lax.ppermute(stream, 'space', up)]
    ppermute x7 -> x5, waiting for transfers between devices: 6.83 us -> 11.8 us  [the longest x2 10.8 us: per_device(): before = lax.ppermute(stream, 'space', down)]
    unnamed x22 -> x12, local copies, waits for them, and re-layouts: 1.62 us -> 0.03 us
  transfers between devices with their start and end apart: 9 -> 5, of which waited for: 6 -> 3; matrix products, arithmetic and copies ran while one was open for 0% -> 3% of each run, Pallas kernels for 3% -> 1%
where the time goes in v2:
time: 99.2 us; the launch traced here: 98.7 us
  blocking collectives  56.5 us (57%)
  starting transfers between devices  21.5 us (22%)
  waiting for transfers between devices  11.8 us (12%)
  Pallas kernels  6.08 us (6%)
  local copies, waits for them, and re-layouts  1.68 us (2%)
    all_to_all x2, blocking collectives, per_device(): lax.all_to_all(filtered.reshape(members, share, half), 'tensor', 0, 0, ti...  29.6 us
    all_to_all x2, blocking collectives, per_device(): lax.all_to_all(partial.reshape(members, share, half), 'tensor', 0, 0, til...  27 us
    ppermute x2, starting transfers between devices, per_device(): after = lax.ppermute(stream, 'space', up)  13.7 us
    ppermute x2, waiting for transfers between devices, per_device(): before = lax.ppermute(stream, 'space', down)  10.8 us
    ppermute x2, starting transfers between devices, per_device(): before = lax.ppermute(stream, 'space', down)  5.88 us
    pallas_call x8, Pallas kernels, call(): pl.pallas_call(body, out_shape=outs, in_specs=[VMEM] * len(args), out_spe...  5.73 us
  transfers between devices with their start and end apart: 5, of which 3 were waited for; matrix products, arithmetic and copies ran while one was open for 3% of the time, Pallas kernels for 1%

profile of v2, /device:TPU:32, one launch (start us, length us, event | category | flops | bytes accessed | tf_op | source)
XLA Modules:
  0.0 98.7 jit_solution(5865987275198294031)
XLA Ops:
  0.0 0.0 copy-start.5
  0.0 0.0 copy-start.1
  0.0 0.0 copy-start
  0.0 11.0 %collective-permute-start.1 = (bf16[4,64,128]{2,1,0:T(8,128)(2,1)}, bf16[4,64,128]{2,1,0:T(8,128)(2,1)S(1)}, u32[]{:S(2)}, u32[]{:S(2)}) collective-permute-start(bf16[4,64,128]{2,1,0:T(8,128)(2,1)} %bitcast.25), channel_id=1, source_target_pairs={{16,0},{32,16},{48,32},{64,48},{80,64},{96,80},{112,96},{128,112},... | collective-permute-start | bytes 196616 | tf_op jit(solution)/shard_map/ppermute | solution.py:169
  11.0 1.9 %collective-permute-start = (bf16[4,64,128]{2,1,0:T(8,128)(2,1)}, bf16[4,64,128]{2,1,0:T(8,128)(2,1)S(1)}, u32[]{:S(2)}, u32[]{:S(2)}) collective-permute-start(bf16[4,64,128]{2,1,0:T(8,128)(2,1)} %bitcast.26), channel_id=1, source_target_pairs={{0,16},{16,32},{32,48},{48,64},{64,80},{80,96},{96,112},{112,128},... | collective-permute-start | bytes 196616 | tf_op jit(solution)/shard_map/ppermute | solution.py:170
  12.9 0.8 bitcast_convert_fusion
  13.7 0.1 copy.13
  13.8 0.8 copy.15
  14.5 0.8 copy.14
  15.3 0.1 maximum_bitcast_fusion
  15.4 0.0 collective-permute-done.1.after_ref
  15.5 0.6 shard_map.91.wide_ref
  16.0 0.0 copy-done.5
  16.0 0.0 copy-done.1
  16.0 0.0 copy-done
  16.1 0.0 copy-start.2
  16.1 0.3 shard_map.93
  16.4 0.0 copy-start.3
  16.4 0.0 copy-start.4
  16.4 5.8 %collective-permute-done.before_ref = bf16[4,64,128]{2,1,0:T(8,128)(2,1)S(1)} collective-permute-done((bf16[4,64,128]{2,1,0:T(8,128)(2,1)}, bf16[4,64,128]{2,1,0:T(8,128)(2,1)S(1)}, u32[]{:S(2)}, u32[]{:S(2)}) %collective-permute-start) | collective-permute-done | bytes 65568 | tf_op jit(solution)/shard_map/ppermute | solution.py:170
  22.3 0.0 copy-done.2
  22.3 0.5 shard_map.92
  22.8 1.9 %collective-permute-start.2 = (bf16[2,2056,256]{2,1,0:T(8,128)(2,1)S(1)}, bf16[2,2056,256]{2,1,0:T(8,128)(2,1)S(1)}, u32[]{:S(2)}, u32[]{:S(2)}) collective-permute-start(bf16[2,2056,256]{2,1,0:T(8,128)(2,1)S(1)} %shard_map.93), channel_id=1, source_target_pairs={{0,1},{1,0},{2,3},{3,2},{4,5},{5,4},{6,7},{7,6},{8,9},{9,8},{10,11... | collective-permute-start | bytes 6316040 | tf_op jit(solution)/shard_map/ppermute | solution.py:186
  24.7 16.1 %all_to_all.20.refs_0_ = bf16[16,64,256]{2,1,0:T(8,128)(2,1)S(1)} all-to-all(bf16[16,64,256]{2,1,0:T(8,128)(2,1)S(1)} %bitcast.21), channel_id=1, replica_groups=mesh['space'=32,'tensor'=16] {'tensor'}, dimensions={0} | all-to-all | bytes 1048576 | tf_op jit(solution)/shard_map/all_to_all | solution.py:187
  40.8 0.0 collective-permute-done.2.refs_6_
  40.8 0.0 copy-done.3
  40.8 0.0 copy-done.4
  40.8 1.4 %shard_map.94 = bf16[8,2,64,256]{3,2,1,0:T(8,128)(2,1)S(1)} custom-call(bf16[16,64,256]{2,1,0:T(8,128)(2,1)S(1)} %all_to_all.20.refs_0_, f32[2,1024]{1,0:T(2,128)S(1)} %copy-done.3, f32[2,1024]{1,0:T(2,128)S(1)} %copy-done.4, bf16[2,1024,256]{2,1,0:T(8,128)(2,1)S(1)} %copy-done, bf16[2,256,1024]{2,1,0:T(8,128)(2,1)S(1)} %copy-done.1, ...), custom_call_target="tpu_custom_call" | custom-call | tf_op jit(solution)/shard_map/pallas_call | solution.py:19
  42.2 13.5 %all_to_all.21 = bf16[16,64,256]{2,1,0:T(8,128)(2,1)S(1)} all-to-all(bf16[16,64,256]{2,1,0:T(8,128)(2,1)S(1)} %bitcast.20), channel_id=1, replica_groups=mesh['space'=32,'tensor'=16] {'tensor'}, dimensions={0} | all-to-all | bytes 1048576 | tf_op jit(solution)/shard_map/all_to_all | solution.py:193
  55.7 0.1 shard_map.95.rows_ref.stream_ref
  55.8 2.8 %collective-permute-start.4 = (bf16[4,64,128]{2,1,0:T(8,128)(2,1)S(1)}, bf16[4,64,128]{2,1,0:T(8,128)(2,1)S(1)}, u32[]{:S(2)}, u32[]{:S(2)}) collective-permute-start(bf16[4,64,128]{2,1,0:T(8,128)(2,1)S(1)} %shard_map.95.rows_ref.stream_ref), channel_id=1, source_target_pairs={{16,0},{32,16},{48,32},{64,48},{80,64},{96,80},{112,96},{128,112},... | collective-permute-start | bytes 196616 | tf_op jit(solution)/shard_map/ppermute | solution.py:169
  58.6 4.0 %collective-permute-start.3 = (bf16[4,64,128]{2,1,0:T(8,128)(2,1)S(1)}, bf16[4,64,128]{2,1,0:T(8,128)(2,1)S(1)}, u32[]{:S(2)}, u32[]{:S(2)}) collective-permute-start(bf16[4,64,128]{2,1,0:T(8,128)(2,1)S(1)} %shard_map.95.rows_ref.stream_ref), channel_id=1, source_target_pairs={{0,16},{16,32},{32,48},{48,64},{64,80},{80,96},{96,112},{112,128},... | collective-permute-start | bytes 196616 | tf_op jit(solution)/shard_map/ppermute | solution.py:170
  62.5 1.0 %collective-permute-done.4.after_ref = bf16[4,64,128]{2,1,0:T(8,128)(2,1)S(1)} collective-permute-done((bf16[4,64,128]{2,1,0:T(8,128)(2,1)S(1)}, bf16[4,64,128]{2,1,0:T(8,128)(2,1)S(1)}, u32[]{:S(2)}, u32[]{:S(2)}) %collective-permute-start.4) | collective-permute-done | bytes 65568 | tf_op jit(solution)/shard_map/ppermute | solution.py:169
  63.6 0.6 shard_map.96.wide_ref
  64.1 5.0 %collective-permute-done.3.before_ref = bf16[4,64,128]{2,1,0:T(8,128)(2,1)S(1)} collective-permute-done((bf16[4,64,128]{2,1,0:T(8,128)(2,1)S(1)}, bf16[4,64,128]{2,1,0:T(8,128)(2,1)S(1)}, u32[]{:S(2)}, u32[]{:S(2)}) %collective-permute-start.3) | collective-permute-done | bytes 65568 | tf_op jit(solution)/shard_map/ppermute | solution.py:170
  69.1 0.5 shard_map.97
  69.7 13.5 %all_to_all.22.refs_0_ = bf16[16,64,256]{2,1,0:T(8,128)(2,1)S(1)} all-to-all(bf16[16,64,256]{2,1,0:T(8,128)(2,1)S(1)} %bitcast.24), channel_id=1, replica_groups=mesh['space'=32,'tensor'=16] {'tensor'}, dimensions={0} | all-to-all | bytes 1048576 | tf_op jit(solution)/shard_map/all_to_all | solution.py:187
  83.2 1.4 %shard_map.98 = bf16[8,2,64,256]{3,2,1,0:T(8,128)(2,1)S(1)} custom-call(bf16[16,64,256]{2,1,0:T(8,128)(2,1)S(1)} %all_to_all.22.refs_0_, f32[2,1024]{1,0:T(2,128)S(1)} %copy-done.3, f32[2,1024]{1,0:T(2,128)S(1)} %copy-done.4, bf16[2,1024,256]{2,1,0:T(8,128)(2,1)S(1)} %copy-done, bf16[2,256,1024]{2,1,0:T(8,128)(2,1)S(1)} %copy-done.1, ...), custom_call_target="tpu_custom_call" | custom-call | tf_op jit(solution)/shard_map/pallas_call | solution.py:19
  84.5 13.5 %all_to_all.23 = bf16[16,64,256]{2,1,0:T(8,128)(2,1)S(1)} all-to-all(bf16[16,64,256]{2,1,0:T(8,128)(2,1)S(1)} %bitcast.19), channel_id=1, replica_groups=mesh['space'=32,'tensor'=16] {'tensor'}, dimensions={0} | all-to-all | bytes 1048576 | tf_op jit(solution)/shard_map/all_to_all | solution.py:193
  98.0 0.7 shard_map.99
  (2 shorter events, 0.0 us)
Async XLA Ops:
  0.0 16.0 %copy-start.5 = (f32[2,256]{1,0:T(2,128)S(1)}, f32[2,256]{1,0:T(2,128)}, u32[]{:S(2)}) copy-start(f32[2,256]{1,0:T(2,128)} %refs_5_.3) | copy-start | bytes 6148
  0.0 16.0 %copy-start.1 = (bf16[2,256,1024]{2,1,0:T(8,128)(2,1)S(1)}, bf16[2,256,1024]{2,1,0:T(8,128)(2,1)}, u32[]{:S(2)}) copy-start(bf16[2,256,1024]{2,1,0:T(8,128)(2,1)} %refs_4_.3) | copy-start | bytes 3145732
  0.0 16.0 %copy-start = (bf16[2,1024,256]{2,1,0:T(8,128)(2,1)S(1)}, bf16[2,1024,256]{2,1,0:T(8,128)(2,1)}, u32[]{:S(2)}) copy-start(bf16[2,1024,256]{2,1,0:T(8,128)(2,1)} %refs_3_.3) | copy-start | bytes 3145732
  0.0 15.4 %collective-permute-start.1 = (bf16[4,64,128]{2,1,0:T(8,128)(2,1)}, bf16[4,64,128]{2,1,0:T(8,128)(2,1)S(1)}, u32[]{:S(2)}, u32[]{:S(2)}) collective-permute-start(bf16[4,64,128]{2,1,0:T(8,128)(2,1)} %bitcast.25), channel_id=1, source_target_pairs={{16,0},{32,16},{48,32},{64,48},{80,64},{96,80},{112,96},{128,112},... | collective-permute-start | bytes 196616 | tf_op jit(solution)/shard_map/ppermute | solution.py:169
  11.0 11.3 %collective-permute-start = (bf16[4,64,128]{2,1,0:T(8,128)(2,1)}, bf16[4,64,128]{2,1,0:T(8,128)(2,1)S(1)}, u32[]{:S(2)}, u32[]{:S(2)}) collective-permute-start(bf16[4,64,128]{2,1,0:T(8,128)(2,1)} %bitcast.26), channel_id=1, source_target_pairs={{0,16},{16,32},{32,48},{48,64},{64,80},{80,96},{96,112},{112,128},... | collective-permute-start | bytes 196616 | tf_op jit(solution)/shard_map/ppermute | solution.py:170
  16.1 6.2 %copy-start.2 = (bf16[4,128,64]{1,2,0:T(8,128)(2,1)S(1)}, bf16[4,128,64]{1,2,0:T(8,128)(2,1)}, u32[]{:S(2)}) copy-start(bf16[4,128,64]{1,2,0:T(8,128)(2,1)} %param.9) | copy-start | bytes 196612
  16.4 24.4 %copy-start.3 = (f32[2,1024]{1,0:T(2,128)S(1)}, f32[2,1024]{1,0:T(2,128)}, u32[]{:S(2)}) copy-start(f32[2,1024]{1,0:T(2,128)} %refs_1_.3) | copy-start | bytes 24580
  16.4 24.4 %copy-start.4 = (f32[2,1024]{1,0:T(2,128)S(1)}, f32[2,1024]{1,0:T(2,128)}, u32[]{:S(2)}) copy-start(f32[2,1024]{1,0:T(2,128)} %refs_2_.3) | copy-start | bytes 24580
  22.8 18.0 %collective-permute-start.2 = (bf16[2,2056,256]{2,1,0:T(8,128)(2,1)S(1)}, bf16[2,2056,256]{2,1,0:T(8,128)(2,1)S(1)}, u32[]{:S(2)}, u32[]{:S(2)}) collective-permute-start(bf16[2,2056,256]{2,1,0:T(8,128)(2,1)S(1)} %shard_map.93), channel_id=1, source_target_pairs={{0,1},{1,0},{2,3},{3,2},{4,5},{5,4},{6,7},{7,6},{8,9},{9,8},{10,11... | collective-permute-start | bytes 6316040 | tf_op jit(solution)/shard_map/ppermute | solution.py:186
  55.8 7.8 %collective-permute-start.4 = (bf16[4,64,128]{2,1,0:T(8,128)(2,1)S(1)}, bf16[4,64,128]{2,1,0:T(8,128)(2,1)S(1)}, u32[]{:S(2)}, u32[]{:S(2)}) collective-permute-start(bf16[4,64,128]{2,1,0:T(8,128)(2,1)S(1)} %shard_map.95.rows_ref.stream_ref), channel_id=1, source_target_pairs={{16,0},{32,16},{48,32},{64,48},{80,64},{96,80},{112,96},{128,112},... | collective-permute-start | bytes 196616 | tf_op jit(solution)/shard_map/ppermute | solution.py:169
  58.6 10.6 %collective-permute-start.3 = (bf16[4,64,128]{2,1,0:T(8,128)(2,1)S(1)}, bf16[4,64,128]{2,1,0:T(8,128)(2,1)S(1)}, u32[]{:S(2)}, u32[]{:S(2)}) collective-permute-start(bf16[4,64,128]{2,1,0:T(8,128)(2,1)S(1)} %shard_map.95.rows_ref.stream_ref), channel_id=1, source_target_pairs={{0,16},{16,32},{32,48},{48,64},{64,80},{80,96},{96,112},{112,128},... | collective-permute-start | bytes 196616 | tf_op jit(solution)/shard_map/ppermute | solution.py:170

commit v3 on v2

--- a/solution.py
+++ b/solution.py
@@ -14,58 +14,58 @@
 VMEM = pl.BlockSpec(memory_space=pltpu.VMEM)
 
 
-def call(body, outs, *args):
+def call(body, outs, *args, cost=None):
     single = not isinstance(outs, (list, tuple))
     return pl.pallas_call(
         body,
         out_shape=outs,
         in_specs=[VMEM] * len(args),
         out_specs=VMEM if single else [VMEM] * len(outs),
+        cost_estimate=cost,
         compiler_params=pltpu.CompilerParams(vmem_limit_bytes=48 << 20),
     )(*args)
 
 
-def spread_kernel(cols_ref, wide_ref):
-    for at in range(cols_ref.shape[1]):
-        wide_ref[at] = jnp.broadcast_to(cols_ref[:, at : at + 1], wide_ref.shape[1:])
-
-
-def pack_kernel(expand_ref, reduce_ref, hidden_bias_ref, pack_ref, sems):
-    units = pack_ref.shape[2]
-    moves = []
-    for block in range(BLOCKS):
-        moves.append((expand_ref.at[block], pack_ref.at[block, pl.ds(0, D)]))
-        for part in range(D // units):
-            moves.append((
-                reduce_ref.at[block, :, pl.ds(units * part, units)],
-                pack_ref.at[block, pl.ds(D + units * part, units)],
-            ))
+def spread_kernel(block, taps_ref, scale_ref, shift_ref, wide_ref):
+    rows = [taps_ref[:, block, :].astype(jnp.float32), scale_ref[block : block + 1, :], shift_ref[block : block + 1, :]]
+    cols = jnp.transpose(jnp.concatenate(rows, axis=0))
+    for at in range(cols.shape[1]):
+        wide_ref[at] = jnp.broadcast_to(cols[:, at : at + 1], wide_ref.shape[1:])
+
+
+def pack_kernel(block, expand_ref, reduce_ref, bias_ref, pack_ref, held_ref, sems):
+    units = pack_ref.shape[1]
+    moves = [(expand_ref.at[block], pack_ref.at[pl.ds(0, D)])]
+    for part in range(D // units):
+        columns = pl.ds(units * part, units)
+        moves.append((reduce_ref.at[block, :, columns], pack_ref.at[pl.ds(D + units * part, units)]))
+    moves.append((bias_ref, held_ref))
     copies = [pltpu.make_async_copy(src, dst, sems.at[i]) for i, (src, dst) in enumerate(moves)]
-    for copy in copies:
+    for copy in reversed(copies):
         copy.start()
-    for block in range(BLOCKS):
-        rest = hidden_bias_ref[block : block + 1, :]
-        pieces = []
-        for _ in range(3):
-            pieces.append(rest.astype(jnp.bfloat16))
-            rest = rest - pieces[-1].astype(jnp.float32)
-        pieces = [piece.astype(jnp.float32) for piece in pieces] + [jnp.zeros((5, units), jnp.float32)]
-        pack_ref[block, 2 * D :, :] = jnp.concatenate(pieces, axis=0).astype(jnp.bfloat16)
+    copies.pop().wait()
+    rest = held_ref[block : block + 1, :]
+    pieces = []
+    for _ in range(3):
+        pieces.append(rest.astype(jnp.bfloat16))
+        rest = rest - pieces[-1].astype(jnp.float32)
+    pieces = [piece.astype(jnp.float32) for piece in pieces] + [jnp.zeros((5, units), jnp.float32)]
+    pack_ref[2 * D :, :] = jnp.concatenate(pieces, axis=0).astype(jnp.bfloat16)
     for copy in copies:
         copy.wait()
 
 
-def packed(w_expand, w_reduce, hidden_bias):
+def packed(block, w_expand, w_reduce, hidden_bias):
     units = w_expand.shape[2]
-    raw = pl.BlockSpec(memory_space=pl.ANY)
+    raw = pl.BlockSpec(memory_space=pltpu.HBM)
     return pl.pallas_call(
-        pack_kernel,
-        out_shape=jax.ShapeDtypeStruct((BLOCKS, 2 * D + 8, units), jnp.bfloat16),
-        in_specs=[raw, raw, VMEM],
+        lambda *refs: pack_kernel(block, *refs),
+        out_shape=jax.ShapeDtypeStruct((2 * D + 8, units), jnp.bfloat16),
+        in_specs=[raw, raw, raw],
         out_specs=VMEM,
-        scratch_shapes=[pltpu.SemaphoreType.DMA((BLOCKS * (1 + D // units),))],
+        scratch_shapes=[pltpu.VMEM(hidden_bias.shape, jnp.float32), pltpu.SemaphoreType.DMA((2 + D // units,))],
         compiler_params=pltpu.CompilerParams(vmem_limit_bytes=48 << 20),
-    )(w_expand, w_reduce, hidden_bias)
+    )(*[pltpu.with_memory_space_constraint(array, pltpu.HBM) for array in (w_expand, w_reduce, hidden_bias)])
 
 
 def conv_kernel(before_ref, rows_ref, after_ref, wide_ref, out_ref):
@@ -115,16 +115,16 @@
         preact = jnp.dot(normed, weights, preferred_element_type=jnp.float32) + unit_bias
         return (0.5 * preact * (1.0 + lax.erf(preact * (0.5**0.5)))).astype(jnp.bfloat16)
 
-    pieces = pack_ref[block, 2 * D :, :].astype(jnp.float32)
+    pieces = pack_ref[2 * D :, :].astype(jnp.float32)
     own = units_of(expand_ref[block], hidden_bias_ref[block : block + 1, :])
-    other = units_of(pack_ref[block, :D, :], pieces[0:1] + pieces[1:2] + pieces[2:3])
+    other = units_of(pack_ref[:D, :], pieces[0:1] + pieces[1:2] + pieces[2:3])
     units = own.shape[1]
     chips, cores, share, half = out_ref.shape
     for part in range(D // units):
         total = jnp.dot(
             own, reduce_ref[block, :, units * part : units * (part + 1)], preferred_element_type=jnp.float32
         ) + jnp.dot(
-            other, pack_ref[block, D + units * part : D + units * (part + 1), :], preferred_element_type=jnp.float32
+            other, pack_ref[D + units * part : D + units * (part + 1), :], preferred_element_type=jnp.float32
         )
         total = jnp.transpose(total.astype(jnp.bfloat16))
         for at in range(units // share):
@@ -155,35 +155,24 @@
     sibling = [(i, i ^ 1) for i in range(members)]
 
     stream = jnp.transpose(features, (0, 2, 1))
-    cols = jnp.concatenate(
-        [
-            depth_kernel.reshape(BLOCKS, TAPS * TAPS, share).astype(jnp.float32),
-            layer_scale[:, None, :],
-            b_reduce[:, None, :],
-        ],
-        axis=1,
-    )
-    cols = jnp.transpose(cols, (0, 2, 1))
+    taps = jnp.transpose(depth_kernel, (1, 2, 0, 3)).reshape(TAPS * TAPS, BLOCKS, share)
 
     for block in range(BLOCKS):
         after = lax.ppermute(stream, "space", up)
         before = lax.ppermute(stream, "space", down)
-        if block == 0:
-            after, cols, own_bias = lax.optimization_barrier((after, cols, b_expand))
-            pack = packed(w_expand, w_reduce, own_bias)
-        else:
-            after, cols = lax.optimization_barrier((after, cols))
+        after, layer_scale, own_bias = lax.optimization_barrier((after, layer_scale, b_expand))
         wide = call(
-            spread_kernel, jax.ShapeDtypeStruct((TAPS * TAPS + 2, share, width), jnp.float32), cols[block]
-        )
+            lambda *refs: spread_kernel(block, *refs),
+            jax.ShapeDtypeStruct((TAPS * TAPS + 2, share, width), jnp.float32),
+            taps, layer_scale, b_reduce,
+        )
+        pack = lax.ppermute(packed(block, w_expand, w_reduce, own_bias), "tensor", sibling)
         filtered = call(
             conv_kernel,
             jax.ShapeDtypeStruct((copies, CORES, share, half), jnp.bfloat16),
             before, stream, after, wide,
-        )
-        if block == 0:
-            filtered, pack = lax.optimization_barrier((filtered, pack))
-            pack = lax.ppermute(pack, "tensor", sibling)
+            cost=pl.CostEstimate(flops=10**9, transcendentals=0, bytes_accessed=10**6),
+        )
         filtered = lax.all_to_all(filtered.reshape(members, share, half), "tensor", 0, 0, tiled=True)
         partial = call(
             lambda *refs: mlp_kernel(block, *refs),

time: 99.2 us -> 98.8 us (level)
  waiting for transfers between devices: 11.8 us -> 8.87 us
  Pallas kernels: 6.08 us -> 8.77 us
  starting transfers between devices: 21.5 us -> 23.6 us
  local copies, waits for them, and re-layouts: 1.68 us -> 0.06 us
    ppermute x2, waiting for transfers between devices: 10.8 us -> 7.55 us  [per_device(): before = lax.ppermute(stream, 'space', down)]
    pallas_call x1 -> x2, Pallas kernels: 0.35 us -> 2.76 us  [packed(): pl.pallas_call(lambda *refs: pack_kernel(block, *refs), out_shape=jax.Sha...]
    ppermute x1 -> x2, starting transfers between devices: 1.92 us -> 3.97 us  [per_device(): lax.ppermute(packed(block, w_expand, w_reduce, own_bias), 'tensor', sibling)]
    broadcast_in_dim x2 -> x0, local copies, waits for them, and re-layouts: 1.55 us -> none  [the longest x1 0.78 us: per_device(): layer_scale[:, None, :]]
    ppermute x2, starting transfers between devices: 5.88 us -> 4.76 us  [per_device(): before = lax.ppermute(stream, 'space', down)]
    ppermute x2, starting transfers between devices: 13.7 us -> 14.9 us  [per_device(): after = lax.ppermute(stream, 'space', up)]
  transfers between devices with their start and end apart: 5 -> 6, of which waited for: 3 -> 4; matrix products, arithmetic and copies ran while one was open for 3% -> 0% of each run, Pallas kernels for 1% -> 5%
where the time goes in v3:
time: 98.8 us; the launch traced here: 98.2 us
  blocking collectives  56.7 us (57%)
  starting transfers between devices  23.6 us (24%)
  waiting for transfers between devices  8.87 us (9%)
  Pallas kernels  8.77 us (9%)
    all_to_all x2, blocking collectives, per_device(): lax.all_to_all(filtered.reshape(members, share, half), 'tensor', 0, 0, ti...  29.7 us
    all_to_all x2, blocking collectives, per_device(): lax.all_to_all(partial.reshape(members, share, half), 'tensor', 0, 0, til...  27 us
    ppermute x2, starting transfers between devices, per_device(): after = lax.ppermute(stream, 'space', up)  14.9 us
    ppermute x2, waiting for transfers between devices, per_device(): before = lax.ppermute(stream, 'space', down)  7.55 us
    pallas_call x8, Pallas kernels, call(): pl.pallas_call(body, out_shape=outs, in_specs=[VMEM] * len(args), out_spe...  6.01 us
    ppermute x2, starting transfers between devices, per_device(): before = lax.ppermute(stream, 'space', down)  4.76 us
    ppermute x2, starting transfers between devices, per_device(): lax.ppermute(packed(block, w_expand, w_reduce, own_bias), 'tensor', sibling)  3.97 us
    pallas_call x2, Pallas kernels, packed(): pl.pallas_call(lambda *refs: pack_kernel(block, *refs), out_shape=jax.Sha...  2.76 us
  transfers between devices with their start and end apart: 6, of which 4 were waited for; matrix products, arithmetic and copies ran while one was open for 0% of the time, Pallas kernels for 5%

profile of v3, /device:TPU:32, one launch (start us, length us, event | category | flops | bytes accessed | tf_op | source)
XLA Modules:
  0.0 98.2 jit_solution(10108711182039226950)
XLA Ops:
  0.0 0.0 copy-start.4
  0.0 0.0 copy-start.10
  0.0 0.0 copy-start.11
  0.0 11.0 %collective-permute-start.1 = (bf16[4,64,128]{2,1,0:T(8,128)(2,1)}, bf16[4,64,128]{2,1,0:T(8,128)(2,1)S(1)}, u32[]{:S(2)}, u32[]{:S(2)}) collective-permute-start(bf16[4,64,128]{2,1,0:T(8,128)(2,1)} %bitcast.19), channel_id=1, source_target_pairs={{16,0},{32,16},{48,32},{64,48},{80,64},{96,80},{112,96},{128,112},... | collective-permute-start | bytes 196616 | tf_op jit(solution)/shard_map/ppermute | solution.py:161
  11.0 1.9 %collective-permute-start = (bf16[4,64,128]{2,1,0:T(8,128)(2,1)}, bf16[4,64,128]{2,1,0:T(8,128)(2,1)S(1)}, u32[]{:S(2)}, u32[]{:S(2)}) collective-permute-start(bf16[4,64,128]{2,1,0:T(8,128)(2,1)} %bitcast.20), channel_id=1, source_target_pairs={{0,16},{16,32},{32,48},{48,64},{64,80},{80,96},{96,112},{112,128},... | collective-permute-start | bytes 196616 | tf_op jit(solution)/shard_map/ppermute | solution.py:162
  12.9 0.3 collective-permute-done.1.after_ref
  13.2 1.4 %shard_map.93 = bf16[2056,256]{1,0:T(8,128)(2,1)S(1)} custom-call(bf16[2,1024,256]{2,1,0:T(8,128)(2,1)} %refs_3_.3, bf16[2,256,1024]{2,1,0:T(8,128)(2,1)} %refs_4_.3, f32[2,256]{1,0:T(2,128)} %refs_5_.3), custom_call_target="tpu_custom_call" | custom-call | tf_op jit(solution)/shard_map/pallas_call | solution.py:61
  14.6 0.0 copy-start.5
  14.6 2.1 %collective-permute-start.2 = (bf16[2056,256]{1,0:T(8,128)(2,1)S(1)}, bf16[2056,256]{1,0:T(8,128)(2,1)S(1)}, u32[]{:S(2)}, u32[]{:S(2)}) collective-permute-start(bf16[2056,256]{1,0:T(8,128)(2,1)S(1)} %shard_map.93), channel_id=1, source_target_pairs={{0,1},{1,0},{2,3},{3,2},{4,5},{5,4},{6,7},{7,6},{8,9},{9,8},{10,11... | collective-permute-start | bytes 3158024 | tf_op jit(solution)/shard_map/ppermute | solution.py:169
  16.6 0.0 copy-done.4
  16.6 0.0 copy-done.10
  16.7 0.0 copy-done.11
  16.7 0.7 shard_map.91.wide_ref
  17.4 0.0 copy-start.8
  17.4 4.9 %collective-permute-done.before_ref = bf16[4,64,128]{2,1,0:T(8,128)(2,1)S(1)} collective-permute-done((bf16[4,64,128]{2,1,0:T(8,128)(2,1)}, bf16[4,64,128]{2,1,0:T(8,128)(2,1)S(1)}, u32[]{:S(2)}, u32[]{:S(2)}) %collective-permute-start) | collective-permute-done | bytes 65568 | tf_op jit(solution)/shard_map/ppermute | solution.py:162
  22.3 0.0 copy-done.5
  22.3 0.0 copy-start.2
  22.3 0.0 copy-start.6
  22.3 0.0 copy-start.7
  22.3 0.5 shard_map.92
  22.8 0.0 copy-start
  22.8 16.1 %all_to_all.20.refs_0_ = bf16[16,64,256]{2,1,0:T(8,128)(2,1)S(1)} all-to-all(bf16[16,64,256]{2,1,0:T(8,128)(2,1)S(1)} %bitcast.15), channel_id=1, replica_groups=mesh['space'=32,'tensor'=16] {'tensor'}, dimensions={0} | all-to-all | bytes 1048576 | tf_op jit(solution)/shard_map/all_to_all | solution.py:176
  38.9 0.0 collective-permute-done.2.refs_6_
  38.9 0.0 copy-done.8
  38.9 0.0 copy-done.2
  38.9 0.0 copy-done.6
  39.0 0.0 copy-done.7
  39.0 0.0 copy-done
  39.0 1.4 %shard_map.94 = bf16[8,2,64,256]{3,2,1,0:T(8,128)(2,1)S(1)} custom-call(bf16[16,64,256]{2,1,0:T(8,128)(2,1)S(1)} %all_to_all.20.refs_0_, f32[2,1024]{1,0:T(2,128)S(1)} %copy-done.6, f32[2,1024]{1,0:T(2,128)S(1)} %copy-done.7, bf16[2,1024,256]{2,1,0:T(8,128)(2,1)S(1)} %copy-done, bf16[2,256,1024]{2,1,0:T(8,128)(2,1)S(1)} %copy-done.2, ...), custom_call_target="tpu_custom_call" | custom-call | tf_op jit(solution)/shard_map/pallas_call | solution.py:19
  40.4 13.5 %all_to_all.21 = bf16[16,64,256]{2,1,0:T(8,128)(2,1)S(1)} all-to-all(bf16[16,64,256]{2,1,0:T(8,128)(2,1)S(1)} %bitcast.11), channel_id=1, replica_groups=mesh['space'=32,'tensor'=16] {'tensor'}, dimensions={0} | all-to-all | bytes 1048576 | tf_op jit(solution)/shard_map/all_to_all | solution.py:182
  53.9 0.1 shard_map.95.rows_ref.stream_ref
  54.0 3.9 %collective-permute-start.4 = (bf16[4,64,128]{2,1,0:T(8,128)(2,1)S(1)}, bf16[4,64,128]{2,1,0:T(8,128)(2,1)S(1)}, u32[]{:S(2)}, u32[]{:S(2)}) collective-permute-start(bf16[4,64,128]{2,1,0:T(8,128)(2,1)S(1)} %shard_map.95.rows_ref.stream_ref), channel_id=1, source_target_pairs={{16,0},{32,16},{48,32},{64,48},{80,64},{96,80},{112,96},{128,112},... | collective-permute-start | bytes 196616 | tf_op jit(solution)/shard_map/ppermute | solution.py:161
  57.9 2.8 %collective-permute-start.3 = (bf16[4,64,128]{2,1,0:T(8,128)(2,1)S(1)}, bf16[4,64,128]{2,1,0:T(8,128)(2,1)S(1)}, u32[]{:S(2)}, u32[]{:S(2)}) collective-permute-start(bf16[4,64,128]{2,1,0:T(8,128)(2,1)S(1)} %shard_map.95.rows_ref.stream_ref), channel_id=1, source_target_pairs={{0,16},{16,32},{32,48},{48,64},{64,80},{80,96},{96,112},{112,128},... | collective-permute-start | bytes 196616 | tf_op jit(solution)/shard_map/ppermute | solution.py:162
  60.7 1.0 %collective-permute-done.4.after_ref = bf16[4,64,128]{2,1,0:T(8,128)(2,1)S(1)} collective-permute-done((bf16[4,64,128]{2,1,0:T(8,128)(2,1)S(1)}, bf16[4,64,128]{2,1,0:T(8,128)(2,1)S(1)}, u32[]{:S(2)}, u32[]{:S(2)}) %collective-permute-start.4) | collective-permute-done | bytes 65568 | tf_op jit(solution)/shard_map/ppermute | solution.py:161
  61.8 1.4 %shard_map.98 = bf16[2056,256]{1,0:T(8,128)(2,1)S(1)} custom-call(bf16[2,1024,256]{2,1,0:T(8,128)(2,1)} %refs_3_.3, bf16[2,256,1024]{2,1,0:T(8,128)(2,1)} %refs_4_.3, f32[2,256]{1,0:T(2,128)} %refs_5_.3), custom_call_target="tpu_custom_call" | custom-call | tf_op jit(solution)/shard_map/pallas_call | solution.py:61
  63.1 1.9 %collective-permute-start.5 = (bf16[2056,256]{1,0:T(8,128)(2,1)S(1)}, bf16[2056,256]{1,0:T(8,128)(2,1)S(1)}, u32[]{:S(2)}, u32[]{:S(2)}) collective-permute-start(bf16[2056,256]{1,0:T(8,128)(2,1)S(1)} %shard_map.98), channel_id=1, source_target_pairs={{0,1},{1,0},{2,3},{3,2},{4,5},{5,4},{6,7},{7,6},{8,9},{9,8},{10,11... | collective-permute-start | bytes 3158024 | tf_op jit(solution)/shard_map/ppermute | solution.py:169
  65.1 0.7 shard_map.96.wide_ref
  65.8 0.0 copy-start.9
  65.8 2.7 %collective-permute-done.3.before_ref = bf16[4,64,128]{2,1,0:T(8,128)(2,1)S(1)} collective-permute-done((bf16[4,64,128]{2,1,0:T(8,128)(2,1)S(1)}, bf16[4,64,128]{2,1,0:T(8,128)(2,1)S(1)}, u32[]{:S(2)}, u32[]{:S(2)}) %collective-permute-start.3) | collective-permute-done | bytes 65568 | tf_op jit(solution)/shard_map/ppermute | solution.py:162
  68.4 0.0 copy-start.3
  68.4 0.5 shard_map.97
  69.0 0.0 copy-start.1
  69.0 13.6 %all_to_all.22.refs_0_ = bf16[16,64,256]{2,1,0:T(8,128)(2,1)S(1)} all-to-all(bf16[16,64,256]{2,1,0:T(8,128)(2,1)S(1)} %bitcast.16), channel_id=1, replica_groups=mesh['space'=32,'tensor'=16] {'tensor'}, dimensions={0} | all-to-all | bytes 1048576 | tf_op jit(solution)/shard_map/all_to_all | solution.py:176
  82.6 0.0 collective-permute-done.5.refs_6_
  82.6 0.0 copy-done.9
  82.6 0.0 copy-done.3
  82.6 0.0 copy-done.1
  82.6 1.4 %shard_map.99 = bf16[8,2,64,256]{3,2,1,0:T(8,128)(2,1)S(1)} custom-call(bf16[16,64,256]{2,1,0:T(8,128)(2,1)S(1)} %all_to_all.22.refs_0_, f32[2,1024]{1,0:T(2,128)S(1)} %copy-done.6, f32[2,1024]{1,0:T(2,128)S(1)} %copy-done.7, bf16[2,1024,256]{2,1,0:T(8,128)(2,1)S(1)} %copy-done.1, bf16[2,256,1024]{2,1,0:T(8,128)(2,1)S(1)} %copy-done.3, ...), custom_call_target="tpu_custom_call" | custom-call | tf_op jit(solution)/shard_map/pallas_call | solution.py:19
  84.0 13.5 %all_to_all.23 = bf16[16,64,256]{2,1,0:T(8,128)(2,1)S(1)} all-to-all(bf16[16,64,256]{2,1,0:T(8,128)(2,1)S(1)} %bitcast.12), channel_id=1, replica_groups=mesh['space'=32,'tensor'=16] {'tensor'}, dimensions={0} | all-to-all | bytes 1048576 | tf_op jit(solution)/shard_map/all_to_all | solution.py:182
  97.5 0.7 shard_map.100
Async XLA Ops:
  0.0 16.6 %copy-start.4 = (bf16[2,7,7,64]{3,0,2,1:T(2,128)(2,1)S(1)}, bf16[2,7,7,64]{3,0,2,1:T(2,128)(2,1)}, u32[]{:S(2)}) copy-start(bf16[2,7,7,64]{3,0,2,1:T(2,128)(2,1)} %param.10) | copy-start | bytes 37636
  0.0 16.6 %copy-start.10 = (f32[2,64]{1,0:T(2,128)S(1)}, f32[2,64]{1,0:T(2,128)}, u32[]{:S(2)}) copy-start(f32[2,64]{1,0:T(2,128)} %refs_1_.7) | copy-start | bytes 1540
  0.0 16.7 %copy-start.11 = (f32[2,64]{1,0:T(2,128)S(1)}, f32[2,64]{1,0:T(2,128)}, u32[]{:S(2)}) copy-start(f32[2,64]{1,0:T(2,128)} %refs_2_.7) | copy-start | bytes 1540
  0.0 13.2 %collective-permute-start.1 = (bf16[4,64,128]{2,1,0:T(8,128)(2,1)}, bf16[4,64,128]{2,1,0:T(8,128)(2,1)S(1)}, u32[]{:S(2)}, u32[]{:S(2)}) collective-permute-start(bf16[4,64,128]{2,1,0:T(8,128)(2,1)} %bitcast.19), channel_id=1, source_target_pairs={{16,0},{32,16},{48,32},{64,48},{80,64},{96,80},{112,96},{128,112},... | collective-permute-start | bytes 196616 | tf_op jit(solution)/shard_map/ppermute | solution.py:161
  11.0 11.3 %collective-permute-start = (bf16[4,64,128]{2,1,0:T(8,128)(2,1)}, bf16[4,64,128]{2,1,0:T(8,128)(2,1)S(1)}, u32[]{:S(2)}, u32[]{:S(2)}) collective-permute-start(bf16[4,64,128]{2,1,0:T(8,128)(2,1)} %bitcast.20), channel_id=1, source_target_pairs={{0,16},{16,32},{32,48},{48,64},{64,80},{80,96},{96,112},{112,128},... | collective-permute-start | bytes 196616 | tf_op jit(solution)/shard_map/ppermute | solution.py:162
  14.6 7.7 %copy-start.5 = (bf16[4,128,64]{1,2,0:T(8,128)(2,1)S(1)}, bf16[4,128,64]{1,2,0:T(8,128)(2,1)}, u32[]{:S(2)}) copy-start(bf16[4,128,64]{1,2,0:T(8,128)(2,1)} %param.9) | copy-start | bytes 196612
  14.6 24.4 %collective-permute-start.2 = (bf16[2056,256]{1,0:T(8,128)(2,1)S(1)}, bf16[2056,256]{1,0:T(8,128)(2,1)S(1)}, u32[]{:S(2)}, u32[]{:S(2)}) collective-permute-start(bf16[2056,256]{1,0:T(8,128)(2,1)S(1)} %shard_map.93), channel_id=1, source_target_pairs={{0,1},{1,0},{2,3},{3,2},{4,5},{5,4},{6,7},{7,6},{8,9},{9,8},{10,11... | collective-permute-start | bytes 3158024 | tf_op jit(solution)/shard_map/ppermute | solution.py:169
  17.4 21.6 %copy-start.8 = (f32[2,256]{1,0:T(2,128)S(1)}, f32[2,256]{1,0:T(2,128)}, u32[]{:S(2)}) copy-start(f32[2,256]{1,0:T(2,128)} %refs_5_.3) | copy-start | bytes 6148
  22.3 16.7 %copy-start.2 = (bf16[2,256,1024]{2,1,0:T(8,128)(2,1)S(1)}, bf16[2,256,1024]{2,1,0:T(8,128)(2,1)}, u32[]{:S(2)}) copy-start(bf16[2,256,1024]{2,1,0:T(8,128)(2,1)} %refs_4_.3) | copy-start | bytes 3145732
  22.3 16.7 %copy-start.6 = (f32[2,1024]{1,0:T(2,128)S(1)}, f32[2,1024]{1,0:T(2,128)}, u32[]{:S(2)}) copy-start(f32[2,1024]{1,0:T(2,128)} %refs_1_.9) | copy-start | bytes 24580
  22.3 16.7 %copy-start.7 = (f32[2,1024]{1,0:T(2,128)S(1)}, f32[2,1024]{1,0:T(2,128)}, u32[]{:S(2)}) copy-start(f32[2,1024]{1,0:T(2,128)} %refs_2_.9) | copy-start | bytes 24580
  22.8 16.2 %copy-start = (bf16[2,1024,256]{2,1,0:T(8,128)(2,1)S(1)}, bf16[2,1024,256]{2,1,0:T(8,128)(2,1)}, u32[]{:S(2)}) copy-start(bf16[2,1024,256]{2,1,0:T(8,128)(2,1)} %refs_3_.3) | copy-start | bytes 3145732
  54.0 7.8 %collective-permute-start.4 = (bf16[4,64,128]{2,1,0:T(8,128)(2,1)S(1)}, bf16[4,64,128]{2,1,0:T(8,128)(2,1)S(1)}, u32[]{:S(2)}, u32[]{:S(2)}) collective-permute-start(bf16[4,64,128]{2,1,0:T(8,128)(2,1)S(1)} %shard_map.95.rows_ref.stream_ref), channel_id=1, source_target_pairs={{16,0},{32,16},{48,32},{64,48},{80,64},{96,80},{112,96},{128,112},... | collective-permute-start | bytes 196616 | tf_op jit(solution)/shard_map/ppermute | solution.py:161
  57.9 10.6 %collective-permute-start.3 = (bf16[4,64,128]{2,1,0:T(8,128)(2,1)S(1)}, bf16[4,64,128]{2,1,0:T(8,128)(2,1)S(1)}, u32[]{:S(2)}, u32[]{:S(2)}) collective-permute-start(bf16[4,64,128]{2,1,0:T(8,128)(2,1)S(1)} %shard_map.95.rows_ref.stream_ref), channel_id=1, source_target_pairs={{0,16},{16,32},{32,48},{48,64},{64,80},{80,96},{96,112},{112,128},... | collective-permute-start | bytes 196616 | tf_op jit(solution)/shard_map/ppermute | solution.py:162
  63.1 19.5 %collective-permute-start.5 = (bf16[2056,256]{1,0:T(8,128)(2,1)S(1)}, bf16[2056,256]{1,0:T(8,128)(2,1)S(1)}, u32[]{:S(2)}, u32[]{:S(2)}) collective-permute-start(bf16[2056,256]{1,0:T(8,128)(2,1)S(1)} %shard_map.98), channel_id=1, source_target_pairs={{0,1},{1,0},{2,3},{3,2},{4,5},{5,4},{6,7},{7,6},{8,9},{9,8},{10,11... | collective-permute-start | bytes 3158024 | tf_op jit(solution)/shard_map/ppermute | solution.py:169
  65.8 16.9 %copy-start.9 = (f32[2,256]{1,0:T(2,128)S(1)}, f32[2,256]{1,0:T(2,128)}, u32[]{:S(2)}) copy-start(f32[2,256]{1,0:T(2,128)} %refs_5_.3) | copy-start | bytes 6148
  68.4 14.2 %copy-start.3 = (bf16[2,256,1024]{2,1,0:T(8,128)(2,1)S(1)}, bf16[2,256,1024]{2,1,0:T(8,128)(2,1)}, u32[]{:S(2)}) copy-start(bf16[2,256,1024]{2,1,0:T(8,128)(2,1)} %refs_4_.3) | copy-start | bytes 3145732
  69.0 13.6 %copy-start.1 = (bf16[2,1024,256]{2,1,0:T(8,128)(2,1)S(1)}, bf16[2,1024,256]{2,1,0:T(8,128)(2,1)}, u32[]{:S(2)}) copy-start(bf16[2,1024,256]{2,1,0:T(8,128)(2,1)} %refs_3_.3) | copy-start | bytes 3145732

commit v4 on v3

v4 whole, which is shorter than its diff:
```python
import jax
import jax.numpy as jnp
from jax import lax
from jax.experimental import pallas as pl
from jax.experimental.pallas import tpu as pltpu
from jax.sharding import PartitionSpec as P

D = 1024
TAPS = 7
HALF = TAPS // 2
BLOCKS = 2
CORES = 2

VMEM = pl.BlockSpec(memory_space=pltpu.VMEM)


def call(body, outs, *args, cost=None):
    single = not isinstance(outs, (list, tuple))
    return pl.pallas_call(
        body,
        out_shape=outs,
        in_specs=[VMEM] * len(args),
        out_specs=VMEM if single else [VMEM] * len(outs),
        cost_estimate=cost,
        compiler_params=pltpu.CompilerParams(vmem_limit_bytes=16 << 20),
    )(*args)


def spread(block, taps_ref, scale_ref, shift_ref, wide_ref, affine_ref):
    rows = [taps_ref[:, block, :].astype(jnp.float32), scale_ref[block : block + 1, :], shift_ref[block : block + 1, :]]
    cols = jnp.transpose(jnp.concatenate(rows, axis=0))
    for at in range(cols.shape[1]):
        col = jnp.broadcast_to(cols[:, at : at + 1], wide_ref.shape[1:])
        if at < wide_ref.shape[0]:
            wide_ref[at] = col
        else:
            affine_ref[at - wide_ref.shape[0]] = col


def enter_kernel(band_ref, taps_in, scale_in, shift_in, wide_ref, affine_ref, rows_ref, taps_ref, scale_ref, shift_ref, sems):
    moves = ((taps_in, taps_ref), (scale_in, scale_ref), (shift_in, shift_ref), (band_ref, rows_ref))
    copies = [pltpu.make_async_copy(src, dst, sems.at[i]) for i, (src, dst) in enumerate(moves)]
    for copy in copies:
        copy.start()
    for copy in copies[:3]:
        copy.wait()
    spread(0, taps_ref, scale_ref, shift_ref, wide_ref, affine_ref)
    copies[3].wait()


def spread_shapes(share, width):
    return tuple(jax.ShapeDtypeStruct((count, share, width), jnp.float32) for count in (TAPS * TAPS, 2))


def entered(band, taps, scale, shift):
    inputs = (band, taps, scale, shift)
    return pl.pallas_call(
        enter_kernel,
        out_shape=[
            *spread_shapes(*band.shape[1:]),
            *[jax.ShapeDtypeStruct(array.shape, array.dtype) for array in inputs],
        ],
        in_specs=[pl.BlockSpec(memory_space=pltpu.HBM)] * 4,
        out_specs=[VMEM] * 6,
        scratch_shapes=[pltpu.SemaphoreType.DMA((4,))],
        compiler_params=pltpu.CompilerParams(vmem_limit_bytes=16 << 20),
    )(*[pltpu.with_memory_space_constraint(array, pltpu.HBM) for array in inputs])


def pack_kernel(expand_ref, reduce_ref, bias_ref, pack_ref, held_ref, sems):
    units = pack_ref.shape[2]
    moves = []
    for block in range(BLOCKS):
        moves.append((expand_ref.at[block], pack_ref.at[block, pl.ds(0, D)]))
        for part in range(D // units):
            columns = pl.ds(units * part, units)
            moves.append((reduce_ref.at[block, :, columns], pack_ref.at[block, pl.ds(D + units * part, units)]))
    moves.append((bias_ref, held_ref))
    copies = [pltpu.make_async_copy(src, dst, sems.at[i]) for i, (src, dst) in enumerate(moves)]
    for copy in reversed(copies):
        copy.start()
    copies.pop().wait()
    for block in range(BLOCKS):
        rest = held_ref[block : block + 1, :]
        pieces = []
        for _ in range(3):
            pieces.append(rest.astype(jnp.bfloat16))
            rest = rest - pieces[-1].astype(jnp.float32)
        pieces = [piece.astype(jnp.float32) for piece in pieces] + [jnp.zeros((5, units), jnp.float32)]
        pack_ref[block, 2 * D :, :] = jnp.concatenate(pieces, axis=0).astype(jnp.bfloat16)
    for copy in copies:
        copy.wait()


def packed(w_expand, w_reduce, hidden_bias):
    units = w_expand.shape[2]
    raw = pl.BlockSpec(memory_space=pltpu.HBM)
    return pl.pallas_call(
        pack_kernel,
        out_shape=pltpu.VMEM((BLOCKS, 2 * D + 8, units), jnp.bfloat16),
        in_specs=[raw, raw, raw],
        out_specs=VMEM,
        scratch_shapes=[
            pltpu.VMEM(hidden_bias.shape, jnp.float32),
            pltpu.SemaphoreType.DMA((1 + BLOCKS * (1 + D // units),)),
        ],
        compiler_params=pltpu.CompilerParams(vmem_limit_bytes=16 << 20),
    )(*[pltpu.with_memory_space_constraint(array, pltpu.HBM) for array in (w_expand, w_reduce, hidden_bias)])


def conv_kernel(before_ref, rows_ref, after_ref, wide_ref, out_ref):
    height, share, width = rows_ref.shape
    copies = out_ref.shape[0]
    size = 16
    column = lax.broadcasted_iota(jnp.int32, (size, width), 1)
    inside = {
        shift: ((column + shift >= 0) & (column + shift < width)).astype(jnp.float32)
        for shift in range(-HALF, HALF + 1)
    }
    for group in range(share // size):
        chans = slice(size * group, size * (group + 1))
        rows = [before_ref[r, chans, :] for r in range(height - HALF, height)]
        rows += [rows_ref[r, chans, :] for r in range(height)]
        rows += [after_ref[r, chans, :] for r in range(HALF)]
        rows = [row.astype(jnp.float32) for row in rows]
        totals = [None] * height
        for j in range(TAPS):
            taps = [wide_ref[i * TAPS + j, chans, :] for i in range(TAPS)]
            shift = j - HALF
            for r in range(height):
                acc = rows[r] * taps[0]
                for i in range(1, TAPS):
                    acc = acc + rows[r + i] * taps[i]
                if shift:
                    acc = pltpu.roll(acc, (-shift) % width, 1) * inside[shift]
                totals[r] = acc if totals[r] is None else totals[r] + acc
        for r in range(height):
            half, at = divmod(r, height // CORES)
            value = totals[r].astype(jnp.bfloat16)
            for copy in range(copies):
                out_ref[copy, half, chans, width * at : width * (at + 1)] = value


def hidden_of(normed, weights, unit_bias):
    preact = jnp.dot(normed, weights, preferred_element_type=jnp.float32) + unit_bias
    return (0.5 * preact * (1.0 + lax.erf(preact * (0.5**0.5)))).astype(jnp.bfloat16)


def bias_of(rows):
    pieces = rows.astype(jnp.float32)
    return pieces[0:1] + pieces[1:2] + pieces[2:3]


def own_kernel(block, x_ref, gain_ref, bias_ref, pack_ref, normed_ref, own_ref):
    x = x_ref[...].reshape(D, x_ref.shape[-1])
    x = jnp.transpose(x).astype(jnp.float32)
    mean = jnp.mean(x, axis=-1, keepdims=True)
    centered = x - mean
    var = jnp.mean(centered * centered, axis=-1, keepdims=True)
    gain = gain_ref[block : block + 1, :]
    bias = bias_ref[block : block + 1, :]
    normed = (centered * lax.rsqrt(var + 1e-06) * gain + bias).astype(jnp.bfloat16)
    normed_ref[...] = normed
    own_ref[...] = hidden_of(normed, pack_ref[block, :D, :], bias_of(pack_ref[block, 2 * D :, :]))


def rest_kernel(block, normed_ref, own_ref, own_pack_ref, pack_ref, out_ref, held_ref, total_ref, sems):
    bounds = ((0, D), (2 * D, pack_ref.shape[1] - 2 * D), (D, D))
    copies = []
    for i, (start, size) in enumerate(bounds):
        rows = pl.ds(start, size)
        copies.append(pltpu.make_async_copy(pack_ref.at[block, rows], held_ref.at[rows], sems.at[i]))
        copies[-1].start()
    own = own_ref[...]
    units = own.shape[1]
    chips, cores, share, half = out_ref.shape
    for part in range(D // units):
        rows = slice(D + units * part, D + units * (part + 1))
        total_ref[part] = jnp.dot(own, own_pack_ref[block, rows, :], preferred_element_type=jnp.float32)
    copies[0].wait()
    copies[1].wait()
    other = hidden_of(normed_ref[...], held_ref[:D, :], bias_of(held_ref[2 * D :, :]))
    copies[2].wait()
    for part in range(D // units):
        rows = slice(D + units * part, D + units * (part + 1))
        total = total_ref[part] + jnp.dot(other, held_ref[rows, :], preferred_element_type=jnp.float32)
        total = jnp.transpose(total.astype(jnp.bfloat16))
        for at in range(units // share):
            chip, core = divmod(part * (units // share) + at, cores)
            out_ref[chip, core] = total[share * at : share * (at + 1), :]


def rest(block, out, normed, own, own_pack, pack):
    units = own.shape[1]
    return pl.pallas_call(
        lambda *refs: rest_kernel(block, *refs),
        out_shape=out,
        in_specs=[VMEM, VMEM, VMEM, pl.BlockSpec(memory_space=pltpu.HBM)],
        out_specs=VMEM,
        scratch_shapes=[
            pltpu.VMEM(pack.shape[1:], jnp.bfloat16),
            pltpu.VMEM((D // units, own.shape[0], units), jnp.float32),
            pltpu.SemaphoreType.DMA((3,)),
        ],
        compiler_params=pltpu.CompilerParams(vmem_limit_bytes=16 << 20),
    )(normed, own, own_pack, pltpu.with_memory_space_constraint(pack, pltpu.HBM))


def mix_kernel(parts_ref, stream_ref, affine_ref, out_ref):
    height, share, width = stream_ref.shape
    scale, shift = affine_ref[0], affine_ref[1]
    for r in range(height):
        half, at = divmod(r, height // CORES)
        lanes = slice(width * at, width * (at + 1))
        mixed = parts_ref[0, half, :, lanes].astype(jnp.float32)
        for copy in range(1, parts_ref.shape[0]):
            mixed = mixed + parts_ref[copy, half, :, lanes].astype(jnp.float32)
        updated = stream_ref[r].astype(jnp.float32) + scale * (mixed + shift)
        out_ref[r] = updated.astype(jnp.bfloat16)


def per_device(features, depth_kernel, norm_gain, norm_bias, w_expand, b_expand, w_reduce, b_reduce, layer_scale):
    height, width, share = features.shape
    bands, members = lax.axis_size("space"), lax.axis_size("tensor")
    copies = members // CORES
    half = height // CORES * width
    units = w_expand.shape[2]
    down = [(i, i + 1) for i in range(bands - 1)]
    up = [(j, i) for i, j in down]
    sibling = [(i, i ^ 1) for i in range(members)]

    stream = jnp.transpose(features, (0, 2, 1))
    taps = jnp.transpose(depth_kernel, (1, 2, 0, 3)).reshape(TAPS * TAPS, BLOCKS, share)

    for block in range(BLOCKS):
        after = lax.ppermute(stream, "space", up)
        before = lax.ppermute(stream, "space", down)
        if block == 0:
            wide, affine, stream, taps, layer_scale, b_reduce = entered(stream, taps, layer_scale, b_reduce)
        else:
            wide, affine = next_wide, next_affine
        filtered = call(
            conv_kernel,
            jax.ShapeDtypeStruct((copies, CORES, share, half), jnp.bfloat16),
            before, stream, after, wide,
        )
        if block == 0:
            filtered, own_bias, next_scale = lax.optimization_barrier((filtered, b_expand, layer_scale))
            own_pack = packed(w_expand, w_reduce, own_bias)
            pack = lax.ppermute(own_pack, "tensor", sibling)
            next_wide, next_affine = call(
                lambda *refs: spread(1, *refs), spread_shapes(share, width), taps, next_scale, b_reduce
            )
        filtered = lax.all_to_all(filtered.reshape(members, share, half), "tensor", 0, 0, tiled=True)
        if block == 0:
            filtered, next_wide, next_affine = lax.optimization_barrier((filtered, next_wide, next_affine))
        normed, own = call(
            lambda *refs: own_kernel(block, *refs),
            (jax.ShapeDtypeStruct((half, D), jnp.bfloat16), jax.ShapeDtypeStruct((half, units), jnp.bfloat16)),
            filtered, norm_gain, norm_bias, own_pack,
            cost=pl.CostEstimate(flops=10**11, transcendentals=0, bytes_accessed=10**6),
        )
        partial = rest(
            block, jax.ShapeDtypeStruct((copies, CORES, share, half), jnp.bfloat16), normed, own, own_pack, pack
        )
        partial = lax.all_to_all(partial.reshape(members, share, half), "tensor", 0, 0, tiled=True)
        stream = call(
            mix_kernel,
            jax.ShapeDtypeStruct((height, share, width), jnp.bfloat16),
            partial.reshape(copies, CORES, share, half), stream, affine,
        )
    return jnp.transpose(stream, (0, 2, 1))


def solution(mesh):
    return jax.shard_map(
        per_device,
        mesh=mesh,
        in_specs=(
            P("space", None, "tensor"),
            P(None, None, None, "tensor"),
            P(),
            P(),
            P(None, None, "tensor"),
            P(None, "tensor"),
            P(None, "tensor", None),
            P(None, "tensor"),
            P(None, "tensor"),
        ),
        out_specs=P("space", None, "tensor"),
        check_vma=False,
    )
```

time: 98.8 us -> 101 us (1.022)
  blocking collectives: 56.7 us -> 40.6 us
  waiting for transfers between devices: 8.87 us -> 18.8 us
  Pallas kernels: 8.77 us -> 12.3 us
  starting transfers between devices: 23.6 us -> 27.1 us
  local copies, waits for them, and re-layouts: 0.06 us -> 1.18 us
    all_to_all x2 -> x1, blocking collectives: 29.7 us -> 13.5 us  [per_device(): lax.all_to_all(filtered.reshape(members, share, half), 'tensor', 0, 0, ti...]
    all_to_all x0 -> x1, starting transfers between devices: none -> 5.31 us  [per_device(): lax.all_to_all(filtered.reshape(members, share, half), 'tensor', 0, 0, ti...]
    ppermute x2, waiting for transfers between devices: 7.55 us -> 12.8 us  [per_device(): before = lax.ppermute(stream, 'space', down)]
    all_to_all x0 -> x1, waiting for transfers between devices: none -> 4.88 us  [per_device(): lax.all_to_all(filtered.reshape(members, share, half), 'tensor', 0, 0, ti...]
    pallas_call x2 -> x4, Pallas kernels: 2.76 us -> 7.43 us  [the longest x2 4.18 us: rest(): pl.pallas_call(lambda *refs: rest_kernel(block, *refs), out_shape=out, in...]
    ppermute x2, starting transfers between devices: 14.9 us -> 12.7 us  [per_device(): after = lax.ppermute(stream, 'space', up)]
    ppermute x2, starting transfers between devices: 4.76 us -> 6.74 us  [per_device(): before = lax.ppermute(stream, 'space', down)]
    ppermute x2 -> x1, starting transfers between devices: 3.97 us -> 2.32 us  [per_device(): pack = lax.ppermute(own_pack, 'tensor', sibling)]
where the time goes in v4:
time: 101 us; the launch traced here: 100 us
  blocking collectives  40.6 us (40%)
  starting transfers between devices  27.1 us (27%)
  waiting for transfers between devices  18.8 us (19%)
  Pallas kernels  12.3 us (12%)
  local copies, waits for them, and re-layouts  1.18 us (1%)
    all_to_all x2, blocking collectives, per_device(): lax.all_to_all(partial.reshape(members, share, half), 'tensor', 0, 0, til...  27.1 us
    all_to_all x1, blocking collectives, per_device(): lax.all_to_all(filtered.reshape(members, share, half), 'tensor', 0, 0, ti...  13.5 us
    ppermute x2, waiting for transfers between devices, per_device(): before = lax.ppermute(stream, 'space', down)  12.8 us
    ppermute x2, starting transfers between devices, per_device(): after = lax.ppermute(stream, 'space', up)  12.7 us
    ppermute x2, starting transfers between devices, per_device(): before = lax.ppermute(stream, 'space', down)  6.74 us
    all_to_all x1, starting transfers between devices, per_device(): lax.all_to_all(filtered.reshape(members, share, half), 'tensor', 0, 0, ti...  5.31 us
    all_to_all x1, waiting for transfers between devices, per_device(): lax.all_to_all(filtered.reshape(members, share, half), 'tensor', 0, 0, ti...  4.88 us
    pallas_call x7, Pallas kernels, call(): pl.pallas_call(body, out_shape=outs, in_specs=[VMEM] * len(args), out_spe...  4.87 us
  transfers between devices with their start and end apart: 6, of which 4 were waited for; matrix products, arithmetic and copies ran while one was open for 0% of the time, Pallas kernels for 5%

profile of v4, /device:TPU:32, one launch (start us, length us, event | category | flops | bytes accessed | tf_op | source)
XLA Modules:
  0.0 100.1 jit_solution(1272859097255367452)
XLA Ops:
  0.0 10.8 %collective-permute-start.1 = (bf16[4,64,128]{2,1,0:T(8,128)(2,1)}, bf16[4,64,128]{2,1,0:T(8,128)(2,1)S(1)}, u32[]{:S(2)}, u32[]{:S(2)}) collective-permute-start(bf16[4,64,128]{2,1,0:T(8,128)(2,1)} %bitcast.16), channel_id=1, source_target_pairs={{16,0},{32,16},{48,32},{64,48},{80,64},{96,80},{112,96},{128,112},... | collective-permute-start | bytes 196616 | tf_op jit(solution)/shard_map/ppermute | solution.py:236
  10.8 1.9 %collective-permute-start = (bf16[4,64,128]{2,1,0:T(8,128)(2,1)}, bf16[4,64,128]{2,1,0:T(8,128)(2,1)S(1)}, u32[]{:S(2)}, u32[]{:S(2)}) collective-permute-start(bf16[4,64,128]{2,1,0:T(8,128)(2,1)} %bitcast.17), channel_id=1, source_target_pairs={{0,16},{16,32},{32,48},{48,64},{64,80},{80,96},{96,112},{112,128},... | collective-permute-start | bytes 196616 | tf_op jit(solution)/shard_map/ppermute | solution.py:237
  12.7 1.5 %shard_map.91 = (f32[49,64,128]{2,1,0:T(8,128)S(1)}, f32[2,64,128]{2,1,0:T(8,128)S(1)}, bf16[4,64,128]{2,1,0:T(8,128)(2,1)S(1)}, bf16[49,2,64]{2,1,0:T(2,128)(2,...) custom-call(bf16[4,64,128]{2,1,0:T(8,128)(2,1)} %bitcast.18, bf16[49,2,64]{2,1,0:T(2,128)(2,1)} %bitcast.19, ...), custom_call_target="tpu_custom_call" | custom-call | tf_op jit(solution)/shard_map/pallas_call | solution.py:57
  14.2 0.0 collective-permute-done.1.after_ref
  14.2 7.9 %collective-permute-done.before_ref = bf16[4,64,128]{2,1,0:T(8,128)(2,1)S(1)} collective-permute-done((bf16[4,64,128]{2,1,0:T(8,128)(2,1)}, bf16[4,64,128]{2,1,0:T(8,128)(2,1)S(1)}, u32[]{:S(2)}, u32[]{:S(2)}) %collective-permute-start) | collective-permute-done | bytes 65568 | tf_op jit(solution)/shard_map/ppermute | solution.py:237
  22.1 1.3 %shard_map.92 = bf16[8,2,64,256]{3,2,1,0:T(8,128)(2,1)} custom-call(bf16[4,64,128]{2,1,0:T(8,128)(2,1)S(1)} %collective-permute-done.before_ref, bf16[4,64,128]{2,1,0:T(8,128)(2,1)S(1)} %get-tuple-element.23.rows_ref.stream_ref, bf16[4,64,128]{2,1,0:T(8,128)(2,1)S(1)} %collective-permute-done.1.after_ref, f32[49,64,128]{2,1,0:T(8,128)S(1)} %get-tuple-element.24.wide_ref), custom_call_target="tpu_custom_call" | custom-call | tf_op jit(solution)/shard_map/pallas_call | solution.py:19
  23.4 5.3 %all-to-all-start = ((bf16[16,64,256]{2,1,0:T(8,128)(2,1)}), bf16[16,64,256]{2,1,0:T(8,128)(2,1)S(1)}, u32[]{:S(2)}, u32[]{:S(2)}) async-start(bf16[16,64,256]{2,1,0:T(8,128)(2,1)} %bitcast.3), calls=%async_computation | async-start | bytes 1048576 | tf_op jit(solution)/shard_map/all_to_all | solution.py:254
  28.7 0.0 copy-start.2
  28.8 0.0 copy-start.3
  28.8 1.8 %shard_map.94.refs_3_.refs_2_ = bf16[2,2056,256]{2,1,0:T(8,128)(2,1)S(1)} custom-call(bf16[2,1024,256]{2,1,0:T(8,128)(2,1)} %expand_ref.1, bf16[2,256,1024]{2,1,0:T(8,128)(2,1)} %reduce_ref.1, f32[2,256]{1,0:T(2,128)} %bias_ref), custom_call_target="tpu_custom_call" | custom-call | tf_op jit(solution)/shard_map/pallas_call | solution.py:98
  30.5 2.3 %collective-permute-start.2 = (bf16[2,2056,256]{2,1,0:T(8,128)(2,1)S(1)}, bf16[2,2056,256]{2,1,0:T(8,128)(2,1)}, u32[]{:S(2)}, u32[]{:S(2)}) collective-permute-start(bf16[2,2056,256]{2,1,0:T(8,128)(2,1)S(1)} %shard_map.94.refs_3_.refs_2_), channel_id=1, source_target_pairs={{0,1},{1,0},{2,3},{3,2},{4,5},{5,4},{6,7},{7,6},{8,9},{9,8},{10,11... | collective-permute-start | bytes 6316040 | tf_op jit(solution)/shard_map/ppermute | solution.py:250
  32.9 0.7 shard_map.93
  33.6 0.0 copy-start
  33.6 1.2 %copy-done = f32[49,64,128]{2,1,0:T(8,128)} copy-done((f32[49,64,128]{2,1,0:T(8,128)}, f32[49,64,128]{2,1,0:T(8,128)S(1)}, u32[]{:S(2)}) %copy-start) | copy-done | bytes 1605656
  34.7 4.9 %all-to-all-done.refs_0_ = bf16[16,64,256]{2,1,0:T(8,128)(2,1)S(1)} async-done(((bf16[16,64,256]{2,1,0:T(8,128)(2,1)}), bf16[16,64,256]{2,1,0:T(8,128)(2,1)S(1)}, u32[]{:S(2)}, u32[]{:S(2)}) %all-to-all-start) | async-done | bytes 524320 | tf_op jit(solution)/shard_map/all_to_all | solution.py:254
  39.6 0.0 copy-done.2
  39.6 0.0 copy-done.3
  39.6 0.8 shard_map.95
  40.4 0.0 collective-permute-done.2.refs_3_
  40.4 2.1 %shard_map.96 = bf16[8,2,64,256]{3,2,1,0:T(8,128)(2,1)S(1)} custom-call(bf16[256,1024]{1,0:T(8,128)(2,1)S(1)} %get-tuple-element.34.refs_0_, bf16[256,256]{1,0:T(8,128)(2,1)S(1)} %get-tuple-element.35.refs_1_, bf16[2,2056,256]{2,1,0:T(8,128)(2,1)S(1)} %shard_map.94.refs_3_.refs_2_, bf16[2,2056,256]{2,1,0:T(8,128)(2,1)} %collective-permute-done.2.refs_3_), custom_call_target="tpu_custom_call" | custom-call | tf_op jit(solution)/shard_map/pallas_call | solution.py:195
  42.5 0.0 copy-start.1
  42.5 13.6 %all_to_all.20 = bf16[16,64,256]{2,1,0:T(8,128)(2,1)S(1)} all-to-all(bf16[16,64,256]{2,1,0:T(8,128)(2,1)S(1)} %bitcast.15), channel_id=1, replica_groups=mesh['space'=32,'tensor'=16] {'tensor'}, dimensions={0} | all-to-all | bytes 1048576 | tf_op jit(solution)/shard_map/all_to_all | solution.py:266
  56.1 0.1 shard_map.97.rows_ref.stream_ref
  56.2 1.9 %collective-permute-start.4 = (bf16[4,64,128]{2,1,0:T(8,128)(2,1)S(1)}, bf16[4,64,128]{2,1,0:T(8,128)(2,1)S(1)}, u32[]{:S(2)}, u32[]{:S(2)}) collective-permute-start(bf16[4,64,128]{2,1,0:T(8,128)(2,1)S(1)} %shard_map.97.rows_ref.stream_ref), channel_id=1, source_target_pairs={{16,0},{32,16},{48,32},{64,48},{80,64},{96,80},{112,96},{128,112},... | collective-permute-start | bytes 196616 | tf_op jit(solution)/shard_map/ppermute | solution.py:236
  58.2 4.8 %collective-permute-start.3 = (bf16[4,64,128]{2,1,0:T(8,128)(2,1)S(1)}, bf16[4,64,128]{2,1,0:T(8,128)(2,1)S(1)}, u32[]{:S(2)}, u32[]{:S(2)}) collective-permute-start(bf16[4,64,128]{2,1,0:T(8,128)(2,1)S(1)} %shard_map.97.rows_ref.stream_ref), channel_id=1, source_target_pairs={{0,16},{16,32},{32,48},{48,64},{64,80},{80,96},{96,112},{112,128},... | collective-permute-start | bytes 196616 | tf_op jit(solution)/shard_map/ppermute | solution.py:237
  63.0 1.0 %collective-permute-done.4.after_ref = bf16[4,64,128]{2,1,0:T(8,128)(2,1)S(1)} collective-permute-done((bf16[4,64,128]{2,1,0:T(8,128)(2,1)S(1)}, bf16[4,64,128]{2,1,0:T(8,128)(2,1)S(1)}, u32[]{:S(2)}, u32[]{:S(2)}) %collective-permute-start.4) | collective-permute-done | bytes 65568 | tf_op jit(solution)/shard_map/ppermute | solution.py:236
  64.0 5.0 %collective-permute-done.3.before_ref = bf16[4,64,128]{2,1,0:T(8,128)(2,1)S(1)} collective-permute-done((bf16[4,64,128]{2,1,0:T(8,128)(2,1)S(1)}, bf16[4,64,128]{2,1,0:T(8,128)(2,1)S(1)}, u32[]{:S(2)}, u32[]{:S(2)}) %collective-permute-start.3) | collective-permute-done | bytes 65568 | tf_op jit(solution)/shard_map/ppermute | solution.py:237
  69.0 0.0 copy-done.1
  69.0 0.5 shard_map.98
  69.5 13.5 %all_to_all.21.refs_0_ = bf16[16,64,256]{2,1,0:T(8,128)(2,1)S(1)} all-to-all(bf16[16,64,256]{2,1,0:T(8,128)(2,1)S(1)} %bitcast.13), channel_id=1, replica_groups=mesh['space'=32,'tensor'=16] {'tensor'}, dimensions={0} | all-to-all | bytes 1048576 | tf_op jit(solution)/shard_map/all_to_all | solution.py:254
  83.0 0.8 shard_map.99
  83.8 2.1 %shard_map.100 = bf16[8,2,64,256]{3,2,1,0:T(8,128)(2,1)S(1)} custom-call(bf16[256,1024]{1,0:T(8,128)(2,1)S(1)} %get-tuple-element.38.refs_0_, bf16[256,256]{1,0:T(8,128)(2,1)S(1)} %get-tuple-element.39.refs_1_, bf16[2,2056,256]{2,1,0:T(8,128)(2,1)S(1)} %shard_map.94.refs_3_.refs_2_, bf16[2,2056,256]{2,1,0:T(8,128)(2,1)} %collective-permute-done.2.refs_3_), custom_call_target="tpu_custom_call" | custom-call | tf_op jit(solution)/shard_map/pallas_call | solution.py:195
  85.9 13.5 %all_to_all.22 = bf16[16,64,256]{2,1,0:T(8,128)(2,1)S(1)} all-to-all(bf16[16,64,256]{2,1,0:T(8,128)(2,1)S(1)} %bitcast.14), channel_id=1, replica_groups=mesh['space'=32,'tensor'=16] {'tensor'}, dimensions={0} | all-to-all | bytes 1048576 | tf_op jit(solution)/shard_map/all_to_all | solution.py:266
  99.4 0.7 shard_map.101
Async XLA Ops:
  0.0 14.2 %collective-permute-start.1 = (bf16[4,64,128]{2,1,0:T(8,128)(2,1)}, bf16[4,64,128]{2,1,0:T(8,128)(2,1)S(1)}, u32[]{:S(2)}, u32[]{:S(2)}) collective-permute-start(bf16[4,64,128]{2,1,0:T(8,128)(2,1)} %bitcast.16), channel_id=1, source_target_pairs={{16,0},{32,16},{48,32},{64,48},{80,64},{96,80},{112,96},{128,112},... | collective-permute-start | bytes 196616 | tf_op jit(solution)/shard_map/ppermute | solution.py:236
  10.8 11.3 %collective-permute-start = (bf16[4,64,128]{2,1,0:T(8,128)(2,1)}, bf16[4,64,128]{2,1,0:T(8,128)(2,1)S(1)}, u32[]{:S(2)}, u32[]{:S(2)}) collective-permute-start(bf16[4,64,128]{2,1,0:T(8,128)(2,1)} %bitcast.17), channel_id=1, source_target_pairs={{0,16},{16,32},{32,48},{48,64},{64,80},{80,96},{96,112},{112,128},... | collective-permute-start | bytes 196616 | tf_op jit(solution)/shard_map/ppermute | solution.py:237
  23.4 16.2 %all-to-all-start = ((bf16[16,64,256]{2,1,0:T(8,128)(2,1)}), bf16[16,64,256]{2,1,0:T(8,128)(2,1)S(1)}, u32[]{:S(2)}, u32[]{:S(2)}) async-start(bf16[16,64,256]{2,1,0:T(8,128)(2,1)} %bitcast.3), calls=%async_computation | async-start | bytes 1048576 | tf_op jit(solution)/shard_map/all_to_all | solution.py:254
  28.7 10.9 %copy-start.2 = (f32[2,1024]{1,0:T(2,128)S(1)}, f32[2,1024]{1,0:T(2,128)}, u32[]{:S(2)}) copy-start(f32[2,1024]{1,0:T(2,128)} %refs_1_.3) | copy-start | bytes 24580
  28.8 10.9 %copy-start.3 = (f32[2,1024]{1,0:T(2,128)S(1)}, f32[2,1024]{1,0:T(2,128)}, u32[]{:S(2)}) copy-start(f32[2,1024]{1,0:T(2,128)} %refs_2_.3) | copy-start | bytes 24580
  30.5 9.8 %collective-permute-start.2 = (bf16[2,2056,256]{2,1,0:T(8,128)(2,1)S(1)}, bf16[2,2056,256]{2,1,0:T(8,128)(2,1)}, u32[]{:S(2)}, u32[]{:S(2)}) collective-permute-start(bf16[2,2056,256]{2,1,0:T(8,128)(2,1)S(1)} %shard_map.94.refs_3_.refs_2_), channel_id=1, source_target_pairs={{0,1},{1,0},{2,3},{3,2},{4,5},{5,4},{6,7},{7,6},{8,9},{9,8},{10,11... | collective-permute-start | bytes 6316040 | tf_op jit(solution)/shard_map/ppermute | solution.py:250
  33.6 1.2 %copy-start = (f32[49,64,128]{2,1,0:T(8,128)}, f32[49,64,128]{2,1,0:T(8,128)S(1)}, u32[]{:S(2)}) copy-start(f32[49,64,128]{2,1,0:T(8,128)S(1)} %get-tuple-element.37.wide_ref) | copy-start | bytes 4816900
  42.5 26.5 %copy-start.1 = (f32[49,64,128]{2,1,0:T(8,128)S(1)}, f32[49,64,128]{2,1,0:T(8,128)}, u32[]{:S(2)}) copy-start(f32[49,64,128]{2,1,0:T(8,128)} %copy-done) | copy-start | bytes 4816900
  56.2 7.8 %collective-permute-start.4 = (bf16[4,64,128]{2,1,0:T(8,128)(2,1)S(1)}, bf16[4,64,128]{2,1,0:T(8,128)(2,1)S(1)}, u32[]{:S(2)}, u32[]{:S(2)}) collective-permute-start(bf16[4,64,128]{2,1,0:T(8,128)(2,1)S(1)} %shard_map.97.rows_ref.stream_ref), channel_id=1, source_target_pairs={{16,0},{32,16},{48,32},{64,48},{80,64},{96,80},{112,96},{128,112},... | collective-permute-start | bytes 196616 | tf_op jit(solution)/shard_map/ppermute | solution.py:236
  58.2 10.9 %collective-permute-start.3 = (bf16[4,64,128]{2,1,0:T(8,128)(2,1)S(1)}, bf16[4,64,128]{2,1,0:T(8,128)(2,1)S(1)}, u32[]{:S(2)}, u32[]{:S(2)}) collective-permute-start(bf16[4,64,128]{2,1,0:T(8,128)(2,1)S(1)} %shard_map.97.rows_ref.stream_ref), channel_id=1, source_target_pairs={{0,16},{16,32},{32,48},{48,64},{64,80},{80,96},{96,112},{112,128},... | collective-permute-start | bytes 196616 | tf_op jit(solution)/shard_map/ppermute | solution.py:237

commit v5 on v4

--- a/solution.py
+++ b/solution.py
@@ -9,6 +9,7 @@
 TAPS = 7
 HALF = TAPS // 2
 BLOCKS = 2
+CHUNKS = 8
 CORES = 2
 
 VMEM = pl.BlockSpec(memory_space=pltpu.VMEM)
@@ -71,10 +72,11 @@
     units = pack_ref.shape[2]
     moves = []
     for block in range(BLOCKS):
-        moves.append((expand_ref.at[block], pack_ref.at[block, pl.ds(0, D)]))
+        ref = pack_ref.at[block]
+        moves.append((expand_ref.at[block], ref.at[pl.ds(0, D)]))
         for part in range(D // units):
             columns = pl.ds(units * part, units)
-            moves.append((reduce_ref.at[block, :, columns], pack_ref.at[block, pl.ds(D + units * part, units)]))
+            moves.append((reduce_ref.at[block, :, columns], ref.at[pl.ds(D + units * part, units)]))
     moves.append((bias_ref, held_ref))
     copies = [pltpu.make_async_copy(src, dst, sems.at[i]) for i, (src, dst) in enumerate(moves)]
     for copy in reversed(copies):
@@ -97,7 +99,7 @@
     raw = pl.BlockSpec(memory_space=pltpu.HBM)
     return pl.pallas_call(
         pack_kernel,
-        out_shape=pltpu.VMEM((BLOCKS, 2 * D + 8, units), jnp.bfloat16),
+        out_shape=jax.ShapeDtypeStruct((BLOCKS, 2 * D + 8, units), jnp.bfloat16),
         in_specs=[raw, raw, raw],
         out_specs=VMEM,
         scratch_shapes=[
@@ -108,7 +110,9 @@
     )(*[pltpu.with_memory_space_constraint(array, pltpu.HBM) for array in (w_expand, w_reduce, hidden_bias)])
 
 
-def conv_kernel(before_ref, rows_ref, after_ref, wide_ref, out_ref):
+def conv_kernel(before_leads, before_ref, rows_ref, after_ref, wide_ref, out_ref):
+    if not before_leads:
+        before_ref, after_ref = after_ref, before_ref
     height, share, width = rows_ref.shape
     copies = out_ref.shape[0]
     size = 16
@@ -119,7 +123,7 @@
     }
     for group in range(share // size):
         chans = slice(size * group, size * (group + 1))
-        rows = [before_ref[r, chans, :] for r in range(height - HALF, height)]
+        rows = [before_ref[r, chans, :] for r in range(before_ref.shape[0] - HALF, before_ref.shape[0])]
         rows += [rows_ref[r, chans, :] for r in range(height)]
         rows += [after_ref[r, chans, :] for r in range(HALF)]
         rows = [row.astype(jnp.float32) for row in rows]
@@ -151,7 +155,7 @@
     return pieces[0:1] + pieces[1:2] + pieces[2:3]
 
 
-def own_kernel(block, x_ref, gain_ref, bias_ref, pack_ref, normed_ref, own_ref):
+def normalized(block, x_ref, gain_ref, bias_ref):
     x = x_ref[...].reshape(D, x_ref.shape[-1])
     x = jnp.transpose(x).astype(jnp.float32)
     mean = jnp.mean(x, axis=-1, keepdims=True)
@@ -159,54 +163,88 @@
     var = jnp.mean(centered * centered, axis=-1, keepdims=True)
     gain = gain_ref[block : block + 1, :]
     bias = bias_ref[block : block + 1, :]
-    normed = (centered * lax.rsqrt(var + 1e-06) * gain + bias).astype(jnp.bfloat16)
+    return (centered * lax.rsqrt(var + 1e-06) * gain + bias).astype(jnp.bfloat16)
+
+
+def scatter(part, total, out_ref):
+    cores, share = out_ref.shape[1:3]
+    total = jnp.transpose(total.astype(jnp.bfloat16))
+    count = total.shape[0] // share
+    for at in range(count):
+        chip, core = divmod(part * count + at, cores)
+        out_ref[chip, core] = total[share * at : share * (at + 1), :]
+
+
+def rows_of(part, units):
+    return slice(D + units * part, D + units * (part + 1))
+
+
+def own_kernel(
+    block, x_ref, gain_ref, bias_ref, unit_bias_ref, expand_in, reduce_in,
+    normed_ref, total_ref, expand_ref, reduce_ref, sems,
+):
+    parts, half, units = total_ref.shape
+    copies = []
+    for i in range(2 * CHUNKS):
+        src, dst = ((expand_in, expand_ref), (reduce_in, reduce_ref))[i // CHUNKS]
+        size = dst.shape[0] // CHUNKS
+        rows = pl.ds(size * (i % CHUNKS), size)
+        copies.append(pltpu.make_async_copy(src.at[block, rows], dst.at[rows], sems.at[i]))
+        copies[-1].start()
+    normed = normalized(block, x_ref, gain_ref, bias_ref)
     normed_ref[...] = normed
-    own_ref[...] = hidden_of(normed, pack_ref[block, :D, :], bias_of(pack_ref[block, 2 * D :, :]))
-
-
-def rest_kernel(block, normed_ref, own_ref, own_pack_ref, pack_ref, out_ref, held_ref, total_ref, sems):
-    bounds = ((0, D), (2 * D, pack_ref.shape[1] - 2 * D), (D, D))
-    copies = []
-    for i, (start, size) in enumerate(bounds):
-        rows = pl.ds(start, size)
-        copies.append(pltpu.make_async_copy(pack_ref.at[block, rows], held_ref.at[rows], sems.at[i]))
-        copies[-1].start()
-    own = own_ref[...]
-    units = own.shape[1]
-    chips, cores, share, half = out_ref.shape
-    for part in range(D // units):
-        rows = slice(D + units * part, D + units * (part + 1))
-        total_ref[part] = jnp.dot(own, own_pack_ref[block, rows, :], preferred_element_type=jnp.float32)
-    copies[0].wait()
-    copies[1].wait()
-    other = hidden_of(normed_ref[...], held_ref[:D, :], bias_of(held_ref[2 * D :, :]))
-    copies[2].wait()
-    for part in range(D // units):
-        rows = slice(D + units * part, D + units * (part + 1))
-        total = total_ref[part] + jnp.dot(other, held_ref[rows, :], preferred_element_type=jnp.float32)
-        total = jnp.transpose(total.astype(jnp.bfloat16))
-        for at in range(units // share):
-            chip, core = divmod(part * (units // share) + at, cores)
-            out_ref[chip, core] = total[share * at : share * (at + 1), :]
-
-
-def rest(block, out, normed, own, own_pack, pack):
-    units = own.shape[1]
+    for copy in copies[:CHUNKS]:
+        copy.wait()
+    hidden = hidden_of(normed, expand_ref[...], unit_bias_ref[block : block + 1, :])
+    for copy in copies[CHUNKS:]:
+        copy.wait()
+    for part in range(parts):
+        weights = reduce_ref[:, units * part : units * (part + 1)]
+        total_ref[part] = jnp.dot(hidden, weights, preferred_element_type=jnp.float32)
+
+
+def own_part(block, x, gain, bias, unit_bias, w_expand, w_reduce):
+    units, half = w_expand.shape[2], x.shape[2]
+    raw = pl.BlockSpec(memory_space=pltpu.HBM)
     return pl.pallas_call(
-        lambda *refs: rest_kernel(block, *refs),
-        out_shape=out,
-        in_specs=[VMEM, VMEM, VMEM, pl.BlockSpec(memory_space=pltpu.HBM)],
-        out_specs=VMEM,
+        lambda *refs: own_kernel(block, *refs),
+        out_shape=[
+            jax.ShapeDtypeStruct((half, D), jnp.bfloat16),
+            jax.ShapeDtypeStruct((D // units, half, units), jnp.float32),
+        ],
+        in_specs=[VMEM, VMEM, VMEM, VMEM, raw, raw],
+        out_specs=[VMEM, VMEM],
         scratch_shapes=[
-            pltpu.VMEM(pack.shape[1:], jnp.bfloat16),
-            pltpu.VMEM((D // units, own.shape[0], units), jnp.float32),
-            pltpu.SemaphoreType.DMA((3,)),
+            pltpu.VMEM(w_expand.shape[1:], jnp.bfloat16),
+            pltpu.VMEM(w_reduce.shape[1:], jnp.bfloat16),
+            pltpu.SemaphoreType.DMA((2 * CHUNKS,)),
         ],
         compiler_params=pltpu.CompilerParams(vmem_limit_bytes=16 << 20),
-    )(normed, own, own_pack, pltpu.with_memory_space_constraint(pack, pltpu.HBM))
-
-
-def mix_kernel(parts_ref, stream_ref, affine_ref, out_ref):
+        cost_estimate=pl.CostEstimate(flops=10**11, transcendentals=0, bytes_accessed=10**6),
+    )(x, gain, bias, unit_bias, *[pltpu.with_memory_space_constraint(array, pltpu.HBM) for array in (w_expand, w_reduce)])
+
+
+def rest_kernel(block, normed_ref, total_ref, pack_ref, out_ref):
+    other = hidden_of(normed_ref[...], pack_ref[block, :D, :], bias_of(pack_ref[block, 2 * D :, :]))
+    for part in range(total_ref.shape[0]):
+        weights = pack_ref[block, rows_of(part, other.shape[1]), :]
+        scatter(part, total_ref[part] + jnp.dot(other, weights, preferred_element_type=jnp.float32), out_ref)
+
+
+def mlp_kernel(block, x_ref, gain_ref, bias_ref, expand_ref, reduce_ref, unit_bias_ref, pack_ref, out_ref):
+    normed = normalized(block, x_ref, gain_ref, bias_ref)
+    own = hidden_of(normed, expand_ref[block], unit_bias_ref[block : block + 1, :])
+    other = hidden_of(normed, pack_ref[block, :D, :], bias_of(pack_ref[block, 2 * D :, :]))
+    units = own.shape[1]
+    for part in range(D // units):
+        own_weights = reduce_ref[block, :, units * part : units * (part + 1)]
+        total = jnp.dot(own, own_weights, preferred_element_type=jnp.float32) + jnp.dot(
+            other, pack_ref[block, rows_of(part, units), :], preferred_element_type=jnp.float32
+        )
+        scatter(part, total, out_ref)
+
+
+def mix_kernel(parts_ref, stream_ref, affine_ref, out_ref, *edge_refs):
     height, share, width = stream_ref.shape
     scale, shift = affine_ref[0], affine_ref[1]
     for r in range(height):
@@ -216,7 +254,11 @@
         for copy in range(1, parts_ref.shape[0]):
             mixed = mixed + parts_ref[copy, half, :, lanes].astype(jnp.float32)
         updated = stream_ref[r].astype(jnp.float32) + scale * (mixed + shift)
-        out_ref[r] = updated.astype(jnp.bfloat16)
+        row = updated.astype(jnp.bfloat16)
+        out_ref[r] = row
+        for ref, start in zip(edge_refs, (height - HALF, 0)):
+            if start <= r < start + HALF:
+                ref[r - start] = row
 
 
 def per_device(features, depth_kernel, norm_gain, norm_bias, w_expand, b_expand, w_reduce, b_reduce, layer_scale):
@@ -232,43 +274,46 @@
     stream = jnp.transpose(features, (0, 2, 1))
     taps = jnp.transpose(depth_kernel, (1, 2, 0, 3)).reshape(TAPS * TAPS, BLOCKS, share)
 
+    last = first = stream
     for block in range(BLOCKS):
-        after = lax.ppermute(stream, "space", up)
-        before = lax.ppermute(stream, "space", down)
+        before = lax.ppermute(last, "space", down)
+        after = lax.ppermute(first, "space", up)
         if block == 0:
             wide, affine, stream, taps, layer_scale, b_reduce = entered(stream, taps, layer_scale, b_reduce)
         else:
             wide, affine = next_wide, next_affine
+        edges = (after, before) if block == 0 else (before, after)
         filtered = call(
-            conv_kernel,
+            lambda *refs: conv_kernel(block > 0, *refs),
             jax.ShapeDtypeStruct((copies, CORES, share, half), jnp.bfloat16),
-            before, stream, after, wide,
+            edges[0], stream, edges[1], wide,
         )
         if block == 0:
             filtered, own_bias, next_scale = lax.optimization_barrier((filtered, b_expand, layer_scale))
-            own_pack = packed(w_expand, w_reduce, own_bias)
-            pack = lax.ppermute(own_pack, "tensor", sibling)
+            pack = lax.ppermute(packed(w_expand, w_reduce, own_bias), "tensor", sibling)
             next_wide, next_affine = call(
                 lambda *refs: spread(1, *refs), spread_shapes(share, width), taps, next_scale, b_reduce
             )
         filtered = lax.all_to_all(filtered.reshape(members, share, half), "tensor", 0, 0, tiled=True)
+        out = jax.ShapeDtypeStruct((copies, CORES, share, half), jnp.bfloat16)
         if block == 0:
             filtered, next_wide, next_affine = lax.optimization_barrier((filtered, next_wide, next_affine))
-        normed, own = call(
-            lambda *refs: own_kernel(block, *refs),
-            (jax.ShapeDtypeStruct((half, D), jnp.bfloat16), jax.ShapeDtypeStruct((half, units), jnp.bfloat16)),
-            filtered, norm_gain, norm_bias, own_pack,
-            cost=pl.CostEstimate(flops=10**11, transcendentals=0, bytes_accessed=10**6),
-        )
-        partial = rest(
-            block, jax.ShapeDtypeStruct((copies, CORES, share, half), jnp.bfloat16), normed, own, own_pack, pack
-        )
+            normed, total = own_part(block, filtered, norm_gain, norm_bias, b_expand, w_expand, w_reduce)
+            partial = call(lambda *refs: rest_kernel(block, *refs), out, normed, total, pack)
+        else:
+            partial = call(
+                lambda *refs: mlp_kernel(block, *refs),
+                out,
+                filtered, norm_gain, norm_bias, w_expand, w_reduce, b_expand, pack,
+            )
         partial = lax.all_to_all(partial.reshape(members, share, half), "tensor", 0, 0, tiled=True)
-        stream = call(
-            mix_kernel,
-            jax.ShapeDtypeStruct((height, share, width), jnp.bfloat16),
-            partial.reshape(copies, CORES, share, half), stream, affine,
-        )
+        partial = partial.reshape(copies, CORES, share, half)
+        whole = jax.ShapeDtypeStruct((height, share, width), jnp.bfloat16)
+        if block + 1 < BLOCKS:
+            edge = jax.ShapeDtypeStruct((HALF, share, width), jnp.bfloat16)
+            stream, last, first = call(mix_kernel, (whole, edge, edge), partial, stream, affine)
+        else:
+            stream = call(mix_kernel, whole, partial, stream, affine)
     return jnp.transpose(stream, (0, 2, 1))
 
 

time: 101 us -> 94.8 us (0.939)
  the two profiles are of different devices: /device:TPU:32 before, /device:TPU:56 now
where the time goes in v5:
time: 94.8 us; the launch traced here: 93.9 us
  blocking collectives  40.5 us (43%)
  starting transfers between devices  29.7 us (31%)
  Pallas kernels  12.3 us (13%)
  waiting for transfers between devices  10.1 us (11%)
  local copies, waits for them, and re-layouts  1.18 us (1%)
    all_to_all x2, blocking collectives, per_device(): lax.all_to_all(partial.reshape(members, share, half), 'tensor', 0, 0, til...  27 us
    all_to_all x1, blocking collectives, per_device(): lax.all_to_all(filtered.reshape(members, share, half), 'tensor', 0, 0, ti...  13.5 us
    ppermute x2, starting transfers between devices, per_device(): before = lax.ppermute(last, 'space', down)  12.6 us
    ppermute x2, starting transfers between devices, per_device(): after = lax.ppermute(first, 'space', up)  10.4 us
    ppermute x2, waiting for transfers between devices, per_device(): after = lax.ppermute(first, 'space', up)  5.93 us
    pallas_call x7, Pallas kernels, call(): pl.pallas_call(body, out_shape=outs, in_specs=[VMEM] * len(args), out_spe...  5.5 us
    all_to_all x1, starting transfers between devices, per_device(): lax.all_to_all(filtered.reshape(members, share, half), 'tensor', 0, 0, ti...  4.4 us
    all_to_all x1, waiting for transfers between devices, per_device(): lax.all_to_all(filtered.reshape(members, share, half), 'tensor', 0, 0, ti...  3.54 us
  transfers between devices with their start and end apart: 6, of which 5 were waited for; matrix products, arithmetic and copies ran while one was open for 0% of the time, Pallas kernels for 8%

profile of v5, /device:TPU:56, one launch (start us, length us, event | category | flops | bytes accessed | tf_op | source)
XLA Modules:
  0.0 93.9 jit_solution(10818718964970450835)
XLA Ops:
  0.0 6.1 %collective-permute-start.1 = (bf16[4,64,128]{2,1,0:T(8,128)(2,1)}, bf16[4,64,128]{2,1,0:T(8,128)(2,1)S(1)}, u32[]{:S(2)}, u32[]{:S(2)}) collective-permute-start(bf16[4,64,128]{2,1,0:T(8,128)(2,1)} %bitcast.16), channel_id=1, source_target_pairs={{0,16},{16,32},{32,48},{48,64},{64,80},{80,96},{96,112},{112,128},... | collective-permute-start | bytes 196616 | tf_op jit(solution)/shard_map/ppermute | solution.py:279
  6.1 7.6 %collective-permute-start = (bf16[4,64,128]{2,1,0:T(8,128)(2,1)}, bf16[4,64,128]{2,1,0:T(8,128)(2,1)S(1)}, u32[]{:S(2)}, u32[]{:S(2)}) collective-permute-start(bf16[4,64,128]{2,1,0:T(8,128)(2,1)} %bitcast.17), channel_id=1, source_target_pairs={{16,0},{32,16},{48,32},{64,48},{80,64},{96,80},{112,96},{128,112},... | collective-permute-start | bytes 196616 | tf_op jit(solution)/shard_map/ppermute | solution.py:280
  13.6 1.5 %shard_map.91 = (f32[49,64,128]{2,1,0:T(8,128)S(1)}, f32[2,64,128]{2,1,0:T(8,128)S(1)}, bf16[4,64,128]{2,1,0:T(8,128)(2,1)S(1)}, bf16[49,2,64]{2,1,0:T(2,128)(2,...) custom-call(bf16[4,64,128]{2,1,0:T(8,128)(2,1)} %bitcast.18, bf16[49,2,64]{2,1,0:T(2,128)(2,1)} %bitcast.19, ...), custom_call_target="tpu_custom_call" | custom-call | tf_op jit(solution)/shard_map/pallas_call | solution.py:58
  15.1 0.2 collective-permute-done.1.refs_2_
  15.3 1.7 %collective-permute-done.refs_0_ = bf16[4,64,128]{2,1,0:T(8,128)(2,1)S(1)} collective-permute-done((bf16[4,64,128]{2,1,0:T(8,128)(2,1)}, bf16[4,64,128]{2,1,0:T(8,128)(2,1)S(1)}, u32[]{:S(2)}, u32[]{:S(2)}) %collective-permute-start) | collective-permute-done | bytes 65568 | tf_op jit(solution)/shard_map/ppermute | solution.py:280
  17.0 1.3 %shard_map.92 = bf16[8,2,64,256]{3,2,1,0:T(8,128)(2,1)} custom-call(bf16[4,64,128]{2,1,0:T(8,128)(2,1)S(1)} %collective-permute-done.refs_0_, bf16[4,64,128]{2,1,0:T(8,128)(2,1)S(1)} %get-tuple-element.24.refs_1_.stream_ref, bf16[4,64,128]{2,1,0:T(8,128)(2,1)S(1)} %collective-permute-done.1.refs_2_, f32[49,64,128]{2,1,0:T(8,128)S(1)} %get-tuple-element.25.refs_3_), custom_call_target="tpu_custom_call" | custom-call | tf_op jit(solution)/shard_map/pallas_call | solution.py:20
  18.3 4.4 %all-to-all-start = ((bf16[16,64,256]{2,1,0:T(8,128)(2,1)}), bf16[16,64,256]{2,1,0:T(8,128)(2,1)S(1)}, u32[]{:S(2)}, u32[]{:S(2)}) async-start(bf16[16,64,256]{2,1,0:T(8,128)(2,1)} %bitcast.3), calls=%async_computation | async-start | bytes 1048576 | tf_op jit(solution)/shard_map/all_to_all | solution.py:297
  22.7 0.0 copy-start.4
  22.7 0.0 copy-start.5
  22.8 0.0 copy-start.6
  22.8 3.1 %shard_map.95 = bf16[2,2056,256]{2,1,0:T(8,128)(2,1)} custom-call(bf16[2,1024,256]{2,1,0:T(8,128)(2,1)} %refs_3_.3, bf16[2,256,1024]{2,1,0:T(8,128)(2,1)} %refs_4_.3, f32[2,256]{1,0:T(2,128)} %refs_5_.3), custom_call_target="tpu_custom_call" | custom-call | tf_op jit(solution)/shard_map/pallas_call | solution.py:100
  25.9 2.3 %collective-permute-start.2 = (bf16[2,2056,256]{2,1,0:T(8,128)(2,1)}, bf16[2,2056,256]{2,1,0:T(8,128)(2,1)S(1)}, u32[]{:S(2)}, u32[]{:S(2)}) collective-permute-start(bf16[2,2056,256]{2,1,0:T(8,128)(2,1)} %shard_map.95), channel_id=1, source_target_pairs={{0,1},{1,0},{2,3},{3,2},{4,5},{5,4},{6,7},{7,6},{8,9},{9,8},{10,11... | collective-permute-start | bytes 6316040 | tf_op jit(solution)/shard_map/ppermute | solution.py:293
  28.2 0.7 shard_map.93
  28.9 0.0 copy-start.2
  28.9 1.1 %copy-done.2 = f32[49,64,128]{2,1,0:T(8,128)} copy-done((f32[49,64,128]{2,1,0:T(8,128)}, f32[49,64,128]{2,1,0:T(8,128)S(1)}, u32[]{:S(2)}) %copy-start.2) | copy-done | bytes 1605656
  30.1 3.5 %all-to-all-done.refs_0_ = bf16[16,64,256]{2,1,0:T(8,128)(2,1)S(1)} async-done(((bf16[16,64,256]{2,1,0:T(8,128)(2,1)}), bf16[16,64,256]{2,1,0:T(8,128)(2,1)S(1)}, u32[]{:S(2)}, u32[]{:S(2)}) %all-to-all-start) | async-done | bytes 524320 | tf_op jit(solution)/shard_map/all_to_all | solution.py:297
  33.6 0.0 copy-done.4
  33.6 0.0 copy-done.5
  33.6 0.0 copy-done.6
  33.6 2.2 %shard_map.94 = (bf16[256,1024]{1,0:T(8,128)(2,1)S(1)}, f32[4,256,256]{2,1,0:T(8,128)S(1)}) custom-call(bf16[16,64,256]{2,1,0:T(8,128)(2,1)S(1)} %all-to-all-done.refs_0_, f32[2,1024]{1,0:T(2,128)S(1)} %copy-done.4, f32[2,1024]{1,0:T(2,128)S(1)} %copy-done.5, f32[2,256]{1,0:T(2,128)S(1)} %copy-done.6, bf16[2,1024,256]{2,1,0:T(8,128)(2,1)} %refs_3_.3, ...), custom_call_target="tpu_custom_call" | custom-call | flops 99999997952 | bytes 1000000 | tf_op jit(solution)/shard_map/pallas_call | solution.py:209
  35.8 0.0 collective-permute-done.2.refs_2_.refs_6_
  35.8 0.0 copy-start.3
  35.8 0.8 shard_map.96
  36.6 13.5 %all_to_all.20 = bf16[16,64,256]{2,1,0:T(8,128)(2,1)S(1)} all-to-all(bf16[16,64,256]{2,1,0:T(8,128)(2,1)S(1)} %bitcast.15), channel_id=1, replica_groups=mesh['space'=32,'tensor'=16] {'tensor'}, dimensions={0} | all-to-all | bytes 1048576 | tf_op jit(solution)/shard_map/all_to_all | solution.py:309
  50.1 0.0 copy-start
  50.1 0.0 copy-start.1
  50.1 0.1 shard_map.97
  50.2 6.5 %collective-permute-start.3 = (bf16[3,64,128]{2,1,0:T(8,128)(2,1)S(1)}, bf16[3,64,128]{2,1,0:T(8,128)(2,1)S(1)}, u32[]{:S(2)}, u32[]{:S(2)}) collective-permute-start(bf16[3,64,128]{2,1,0:T(8,128)(2,1)S(1)} %get-tuple-element.38), channel_id=1, source_target_pairs={{0,16},{16,32},{32,48},{48,64},{64,80},{80,96},{96,112},{112,128},... | collective-permute-start | bytes 147464 | tf_op jit(solution)/shard_map/ppermute | solution.py:279
  56.7 2.9 %collective-permute-start.4 = (bf16[3,64,128]{2,1,0:T(8,128)(2,1)S(1)}, bf16[3,64,128]{2,1,0:T(8,128)(2,1)S(1)}, u32[]{:S(2)}, u32[]{:S(2)}) collective-permute-start(bf16[3,64,128]{2,1,0:T(8,128)(2,1)S(1)} %get-tuple-element.40), channel_id=1, source_target_pairs={{16,0},{32,16},{48,32},{64,48},{80,64},{96,80},{112,96},{128,112},... | collective-permute-start | bytes 147464 | tf_op jit(solution)/shard_map/ppermute | solution.py:280
  59.6 0.4 collective-permute-done.3.refs_0_
  60.0 4.3 %collective-permute-done.4.refs_2_ = bf16[3,64,128]{2,1,0:T(8,128)(2,1)S(1)} collective-permute-done((bf16[3,64,128]{2,1,0:T(8,128)(2,1)S(1)}, bf16[3,64,128]{2,1,0:T(8,128)(2,1)S(1)}, u32[]{:S(2)}, u32[]{:S(2)}) %collective-permute-start.4) | collective-permute-done | bytes 49184 | tf_op jit(solution)/shard_map/ppermute | solution.py:280
  64.3 0.0 copy-done.3
  64.3 0.5 shard_map.98
  64.8 13.5 %all_to_all.21.refs_0_ = bf16[16,64,256]{2,1,0:T(8,128)(2,1)S(1)} all-to-all(bf16[16,64,256]{2,1,0:T(8,128)(2,1)S(1)} %bitcast.14), channel_id=1, replica_groups=mesh['space'=32,'tensor'=16] {'tensor'}, dimensions={0} | all-to-all | bytes 1048576 | tf_op jit(solution)/shard_map/all_to_all | solution.py:297
  78.3 0.0 copy-done
  78.3 0.0 copy-done.1
  78.3 1.4 %shard_map.99 = bf16[8,2,64,256]{3,2,1,0:T(8,128)(2,1)S(1)} custom-call(bf16[16,64,256]{2,1,0:T(8,128)(2,1)S(1)} %all_to_all.21.refs_0_, f32[2,1024]{1,0:T(2,128)S(1)} %copy-done.4, f32[2,1024]{1,0:T(2,128)S(1)} %copy-done.5, bf16[2,1024,256]{2,1,0:T(8,128)(2,1)S(1)} %copy-done, bf16[2,256,1024]{2,1,0:T(8,128)(2,1)S(1)} %copy-done.1, ...), custom_call_target="tpu_custom_call" | custom-call | tf_op jit(solution)/shard_map/pallas_call | solution.py:20
  79.6 13.5 %all_to_all.22 = bf16[16,64,256]{2,1,0:T(8,128)(2,1)S(1)} all-to-all(bf16[16,64,256]{2,1,0:T(8,128)(2,1)S(1)} %bitcast.11), channel_id=1, replica_groups=mesh['space'=32,'tensor'=16] {'tensor'}, dimensions={0} | all-to-all | bytes 1048576 | tf_op jit(solution)/shard_map/all_to_all | solution.py:309
  93.1 0.7 shard_map.100
Async XLA Ops:
  0.0 15.3 %collective-permute-start.1 = (bf16[4,64,128]{2,1,0:T(8,128)(2,1)}, bf16[4,64,128]{2,1,0:T(8,128)(2,1)S(1)}, u32[]{:S(2)}, u32[]{:S(2)}) collective-permute-start(bf16[4,64,128]{2,1,0:T(8,128)(2,1)} %bitcast.16), channel_id=1, source_target_pairs={{0,16},{16,32},{32,48},{48,64},{64,80},{80,96},{96,112},{112,128},... | collective-permute-start | bytes 196616 | tf_op jit(solution)/shard_map/ppermute | solution.py:279
  6.1 10.9 %collective-permute-start = (bf16[4,64,128]{2,1,0:T(8,128)(2,1)}, bf16[4,64,128]{2,1,0:T(8,128)(2,1)S(1)}, u32[]{:S(2)}, u32[]{:S(2)}) collective-permute-start(bf16[4,64,128]{2,1,0:T(8,128)(2,1)} %bitcast.17), channel_id=1, source_target_pairs={{16,0},{32,16},{48,32},{64,48},{80,64},{96,80},{112,96},{128,112},... | collective-permute-start | bytes 196616 | tf_op jit(solution)/shard_map/ppermute | solution.py:280
  18.3 15.3 %all-to-all-start = ((bf16[16,64,256]{2,1,0:T(8,128)(2,1)}), bf16[16,64,256]{2,1,0:T(8,128)(2,1)S(1)}, u32[]{:S(2)}, u32[]{:S(2)}) async-start(bf16[16,64,256]{2,1,0:T(8,128)(2,1)} %bitcast.3), calls=%async_computation | async-start | bytes 1048576 | tf_op jit(solution)/shard_map/all_to_all | solution.py:297
  22.7 10.9 %copy-start.4 = (f32[2,1024]{1,0:T(2,128)S(1)}, f32[2,1024]{1,0:T(2,128)}, u32[]{:S(2)}) copy-start(f32[2,1024]{1,0:T(2,128)} %refs_1_.3) | copy-start | bytes 24580
  22.7 10.9 %copy-start.5 = (f32[2,1024]{1,0:T(2,128)S(1)}, f32[2,1024]{1,0:T(2,128)}, u32[]{:S(2)}) copy-start(f32[2,1024]{1,0:T(2,128)} %refs_2_.3) | copy-start | bytes 24580
  22.8 10.8 %copy-start.6 = (f32[2,256]{1,0:T(2,128)S(1)}, f32[2,256]{1,0:T(2,128)}, u32[]{:S(2)}) copy-start(f32[2,256]{1,0:T(2,128)} %refs_5_.3) | copy-start | bytes 6148
  25.9 9.9 %collective-permute-start.2 = (bf16[2,2056,256]{2,1,0:T(8,128)(2,1)}, bf16[2,2056,256]{2,1,0:T(8,128)(2,1)S(1)}, u32[]{:S(2)}, u32[]{:S(2)}) collective-permute-start(bf16[2,2056,256]{2,1,0:T(8,128)(2,1)} %shard_map.95), channel_id=1, source_target_pairs={{0,1},{1,0},{2,3},{3,2},{4,5},{5,4},{6,7},{7,6},{8,9},{9,8},{10,11... | collective-permute-start | bytes 6316040 | tf_op jit(solution)/shard_map/ppermute | solution.py:293
  28.9 1.2 %copy-start.2 = (f32[49,64,128]{2,1,0:T(8,128)}, f32[49,64,128]{2,1,0:T(8,128)S(1)}, u32[]{:S(2)}) copy-start(f32[49,64,128]{2,1,0:T(8,128)S(1)} %get-tuple-element.41.refs_3_) | copy-start | bytes 4816900
  35.8 28.4 %copy-start.3 = (f32[49,64,128]{2,1,0:T(8,128)S(1)}, f32[49,64,128]{2,1,0:T(8,128)}, u32[]{:S(2)}) copy-start(f32[49,64,128]{2,1,0:T(8,128)} %copy-done.2) | copy-start | bytes 4816900
  50.1 28.1 %copy-start = (bf16[2,1024,256]{2,1,0:T(8,128)(2,1)S(1)}, bf16[2,1024,256]{2,1,0:T(8,128)(2,1)}, u32[]{:S(2)}) copy-start(bf16[2,1024,256]{2,1,0:T(8,128)(2,1)} %refs_3_.3) | copy-start | bytes 3145732
  50.1 28.1 %copy-start.1 = (bf16[2,256,1024]{2,1,0:T(8,128)(2,1)S(1)}, bf16[2,256,1024]{2,1,0:T(8,128)(2,1)}, u32[]{:S(2)}) copy-start(bf16[2,256,1024]{2,1,0:T(8,128)(2,1)} %refs_4_.3) | copy-start | bytes 3145732
  50.2 9.8 %collective-permute-start.3 = (bf16[3,64,128]{2,1,0:T(8,128)(2,1)S(1)}, bf16[3,64,128]{2,1,0:T(8,128)(2,1)S(1)}, u32[]{:S(2)}, u32[]{:S(2)}) collective-permute-start(bf16[3,64,128]{2,1,0:T(8,128)(2,1)S(1)} %get-tuple-element.38), channel_id=1, source_target_pairs={{0,16},{16,32},{32,48},{48,64},{64,80},{80,96},{96,112},{112,128},... | collective-permute-start | bytes 147464 | tf_op jit(solution)/shard_map/ppermute | solution.py:279
  56.7 7.5 %collective-permute-start.4 = (bf16[3,64,128]{2,1,0:T(8,128)(2,1)S(1)}, bf16[3,64,128]{2,1,0:T(8,128)(2,1)S(1)}, u32[]{:S(2)}, u32[]{:S(2)}) collective-permute-start(bf16[3,64,128]{2,1,0:T(8,128)(2,1)S(1)} %get-tuple-element.40), channel_id=1, source_target_pairs={{16,0},{32,16},{48,32},{64,48},{80,64},{96,80},{112,96},{128,112},... | collective-permute-start | bytes 147464 | tf_op jit(solution)/shard_map/ppermute | solution.py:280

commit v6 on v5

--- a/solution.py
+++ b/solution.py
@@ -9,7 +9,6 @@
 TAPS = 7
 HALF = TAPS // 2
 BLOCKS = 2
-CHUNKS = 8
 CORES = 2
 
 VMEM = pl.BlockSpec(memory_space=pltpu.VMEM)
@@ -179,56 +178,22 @@
     return slice(D + units * part, D + units * (part + 1))
 
 
-def own_kernel(
-    block, x_ref, gain_ref, bias_ref, unit_bias_ref, expand_in, reduce_in,
-    normed_ref, total_ref, expand_ref, reduce_ref, sems,
-):
-    parts, half, units = total_ref.shape
-    copies = []
-    for i in range(2 * CHUNKS):
-        src, dst = ((expand_in, expand_ref), (reduce_in, reduce_ref))[i // CHUNKS]
-        size = dst.shape[0] // CHUNKS
-        rows = pl.ds(size * (i % CHUNKS), size)
-        copies.append(pltpu.make_async_copy(src.at[block, rows], dst.at[rows], sems.at[i]))
-        copies[-1].start()
+def own_kernel(block, x_ref, gain_ref, bias_ref, unit_bias_ref, expand_ref, normed_ref, own_ref):
     normed = normalized(block, x_ref, gain_ref, bias_ref)
     normed_ref[...] = normed
-    for copy in copies[:CHUNKS]:
-        copy.wait()
-    hidden = hidden_of(normed, expand_ref[...], unit_bias_ref[block : block + 1, :])
-    for copy in copies[CHUNKS:]:
-        copy.wait()
-    for part in range(parts):
-        weights = reduce_ref[:, units * part : units * (part + 1)]
-        total_ref[part] = jnp.dot(hidden, weights, preferred_element_type=jnp.float32)
-
-
-def own_part(block, x, gain, bias, unit_bias, w_expand, w_reduce):
-    units, half = w_expand.shape[2], x.shape[2]
-    raw = pl.BlockSpec(memory_space=pltpu.HBM)
-    return pl.pallas_call(
-        lambda *refs: own_kernel(block, *refs),
-        out_shape=[
-            jax.ShapeDtypeStruct((half, D), jnp.bfloat16),
-            jax.ShapeDtypeStruct((D // units, half, units), jnp.float32),
-        ],
-        in_specs=[VMEM, VMEM, VMEM, VMEM, raw, raw],
-        out_specs=[VMEM, VMEM],
-        scratch_shapes=[
-            pltpu.VMEM(w_expand.shape[1:], jnp.bfloat16),
-            pltpu.VMEM(w_reduce.shape[1:], jnp.bfloat16),
-            pltpu.SemaphoreType.DMA((2 * CHUNKS,)),
-        ],
-        compiler_params=pltpu.CompilerParams(vmem_limit_bytes=16 << 20),
-        cost_estimate=pl.CostEstimate(flops=10**11, transcendentals=0, bytes_accessed=10**6),
-    )(x, gain, bias, unit_bias, *[pltpu.with_memory_space_constraint(array, pltpu.HBM) for array in (w_expand, w_reduce)])
-
-
-def rest_kernel(block, normed_ref, total_ref, pack_ref, out_ref):
+    own_ref[...] = hidden_of(normed, expand_ref[block], unit_bias_ref[block : block + 1, :])
+
+
+def rest_kernel(block, normed_ref, own_ref, reduce_ref, pack_ref, out_ref):
+    own = own_ref[...]
+    units = own.shape[1]
     other = hidden_of(normed_ref[...], pack_ref[block, :D, :], bias_of(pack_ref[block, 2 * D :, :]))
-    for part in range(total_ref.shape[0]):
-        weights = pack_ref[block, rows_of(part, other.shape[1]), :]
-        scatter(part, total_ref[part] + jnp.dot(other, weights, preferred_element_type=jnp.float32), out_ref)
+    for part in range(D // units):
+        own_weights = reduce_ref[block, :, units * part : units * (part + 1)]
+        total = jnp.dot(own, own_weights, preferred_element_type=jnp.float32) + jnp.dot(
+            other, pack_ref[block, rows_of(part, units), :], preferred_element_type=jnp.float32
+        )
+        scatter(part, total, out_ref)
 
 
 def mlp_kernel(block, x_ref, gain_ref, bias_ref, expand_ref, reduce_ref, unit_bias_ref, pack_ref, out_ref):
@@ -298,8 +263,13 @@
         out = jax.ShapeDtypeStruct((copies, CORES, share, half), jnp.bfloat16)
         if block == 0:
             filtered, next_wide, next_affine = lax.optimization_barrier((filtered, next_wide, next_affine))
-            normed, total = own_part(block, filtered, norm_gain, norm_bias, b_expand, w_expand, w_reduce)
-            partial = call(lambda *refs: rest_kernel(block, *refs), out, normed, total, pack)
+            normed, own = call(
+                lambda *refs: own_kernel(block, *refs),
+                (jax.ShapeDtypeStruct((half, D), jnp.bfloat16), jax.ShapeDtypeStruct((half, units), jnp.bfloat16)),
+                filtered, norm_gain, norm_bias, b_expand, w_expand,
+                cost=pl.CostEstimate(flops=10**11, transcendentals=0, bytes_accessed=10**6),
+            )
+            partial = call(lambda *refs: rest_kernel(block, *refs), out, normed, own, w_reduce, pack)
         else:
             partial = call(
                 lambda *refs: mlp_kernel(block, *refs),

time: 94.8 us -> 94.6 us (level)
    pallas_call x1 -> x0, Pallas kernels: 2.2 us -> none  [own_part(): pl.pallas_call(lambda *refs: own_kernel(block, *refs), out_shape=[jax.Sha...]
    pallas_call x7 -> x8, Pallas kernels: 5.5 us -> 7.57 us  [call(): pl.pallas_call(body, out_shape=outs, in_specs=[VMEM] * len(args), out_spe...]
where the time goes in v6:
time: 94.6 us; the launch traced here: 93.7 us
  blocking collectives  40.5 us (43%)
  starting transfers between devices  29.6 us (31%)
  Pallas kernels  12.2 us (13%)
  waiting for transfers between devices  10.1 us (11%)
  local copies, waits for them, and re-layouts  1.18 us (1%)
    all_to_all x2, blocking collectives, per_device(): lax.all_to_all(partial.reshape(members, share, half), 'tensor', 0, 0, til...  27 us
    all_to_all x1, blocking collectives, per_device(): lax.all_to_all(filtered.reshape(members, share, half), 'tensor', 0, 0, ti...  13.5 us
    ppermute x2, starting transfers between devices, per_device(): before = lax.ppermute(last, 'space', down)  12.4 us
    ppermute x2, starting transfers between devices, per_device(): after = lax.ppermute(first, 'space', up)  10.4 us
    pallas_call x8, Pallas kernels, call(): pl.pallas_call(body, out_shape=outs, in_specs=[VMEM] * len(args), out_spe...  7.57 us
    ppermute x2, waiting for transfers between devices, per_device(): after = lax.ppermute(first, 'space', up)  5.93 us
    all_to_all x1, starting transfers between devices, per_device(): lax.all_to_all(filtered.reshape(members, share, half), 'tensor', 0, 0, ti...  4.46 us
    all_to_all x1, waiting for transfers between devices, per_device(): lax.all_to_all(filtered.reshape(members, share, half), 'tensor', 0, 0, ti...  3.57 us
  transfers between devices with their start and end apart: 6, of which 5 were waited for; matrix products, arithmetic and copies ran while one was open for 0% of the time, Pallas kernels for 8%

profile of v6, /device:TPU:56, one launch (start us, length us, event | category | flops | bytes accessed | tf_op | source)
XLA Modules:
  0.0 93.7 jit_solution(4848512910520310694)
XLA Ops:
  0.0 6.1 %collective-permute-start.1 = (bf16[4,64,128]{2,1,0:T(8,128)(2,1)}, bf16[4,64,128]{2,1,0:T(8,128)(2,1)S(1)}, u32[]{:S(2)}, u32[]{:S(2)}) collective-permute-start(bf16[4,64,128]{2,1,0:T(8,128)(2,1)} %bitcast.16), channel_id=1, source_target_pairs={{0,16},{16,32},{32,48},{48,64},{64,80},{80,96},{96,112},{112,128},... | collective-permute-start | bytes 196616 | tf_op jit(solution)/shard_map/ppermute | solution.py:244
  6.1 7.6 %collective-permute-start = (bf16[4,64,128]{2,1,0:T(8,128)(2,1)}, bf16[4,64,128]{2,1,0:T(8,128)(2,1)S(1)}, u32[]{:S(2)}, u32[]{:S(2)}) collective-permute-start(bf16[4,64,128]{2,1,0:T(8,128)(2,1)} %bitcast.17), channel_id=1, source_target_pairs={{16,0},{32,16},{48,32},{64,48},{80,64},{96,80},{112,96},{128,112},... | collective-permute-start | bytes 196616 | tf_op jit(solution)/shard_map/ppermute | solution.py:245
  13.6 1.5 %shard_map.91 = (f32[49,64,128]{2,1,0:T(8,128)S(1)}, f32[2,64,128]{2,1,0:T(8,128)S(1)}, bf16[4,64,128]{2,1,0:T(8,128)(2,1)S(1)}, bf16[49,2,64]{2,1,0:T(2,128)(2,...) custom-call(bf16[4,64,128]{2,1,0:T(8,128)(2,1)} %bitcast.18, bf16[49,2,64]{2,1,0:T(2,128)(2,1)} %bitcast.19, ...), custom_call_target="tpu_custom_call" | custom-call | tf_op jit(solution)/shard_map/pallas_call | solution.py:57
  15.1 0.2 collective-permute-done.1.refs_2_
  15.3 1.7 %collective-permute-done.refs_0_ = bf16[4,64,128]{2,1,0:T(8,128)(2,1)S(1)} collective-permute-done((bf16[4,64,128]{2,1,0:T(8,128)(2,1)}, bf16[4,64,128]{2,1,0:T(8,128)(2,1)S(1)}, u32[]{:S(2)}, u32[]{:S(2)}) %collective-permute-start) | collective-permute-done | bytes 65568 | tf_op jit(solution)/shard_map/ppermute | solution.py:245
  17.0 1.3 %shard_map.92 = bf16[8,2,64,256]{3,2,1,0:T(8,128)(2,1)} custom-call(bf16[4,64,128]{2,1,0:T(8,128)(2,1)S(1)} %collective-permute-done.refs_0_, bf16[4,64,128]{2,1,0:T(8,128)(2,1)S(1)} %get-tuple-element.24.refs_1_.stream_ref, bf16[4,64,128]{2,1,0:T(8,128)(2,1)S(1)} %collective-permute-done.1.refs_2_, f32[49,64,128]{2,1,0:T(8,128)S(1)} %get-tuple-element.25.refs_3_), custom_call_target="tpu_custom_call" | custom-call | tf_op jit(solution)/shard_map/pallas_call | solution.py:19
  18.3 4.5 %all-to-all-start = ((bf16[16,64,256]{2,1,0:T(8,128)(2,1)}), bf16[16,64,256]{2,1,0:T(8,128)(2,1)}, u32[]{:S(2)}, u32[]{:S(2)}) async-start(bf16[16,64,256]{2,1,0:T(8,128)(2,1)} %bitcast.3), calls=%async_computation | async-start | bytes 1048576 | tf_op jit(solution)/shard_map/all_to_all | solution.py:262
  22.8 0.0 copy-start.1
  22.8 0.0 copy-start.4
  22.8 0.0 copy-start.5
  22.8 0.0 copy-start.6
  22.8 3.2 %shard_map.95 = bf16[2,2056,256]{2,1,0:T(8,128)(2,1)} custom-call(bf16[2,1024,256]{2,1,0:T(8,128)(2,1)} %refs_3_.3, bf16[2,256,1024]{2,1,0:T(8,128)(2,1)} %refs_4_.3, f32[2,256]{1,0:T(2,128)} %refs_5_.1), custom_call_target="tpu_custom_call" | custom-call | tf_op jit(solution)/shard_map/pallas_call | solution.py:99
  26.0 2.3 %collective-permute-start.2 = (bf16[2,2056,256]{2,1,0:T(8,128)(2,1)}, bf16[2,2056,256]{2,1,0:T(8,128)(2,1)S(1)}, u32[]{:S(2)}, u32[]{:S(2)}) collective-permute-start(bf16[2,2056,256]{2,1,0:T(8,128)(2,1)} %shard_map.95), channel_id=1, source_target_pairs={{0,1},{1,0},{2,3},{3,2},{4,5},{5,4},{6,7},{7,6},{8,9},{9,8},{10,11... | collective-permute-start | bytes 6316040 | tf_op jit(solution)/shard_map/ppermute | solution.py:258
  28.3 0.7 shard_map.93
  29.0 0.0 copy-start.2
  29.0 1.1 %copy-done.2 = f32[49,64,128]{2,1,0:T(8,128)} copy-done((f32[49,64,128]{2,1,0:T(8,128)}, f32[49,64,128]{2,1,0:T(8,128)S(1)}, u32[]{:S(2)}) %copy-start.2) | copy-done | bytes 1605656
  30.1 3.6 %all-to-all-done.refs_0_ = bf16[16,64,256]{2,1,0:T(8,128)(2,1)} async-done(((bf16[16,64,256]{2,1,0:T(8,128)(2,1)}), bf16[16,64,256]{2,1,0:T(8,128)(2,1)}, u32[]{:S(2)}, u32[]{:S(2)}) %all-to-all-start) | async-done | bytes 524320 | tf_op jit(solution)/shard_map/all_to_all | solution.py:262
  33.7 0.0 copy-done.1
  33.7 0.0 copy-done.4
  33.7 0.0 copy-done.5
  33.7 0.0 copy-done.6
  33.7 0.0 copy-start
  33.7 1.9 %shard_map.94 = (bf16[256,1024]{1,0:T(8,128)(2,1)S(1)}, bf16[256,256]{1,0:T(8,128)(2,1)S(1)}) custom-call(bf16[16,64,256]{2,1,0:T(8,128)(2,1)} %all-to-all-done.refs_0_, f32[2,1024]{1,0:T(2,128)S(1)} %copy-done.4, f32[2,1024]{1,0:T(2,128)S(1)} %copy-done.5, f32[2,256]{1,0:T(2,128)S(1)} %copy-done.6, bf16[2,1024,256]{2,1,0:T(8,128)(2,1)S(1)} %copy-done.1), custom_call_target="tpu_custom_call" | custom-call | flops 99999997952 | bytes 1000000 | tf_op jit(solution)/shard_map/pallas_call | solution.py:19
  35.6 0.0 collective-permute-done.2.refs_3_.refs_6_
  35.7 0.0 copy-done
  35.7 0.0 copy-start.3
  35.7 1.0 %shard_map.96 = bf16[8,2,64,256]{3,2,1,0:T(8,128)(2,1)S(1)} custom-call(bf16[256,1024]{1,0:T(8,128)(2,1)S(1)} %get-tuple-element.34.refs_0_, bf16[256,256]{1,0:T(8,128)(2,1)S(1)} %get-tuple-element.35.refs_1_, bf16[2,256,1024]{2,1,0:T(8,128)(2,1)S(1)} %copy-done, bf16[2,2056,256]{2,1,0:T(8,128)(2,1)S(1)} %collective-permute-done.2.refs_3_.refs_6_), custom_call_target="tpu_custom_call" | custom-call | tf_op jit(solution)/shard_map/pallas_call | solution.py:19
  36.7 13.5 %all_to_all.20 = bf16[16,64,256]{2,1,0:T(8,128)(2,1)S(1)} all-to-all(bf16[16,64,256]{2,1,0:T(8,128)(2,1)S(1)} %bitcast.11), channel_id=1, replica_groups=mesh['space'=32,'tensor'=16] {'tensor'}, dimensions={0} | all-to-all | bytes 1048576 | tf_op jit(solution)/shard_map/all_to_all | solution.py:279
  50.1 0.1 shard_map.97
  50.2 6.4 %collective-permute-start.3 = (bf16[3,64,128]{2,1,0:T(8,128)(2,1)S(1)}, bf16[3,64,128]{2,1,0:T(8,128)(2,1)S(1)}, u32[]{:S(2)}, u32[]{:S(2)}) collective-permute-start(bf16[3,64,128]{2,1,0:T(8,128)(2,1)S(1)} %get-tuple-element.38), channel_id=1, source_target_pairs={{0,16},{16,32},{32,48},{48,64},{64,80},{80,96},{96,112},{112,128},... | collective-permute-start | bytes 147464 | tf_op jit(solution)/shard_map/ppermute | solution.py:244
  56.6 2.9 %collective-permute-start.4 = (bf16[3,64,128]{2,1,0:T(8,128)(2,1)S(1)}, bf16[3,64,128]{2,1,0:T(8,128)(2,1)S(1)}, u32[]{:S(2)}, u32[]{:S(2)}) collective-permute-start(bf16[3,64,128]{2,1,0:T(8,128)(2,1)S(1)} %get-tuple-element.40), channel_id=1, source_target_pairs={{16,0},{32,16},{48,32},{64,48},{80,64},{96,80},{112,96},{128,112},... | collective-permute-start | bytes 147464 | tf_op jit(solution)/shard_map/ppermute | solution.py:245
  59.5 0.4 collective-permute-done.3.refs_0_
  59.9 4.3 %collective-permute-done.4.refs_2_ = bf16[3,64,128]{2,1,0:T(8,128)(2,1)S(1)} collective-permute-done((bf16[3,64,128]{2,1,0:T(8,128)(2,1)S(1)}, bf16[3,64,128]{2,1,0:T(8,128)(2,1)S(1)}, u32[]{:S(2)}, u32[]{:S(2)}) %collective-permute-start.4) | collective-permute-done | bytes 49184 | tf_op jit(solution)/shard_map/ppermute | solution.py:245
  64.1 0.0 copy-done.3
  64.1 0.5 shard_map.98
  64.7 13.5 %all_to_all.21.refs_0_ = bf16[16,64,256]{2,1,0:T(8,128)(2,1)S(1)} all-to-all(bf16[16,64,256]{2,1,0:T(8,128)(2,1)S(1)} %bitcast.15), channel_id=1, replica_groups=mesh['space'=32,'tensor'=16] {'tensor'}, dimensions={0} | all-to-all | bytes 1048576 | tf_op jit(solution)/shard_map/all_to_all | solution.py:262
  78.2 1.4 %shard_map.99 = bf16[8,2,64,256]{3,2,1,0:T(8,128)(2,1)S(1)} custom-call(bf16[16,64,256]{2,1,0:T(8,128)(2,1)S(1)} %all_to_all.21.refs_0_, f32[2,1024]{1,0:T(2,128)S(1)} %copy-done.4, f32[2,1024]{1,0:T(2,128)S(1)} %copy-done.5, bf16[2,1024,256]{2,1,0:T(8,128)(2,1)S(1)} %copy-done.1, bf16[2,256,1024]{2,1,0:T(8,128)(2,1)S(1)} %copy-done, ...), custom_call_target="tpu_custom_call" | custom-call | tf_op jit(solution)/shard_map/pallas_call | solution.py:19
  79.5 13.5 %all_to_all.22 = bf16[16,64,256]{2,1,0:T(8,128)(2,1)S(1)} all-to-all(bf16[16,64,256]{2,1,0:T(8,128)(2,1)S(1)} %bitcast.12), channel_id=1, replica_groups=mesh['space'=32,'tensor'=16] {'tensor'}, dimensions={0} | all-to-all | bytes 1048576 | tf_op jit(solution)/shard_map/all_to_all | solution.py:279
  93.0 0.7 shard_map.100
Async XLA Ops:
  0.0 15.3 %collective-permute-start.1 = (bf16[4,64,128]{2,1,0:T(8,128)(2,1)}, bf16[4,64,128]{2,1,0:T(8,128)(2,1)S(1)}, u32[]{:S(2)}, u32[]{:S(2)}) collective-permute-start(bf16[4,64,128]{2,1,0:T(8,128)(2,1)} %bitcast.16), channel_id=1, source_target_pairs={{0,16},{16,32},{32,48},{48,64},{64,80},{80,96},{96,112},{112,128},... | collective-permute-start | bytes 196616 | tf_op jit(solution)/shard_map/ppermute | solution.py:244
  6.1 10.9 %collective-permute-start = (bf16[4,64,128]{2,1,0:T(8,128)(2,1)}, bf16[4,64,128]{2,1,0:T(8,128)(2,1)S(1)}, u32[]{:S(2)}, u32[]{:S(2)}) collective-permute-start(bf16[4,64,128]{2,1,0:T(8,128)(2,1)} %bitcast.17), channel_id=1, source_target_pairs={{16,0},{32,16},{48,32},{64,48},{80,64},{96,80},{112,96},{128,112},... | collective-permute-start | bytes 196616 | tf_op jit(solution)/shard_map/ppermute | solution.py:245
  18.3 15.4 %all-to-all-start = ((bf16[16,64,256]{2,1,0:T(8,128)(2,1)}), bf16[16,64,256]{2,1,0:T(8,128)(2,1)}, u32[]{:S(2)}, u32[]{:S(2)}) async-start(bf16[16,64,256]{2,1,0:T(8,128)(2,1)} %bitcast.3), calls=%async_computation | async-start | bytes 1048576 | tf_op jit(solution)/shard_map/all_to_all | solution.py:262
  22.8 10.9 %copy-start.1 = (bf16[2,1024,256]{2,1,0:T(8,128)(2,1)S(1)}, bf16[2,1024,256]{2,1,0:T(8,128)(2,1)}, u32[]{:S(2)}) copy-start(bf16[2,1024,256]{2,1,0:T(8,128)(2,1)} %refs_3_.3) | copy-start | bytes 3145732
  22.8 10.9 %copy-start.4 = (f32[2,1024]{1,0:T(2,128)S(1)}, f32[2,1024]{1,0:T(2,128)}, u32[]{:S(2)}) copy-start(f32[2,1024]{1,0:T(2,128)} %refs_1_.3) | copy-start | bytes 24580
  22.8 10.9 %copy-start.5 = (f32[2,1024]{1,0:T(2,128)S(1)}, f32[2,1024]{1,0:T(2,128)}, u32[]{:S(2)}) copy-start(f32[2,1024]{1,0:T(2,128)} %refs_2_.5) | copy-start | bytes 24580
  22.8 10.9 %copy-start.6 = (f32[2,256]{1,0:T(2,128)S(1)}, f32[2,256]{1,0:T(2,128)}, u32[]{:S(2)}) copy-start(f32[2,256]{1,0:T(2,128)} %refs_5_.1) | copy-start | bytes 6148
  26.0 9.6 %collective-permute-start.2 = (bf16[2,2056,256]{2,1,0:T(8,128)(2,1)}, bf16[2,2056,256]{2,1,0:T(8,128)(2,1)S(1)}, u32[]{:S(2)}, u32[]{:S(2)}) collective-permute-start(bf16[2,2056,256]{2,1,0:T(8,128)(2,1)} %shard_map.95), channel_id=1, source_target_pairs={{0,1},{1,0},{2,3},{3,2},{4,5},{5,4},{6,7},{7,6},{8,9},{9,8},{10,11... | collective-permute-start | bytes 6316040 | tf_op jit(solution)/shard_map/ppermute | solution.py:258
  29.0 1.2 %copy-start.2 = (f32[49,64,128]{2,1,0:T(8,128)}, f32[49,64,128]{2,1,0:T(8,128)S(1)}, u32[]{:S(2)}) copy-start(f32[49,64,128]{2,1,0:T(8,128)S(1)} %get-tuple-element.41.refs_3_) | copy-start | bytes 4816900
  33.7 1.9 %copy-start = (bf16[2,256,1024]{2,1,0:T(8,128)(2,1)S(1)}, bf16[2,256,1024]{2,1,0:T(8,128)(2,1)}, u32[]{:S(2)}) copy-start(bf16[2,256,1024]{2,1,0:T(8,128)(2,1)} %refs_4_.3) | copy-start | bytes 3145732
  35.7 28.5 %copy-start.3 = (f32[49,64,128]{2,1,0:T(8,128)S(1)}, f32[49,64,128]{2,1,0:T(8,128)}, u32[]{:S(2)}) copy-start(f32[49,64,128]{2,1,0:T(8,128)} %copy-done.2) | copy-start | bytes 4816900
  50.2 9.6 %collective-permute-start.3 = (bf16[3,64,128]{2,1,0:T(8,128)(2,1)S(1)}, bf16[3,64,128]{2,1,0:T(8,128)(2,1)S(1)}, u32[]{:S(2)}, u32[]{:S(2)}) collective-permute-start(bf16[3,64,128]{2,1,0:T(8,128)(2,1)S(1)} %get-tuple-element.38), channel_id=1, source_target_pairs={{0,16},{16,32},{32,48},{48,64},{64,80},{80,96},{96,112},{112,128},... | collective-permute-start | bytes 147464 | tf_op jit(solution)/shard_map/ppermute | solution.py:244
  56.6 7.5 %collective-permute-start.4 = (bf16[3,64,128]{2,1,0:T(8,128)(2,1)S(1)}, bf16[3,64,128]{2,1,0:T(8,128)(2,1)S(1)}, u32[]{:S(2)}, u32[]{:S(2)}) collective-permute-start(bf16[3,64,128]{2,1,0:T(8,128)(2,1)S(1)} %get-tuple-element.40), channel_id=1, source_target_pairs={{16,0},{32,16},{48,32},{64,48},{80,64},{96,80},{112,96},{128,112},... | collective-permute-start | bytes 147464 | tf_op jit(solution)/shard_map/ppermute | solution.py:245

commit v7 on v6

--- a/solution.py
+++ b/solution.py
@@ -178,24 +178,6 @@
     return slice(D + units * part, D + units * (part + 1))
 
 
-def own_kernel(block, x_ref, gain_ref, bias_ref, unit_bias_ref, expand_ref, normed_ref, own_ref):
-    normed = normalized(block, x_ref, gain_ref, bias_ref)
-    normed_ref[...] = normed
-    own_ref[...] = hidden_of(normed, expand_ref[block], unit_bias_ref[block : block + 1, :])
-
-
-def rest_kernel(block, normed_ref, own_ref, reduce_ref, pack_ref, out_ref):
-    own = own_ref[...]
-    units = own.shape[1]
-    other = hidden_of(normed_ref[...], pack_ref[block, :D, :], bias_of(pack_ref[block, 2 * D :, :]))
-    for part in range(D // units):
-        own_weights = reduce_ref[block, :, units * part : units * (part + 1)]
-        total = jnp.dot(own, own_weights, preferred_element_type=jnp.float32) + jnp.dot(
-            other, pack_ref[block, rows_of(part, units), :], preferred_element_type=jnp.float32
-        )
-        scatter(part, total, out_ref)
-
-
 def mlp_kernel(block, x_ref, gain_ref, bias_ref, expand_ref, reduce_ref, unit_bias_ref, pack_ref, out_ref):
     normed = normalized(block, x_ref, gain_ref, bias_ref)
     own = hidden_of(normed, expand_ref[block], unit_bias_ref[block : block + 1, :])
@@ -245,37 +227,27 @@
         after = lax.ppermute(first, "space", up)
         if block == 0:
             wide, affine, stream, taps, layer_scale, b_reduce = entered(stream, taps, layer_scale, b_reduce)
+            layer_scale, own_bias = lax.optimization_barrier((layer_scale, b_expand))
+            pack = lax.ppermute(packed(w_expand, w_reduce, own_bias), "tensor", sibling)
         else:
-            wide, affine = next_wide, next_affine
+            stream, next_scale = lax.optimization_barrier((stream, layer_scale))
+            wide, affine = call(
+                lambda *refs: spread(1, *refs), spread_shapes(share, width), taps, next_scale, b_reduce
+            )
         edges = (after, before) if block == 0 else (before, after)
         filtered = call(
             lambda *refs: conv_kernel(block > 0, *refs),
             jax.ShapeDtypeStruct((copies, CORES, share, half), jnp.bfloat16),
             edges[0], stream, edges[1], wide,
+            cost=pl.CostEstimate(flops=10**11, transcendentals=0, bytes_accessed=10**6) if block == 0 else None,
         )
-        if block == 0:
-            filtered, own_bias, next_scale = lax.optimization_barrier((filtered, b_expand, layer_scale))
-            pack = lax.ppermute(packed(w_expand, w_reduce, own_bias), "tensor", sibling)
-            next_wide, next_affine = call(
-                lambda *refs: spread(1, *refs), spread_shapes(share, width), taps, next_scale, b_reduce
-            )
         filtered = lax.all_to_all(filtered.reshape(members, share, half), "tensor", 0, 0, tiled=True)
         out = jax.ShapeDtypeStruct((copies, CORES, share, half), jnp.bfloat16)
-        if block == 0:
-            filtered, next_wide, next_affine = lax.optimization_barrier((filtered, next_wide, next_affine))
-            normed, own = call(
-                lambda *refs: own_kernel(block, *refs),
-                (jax.ShapeDtypeStruct((half, D), jnp.bfloat16), jax.ShapeDtypeStruct((half, units), jnp.bfloat16)),
-                filtered, norm_gain, norm_bias, b_expand, w_expand,
-                cost=pl.CostEstimate(flops=10**11, transcendentals=0, bytes_accessed=10**6),
-            )
-            partial = call(lambda *refs: rest_kernel(block, *refs), out, normed, own, w_reduce, pack)
-        else:
-            partial = call(
-                lambda *refs: mlp_kernel(block, *refs),
-                out,
-                filtered, norm_gain, norm_bias, w_expand, w_reduce, b_expand, pack,
-            )
+        partial = call(
+            lambda *refs: mlp_kernel(block, *refs),
+            out,
+            filtered, norm_gain, norm_bias, w_expand, w_reduce, b_expand, pack,
+        )
         partial = lax.all_to_all(partial.reshape(members, share, half), "tensor", 0, 0, tiled=True)
         partial = partial.reshape(copies, CORES, share, half)
         whole = jax.ShapeDtypeStruct((height, share, width), jnp.bfloat16)

time: 94.6 us -> 91.9 us (0.971)
  blocking collectives: 40.5 us -> 56.7 us
  waiting for transfers between devices: 10.1 us -> 1.33 us
  starting transfers between devices: 29.6 us -> 24.4 us
  Pallas kernels: 12.2 us -> 8.5 us
  local copies, waits for them, and re-layouts: 1.18 us -> 0.03 us
    all_to_all x1 -> x2, blocking collectives: 13.5 us -> 29.7 us  [per_device(): lax.all_to_all(filtered.reshape(members, share, half), 'tensor', 0, 0, ti...]
    ppermute x2, waiting for transfers between devices: 5.93 us -> 1.32 us  [per_device(): after = lax.ppermute(first, 'space', up)]
    all_to_all x1 -> x0, starting transfers between devices: 4.46 us -> none  [per_device(): lax.all_to_all(filtered.reshape(members, share, half), 'tensor', 0, 0, ti...]
    all_to_all x1 -> x0, waiting for transfers between devices: 3.57 us -> none  [per_device(): lax.all_to_all(filtered.reshape(members, share, half), 'tensor', 0, 0, ti...]
    ppermute x2, starting transfers between devices: 12.4 us -> 9.55 us  [per_device(): before = lax.ppermute(last, 'space', down)]
    ppermute x2, starting transfers between devices: 10.4 us -> 12.9 us  [per_device(): after = lax.ppermute(first, 'space', up)]
    pallas_call x8 -> x7, Pallas kernels: 7.57 us -> 5.26 us  [call(): pl.pallas_call(body, out_shape=outs, in_specs=[VMEM] * len(args), out_spe...]
    pallas_call x1, Pallas kernels: 3.17 us -> 1.76 us  [packed(): pl.pallas_call(pack_kernel, out_shape=jax.ShapeDtypeStruct((BLOCKS, 2 * D...]
  transfers between devices with their start and end apart: 6 -> 5, of which waited for: 5 -> 1; matrix products, arithmetic and copies ran while one was open for 0% -> 0% of each run, Pallas kernels for 8% -> 5%
where the time goes in v7:
time: 91.9 us; the launch traced here: 91.1 us
  blocking collectives  56.7 us (62%)
  starting transfers between devices  24.4 us (27%)
  Pallas kernels  8.5 us (9%)
  waiting for transfers between devices  1.33 us (1%)
    all_to_all x2, blocking collectives, per_device(): lax.all_to_all(filtered.reshape(members, share, half), 'tensor', 0, 0, ti...  29.7 us
    all_to_all x2, blocking collectives, per_device(): lax.all_to_all(partial.reshape(members, share, half), 'tensor', 0, 0, til...  27 us
    ppermute x2, starting transfers between devices, per_device(): after = lax.ppermute(first, 'space', up)  12.9 us
    ppermute x2, starting transfers between devices, per_device(): before = lax.ppermute(last, 'space', down)  9.55 us
    pallas_call x7, Pallas kernels, call(): pl.pallas_call(body, out_shape=outs, in_specs=[VMEM] * len(args), out_spe...  5.26 us
    ppermute x1, starting transfers between devices, per_device(): pack = lax.ppermute(packed(w_expand, w_reduce, own_bias), 'tensor', sibling)  1.92 us
  transfers between devices with their start and end apart: 5, of which 1 were waited for; matrix products, arithmetic and copies ran while one was open for 0% of the time, Pallas kernels for 5%

profile of v7, /device:TPU:56, one launch (start us, length us, event | category | flops | bytes accessed | tf_op | source)
XLA Modules:
  0.0 91.1 jit_solution(15651331571551146116)
XLA Ops:
  0.0 6.1 %collective-permute-start.1 = (bf16[4,64,128]{2,1,0:T(8,128)(2,1)}, bf16[4,64,128]{2,1,0:T(8,128)(2,1)S(1)}, u32[]{:S(2)}, u32[]{:S(2)}) collective-permute-start(bf16[4,64,128]{2,1,0:T(8,128)(2,1)} %bitcast.17), channel_id=1, source_target_pairs={{0,16},{16,32},{32,48},{48,64},{64,80},{80,96},{96,112},{112,128},... | collective-permute-start | bytes 196616 | tf_op jit(solution)/shard_map/ppermute | solution.py:226
  6.1 7.6 %collective-permute-start = (bf16[4,64,128]{2,1,0:T(8,128)(2,1)}, bf16[4,64,128]{2,1,0:T(8,128)(2,1)S(1)}, u32[]{:S(2)}, u32[]{:S(2)}) collective-permute-start(bf16[4,64,128]{2,1,0:T(8,128)(2,1)} %bitcast.18), channel_id=1, source_target_pairs={{16,0},{32,16},{48,32},{64,48},{80,64},{96,80},{112,96},{128,112},... | collective-permute-start | bytes 196616 | tf_op jit(solution)/shard_map/ppermute | solution.py:227
  13.6 1.5 %shard_map.91 = (f32[49,64,128]{2,1,0:T(8,128)S(1)}, f32[2,64,128]{2,1,0:T(8,128)S(1)}, bf16[4,64,128]{2,1,0:T(8,128)(2,1)S(1)}, bf16[49,2,64]{2,1,0:T(2,128)(2,...) custom-call(bf16[4,64,128]{2,1,0:T(8,128)(2,1)} %bitcast.19, bf16[49,2,64]{2,1,0:T(2,128)(2,1)} %bitcast.20, ...), custom_call_target="tpu_custom_call" | custom-call | tf_op jit(solution)/shard_map/pallas_call | solution.py:57
  15.1 1.8 %shard_map.93 = bf16[2,2056,256]{2,1,0:T(8,128)(2,1)S(1)} custom-call(bf16[2,1024,256]{2,1,0:T(8,128)(2,1)} %refs_3_.3, bf16[2,256,1024]{2,1,0:T(8,128)(2,1)} %refs_4_.3, f32[2,256]{1,0:T(2,128)} %refs_5_.3), custom_call_target="tpu_custom_call" | custom-call | tf_op jit(solution)/shard_map/pallas_call | solution.py:99
  16.9 1.9 %collective-permute-start.2 = (bf16[2,2056,256]{2,1,0:T(8,128)(2,1)S(1)}, bf16[2,2056,256]{2,1,0:T(8,128)(2,1)S(1)}, u32[]{:S(2)}, u32[]{:S(2)}) collective-permute-start(bf16[2,2056,256]{2,1,0:T(8,128)(2,1)S(1)} %shard_map.93), channel_id=1, source_target_pairs={{0,1},{1,0},{2,3},{3,2},{4,5},{5,4},{6,7},{7,6},{8,9},{9,8},{10,11... | collective-permute-start | bytes 6316040 | tf_op jit(solution)/shard_map/ppermute | solution.py:231
  18.8 0.0 collective-permute-done.1.refs_2_
  18.8 0.0 collective-permute-done.refs_0_
  18.9 0.0 copy-start
  18.9 0.0 copy-start.1
  18.9 0.0 copy-start.2
  18.9 0.0 copy-start.3
  18.9 0.0 copy-start.4
  18.9 0.5 shard_map.92
  19.4 16.2 %all_to_all.20.refs_0_ = bf16[16,64,256]{2,1,0:T(8,128)(2,1)S(1)} all-to-all(bf16[16,64,256]{2,1,0:T(8,128)(2,1)S(1)} %bitcast.16), channel_id=1, replica_groups=mesh['space'=32,'tensor'=16] {'tensor'}, dimensions={0} | all-to-all | bytes 1048576 | tf_op jit(solution)/shard_map/all_to_all | solution.py:244
  35.7 0.0 collective-permute-done.2.refs_6_
  35.7 0.0 copy-done
  35.7 0.0 copy-done.1
  35.7 0.0 copy-done.2
  35.7 0.0 copy-done.3
  35.7 0.0 copy-done.4
  35.7 1.4 %shard_map.94 = bf16[8,2,64,256]{3,2,1,0:T(8,128)(2,1)S(1)} custom-call(bf16[16,64,256]{2,1,0:T(8,128)(2,1)S(1)} %all_to_all.20.refs_0_, f32[2,1024]{1,0:T(2,128)S(1)} %copy-done.2, f32[2,1024]{1,0:T(2,128)S(1)} %copy-done.3, bf16[2,1024,256]{2,1,0:T(8,128)(2,1)S(1)} %copy-done, bf16[2,256,1024]{2,1,0:T(8,128)(2,1)S(1)} %copy-done.1, ...), custom_call_target="tpu_custom_call" | custom-call | tf_op jit(solution)/shard_map/pallas_call | solution.py:19
  37.1 13.5 %all_to_all.21 = bf16[16,64,256]{2,1,0:T(8,128)(2,1)S(1)} all-to-all(bf16[16,64,256]{2,1,0:T(8,128)(2,1)S(1)} %bitcast.12), channel_id=1, replica_groups=mesh['space'=32,'tensor'=16] {'tensor'}, dimensions={0} | all-to-all | bytes 1048576 | tf_op jit(solution)/shard_map/all_to_all | solution.py:251
  50.5 0.1 shard_map.95
  50.6 3.5 %collective-permute-start.3 = (bf16[3,64,128]{2,1,0:T(8,128)(2,1)S(1)}, bf16[3,64,128]{2,1,0:T(8,128)(2,1)S(1)}, u32[]{:S(2)}, u32[]{:S(2)}) collective-permute-start(bf16[3,64,128]{2,1,0:T(8,128)(2,1)S(1)} %get-tuple-element.25), channel_id=1, source_target_pairs={{0,16},{16,32},{32,48},{48,64},{64,80},{80,96},{96,112},{112,128},... | collective-permute-start | bytes 147464 | tf_op jit(solution)/shard_map/ppermute | solution.py:226
  54.1 5.4 %collective-permute-start.4 = (bf16[3,64,128]{2,1,0:T(8,128)(2,1)S(1)}, bf16[3,64,128]{2,1,0:T(8,128)(2,1)S(1)}, u32[]{:S(2)}, u32[]{:S(2)}) collective-permute-start(bf16[3,64,128]{2,1,0:T(8,128)(2,1)S(1)} %get-tuple-element.29), channel_id=1, source_target_pairs={{16,0},{32,16},{48,32},{64,48},{80,64},{96,80},{112,96},{128,112},... | collective-permute-start | bytes 147464 | tf_op jit(solution)/shard_map/ppermute | solution.py:227
  59.5 0.7 shard_map.96
  60.2 0.0 collective-permute-done.3.refs_0_
  60.2 1.3 %collective-permute-done.4.refs_2_ = bf16[3,64,128]{2,1,0:T(8,128)(2,1)S(1)} collective-permute-done((bf16[3,64,128]{2,1,0:T(8,128)(2,1)S(1)}, bf16[3,64,128]{2,1,0:T(8,128)(2,1)S(1)}, u32[]{:S(2)}, u32[]{:S(2)}) %collective-permute-start.4) | collective-permute-done | bytes 49184 | tf_op jit(solution)/shard_map/ppermute | solution.py:227
  61.5 0.5 shard_map.97
  62.1 13.5 %all_to_all.22.refs_0_ = bf16[16,64,256]{2,1,0:T(8,128)(2,1)S(1)} all-to-all(bf16[16,64,256]{2,1,0:T(8,128)(2,1)S(1)} %bitcast.15), channel_id=1, replica_groups=mesh['space'=32,'tensor'=16] {'tensor'}, dimensions={0} | all-to-all | bytes 1048576 | tf_op jit(solution)/shard_map/all_to_all | solution.py:244
  75.5 1.4 %shard_map.98 = bf16[8,2,64,256]{3,2,1,0:T(8,128)(2,1)S(1)} custom-call(bf16[16,64,256]{2,1,0:T(8,128)(2,1)S(1)} %all_to_all.22.refs_0_, f32[2,1024]{1,0:T(2,128)S(1)} %copy-done.2, f32[2,1024]{1,0:T(2,128)S(1)} %copy-done.3, bf16[2,1024,256]{2,1,0:T(8,128)(2,1)S(1)} %copy-done, bf16[2,256,1024]{2,1,0:T(8,128)(2,1)S(1)} %copy-done.1, ...), custom_call_target="tpu_custom_call" | custom-call | tf_op jit(solution)/shard_map/pallas_call | solution.py:19
  76.9 13.5 %all_to_all.23 = bf16[16,64,256]{2,1,0:T(8,128)(2,1)S(1)} all-to-all(bf16[16,64,256]{2,1,0:T(8,128)(2,1)S(1)} %bitcast.11), channel_id=1, replica_groups=mesh['space'=32,'tensor'=16] {'tensor'}, dimensions={0} | all-to-all | bytes 1048576 | tf_op jit(solution)/shard_map/all_to_all | solution.py:251
  90.4 0.7 shard_map.99
Async XLA Ops:
  0.0 18.8 %collective-permute-start.1 = (bf16[4,64,128]{2,1,0:T(8,128)(2,1)}, bf16[4,64,128]{2,1,0:T(8,128)(2,1)S(1)}, u32[]{:S(2)}, u32[]{:S(2)}) collective-permute-start(bf16[4,64,128]{2,1,0:T(8,128)(2,1)} %bitcast.17), channel_id=1, source_target_pairs={{0,16},{16,32},{32,48},{48,64},{64,80},{80,96},{96,112},{112,128},... | collective-permute-start | bytes 196616 | tf_op jit(solution)/shard_map/ppermute | solution.py:226
  6.1 12.8 %collective-permute-start = (bf16[4,64,128]{2,1,0:T(8,128)(2,1)}, bf16[4,64,128]{2,1,0:T(8,128)(2,1)S(1)}, u32[]{:S(2)}, u32[]{:S(2)}) collective-permute-start(bf16[4,64,128]{2,1,0:T(8,128)(2,1)} %bitcast.18), channel_id=1, source_target_pairs={{16,0},{32,16},{48,32},{64,48},{80,64},{96,80},{112,96},{128,112},... | collective-permute-start | bytes 196616 | tf_op jit(solution)/shard_map/ppermute | solution.py:227
  16.9 18.8 %collective-permute-start.2 = (bf16[2,2056,256]{2,1,0:T(8,128)(2,1)S(1)}, bf16[2,2056,256]{2,1,0:T(8,128)(2,1)S(1)}, u32[]{:S(2)}, u32[]{:S(2)}) collective-permute-start(bf16[2,2056,256]{2,1,0:T(8,128)(2,1)S(1)} %shard_map.93), channel_id=1, source_target_pairs={{0,1},{1,0},{2,3},{3,2},{4,5},{5,4},{6,7},{7,6},{8,9},{9,8},{10,11... | collective-permute-start | bytes 6316040 | tf_op jit(solution)/shard_map/ppermute | solution.py:231
  18.9 16.8 %copy-start = (bf16[2,1024,256]{2,1,0:T(8,128)(2,1)S(1)}, bf16[2,1024,256]{2,1,0:T(8,128)(2,1)}, u32[]{:S(2)}) copy-start(bf16[2,1024,256]{2,1,0:T(8,128)(2,1)} %refs_3_.3) | copy-start | bytes 3145732
  18.9 16.8 %copy-start.1 = (bf16[2,256,1024]{2,1,0:T(8,128)(2,1)S(1)}, bf16[2,256,1024]{2,1,0:T(8,128)(2,1)}, u32[]{:S(2)}) copy-start(bf16[2,256,1024]{2,1,0:T(8,128)(2,1)} %refs_4_.3) | copy-start | bytes 3145732
  18.9 16.8 %copy-start.2 = (f32[2,1024]{1,0:T(2,128)S(1)}, f32[2,1024]{1,0:T(2,128)}, u32[]{:S(2)}) copy-start(f32[2,1024]{1,0:T(2,128)} %refs_1_.3) | copy-start | bytes 24580
  18.9 16.8 %copy-start.3 = (f32[2,1024]{1,0:T(2,128)S(1)}, f32[2,1024]{1,0:T(2,128)}, u32[]{:S(2)}) copy-start(f32[2,1024]{1,0:T(2,128)} %refs_2_.3) | copy-start | bytes 24580
  18.9 16.8 %copy-start.4 = (f32[2,256]{1,0:T(2,128)S(1)}, f32[2,256]{1,0:T(2,128)}, u32[]{:S(2)}) copy-start(f32[2,256]{1,0:T(2,128)} %refs_5_.3) | copy-start | bytes 6148
  50.6 9.6 %collective-permute-start.3 = (bf16[3,64,128]{2,1,0:T(8,128)(2,1)S(1)}, bf16[3,64,128]{2,1,0:T(8,128)(2,1)S(1)}, u32[]{:S(2)}, u32[]{:S(2)}) collective-permute-start(bf16[3,64,128]{2,1,0:T(8,128)(2,1)S(1)} %get-tuple-element.25), channel_id=1, source_target_pairs={{0,16},{16,32},{32,48},{48,64},{64,80},{80,96},{96,112},{112,128},... | collective-permute-start | bytes 147464 | tf_op jit(solution)/shard_map/ppermute | solution.py:226
  54.1 7.4 %collective-permute-start.4 = (bf16[3,64,128]{2,1,0:T(8,128)(2,1)S(1)}, bf16[3,64,128]{2,1,0:T(8,128)(2,1)S(1)}, u32[]{:S(2)}, u32[]{:S(2)}) collective-permute-start(bf16[3,64,128]{2,1,0:T(8,128)(2,1)S(1)} %get-tuple-element.29), channel_id=1, source_target_pairs={{16,0},{32,16},{48,32},{64,48},{80,64},{96,80},{112,96},{128,112},... | collective-permute-start | bytes 147464 | tf_op jit(solution)/shard_map/ppermute | solution.py:227

commit v8 on v7

--- a/solution.py
+++ b/solution.py
@@ -37,50 +37,26 @@
             affine_ref[at - wide_ref.shape[0]] = col
 
 
-def enter_kernel(band_ref, taps_in, scale_in, shift_in, wide_ref, affine_ref, rows_ref, taps_ref, scale_ref, shift_ref, sems):
-    moves = ((taps_in, taps_ref), (scale_in, scale_ref), (shift_in, shift_ref), (band_ref, rows_ref))
+def enter_kernel(
+    band_in, taps_in, scale_in, shift_in, expand_in, reduce_in, bias_in,
+    wide_ref, affine_ref, rows_ref, taps_ref, scale_ref, shift_ref, pack_ref, held_ref, sems,
+):
+    units = pack_ref.shape[2]
+    moves = [(taps_in, taps_ref), (scale_in, scale_ref), (shift_in, shift_ref), (bias_in, held_ref)]
+    small = len(moves)
+    for block in range(BLOCKS):
+        ref = pack_ref.at[block]
+        moves.append((expand_in.at[block], ref.at[pl.ds(0, D)]))
+        for part in range(D // units):
+            columns = pl.ds(units * part, units)
+            moves.append((reduce_in.at[block, :, columns], ref.at[pl.ds(D + units * part, units)]))
+    moves.append((band_in, rows_ref))
     copies = [pltpu.make_async_copy(src, dst, sems.at[i]) for i, (src, dst) in enumerate(moves)]
     for copy in copies:
         copy.start()
-    for copy in copies[:3]:
+    for copy in copies[:small]:
         copy.wait()
     spread(0, taps_ref, scale_ref, shift_ref, wide_ref, affine_ref)
-    copies[3].wait()
-
-
-def spread_shapes(share, width):
-    return tuple(jax.ShapeDtypeStruct((count, share, width), jnp.float32) for count in (TAPS * TAPS, 2))
-
-
-def entered(band, taps, scale, shift):
-    inputs = (band, taps, scale, shift)
-    return pl.pallas_call(
-        enter_kernel,
-        out_shape=[
-            *spread_shapes(*band.shape[1:]),
-            *[jax.ShapeDtypeStruct(array.shape, array.dtype) for array in inputs],
-        ],
-        in_specs=[pl.BlockSpec(memory_space=pltpu.HBM)] * 4,
-        out_specs=[VMEM] * 6,
-        scratch_shapes=[pltpu.SemaphoreType.DMA((4,))],
-        compiler_params=pltpu.CompilerParams(vmem_limit_bytes=16 << 20),
-    )(*[pltpu.with_memory_space_constraint(array, pltpu.HBM) for array in inputs])
-
-
-def pack_kernel(expand_ref, reduce_ref, bias_ref, pack_ref, held_ref, sems):
-    units = pack_ref.shape[2]
-    moves = []
-    for block in range(BLOCKS):
-        ref = pack_ref.at[block]
-        moves.append((expand_ref.at[block], ref.at[pl.ds(0, D)]))
-        for part in range(D // units):
-            columns = pl.ds(units * part, units)
-            moves.append((reduce_ref.at[block, :, columns], ref.at[pl.ds(D + units * part, units)]))
-    moves.append((bias_ref, held_ref))
-    copies = [pltpu.make_async_copy(src, dst, sems.at[i]) for i, (src, dst) in enumerate(moves)]
-    for copy in reversed(copies):
-        copy.start()
-    copies.pop().wait()
     for block in range(BLOCKS):
         rest = held_ref[block : block + 1, :]
         pieces = []
@@ -89,24 +65,33 @@
             rest = rest - pieces[-1].astype(jnp.float32)
         pieces = [piece.astype(jnp.float32) for piece in pieces] + [jnp.zeros((5, units), jnp.float32)]
         pack_ref[block, 2 * D :, :] = jnp.concatenate(pieces, axis=0).astype(jnp.bfloat16)
-    for copy in copies:
+    for copy in copies[small:]:
         copy.wait()
 
 
-def packed(w_expand, w_reduce, hidden_bias):
+def spread_shapes(share, width):
+    return tuple(jax.ShapeDtypeStruct((count, share, width), jnp.float32) for count in (TAPS * TAPS, 2))
+
+
+def entered(band, taps, scale, shift, w_expand, w_reduce, b_expand):
     units = w_expand.shape[2]
-    raw = pl.BlockSpec(memory_space=pltpu.HBM)
+    inputs = (band, taps, scale, shift, w_expand, w_reduce, b_expand)
+    outs = [
+        *spread_shapes(*band.shape[1:]),
+        *[jax.ShapeDtypeStruct(array.shape, array.dtype) for array in inputs[:4]],
+        jax.ShapeDtypeStruct((BLOCKS, 2 * D + 8, units), jnp.bfloat16),
+    ]
     return pl.pallas_call(
-        pack_kernel,
-        out_shape=jax.ShapeDtypeStruct((BLOCKS, 2 * D + 8, units), jnp.bfloat16),
-        in_specs=[raw, raw, raw],
-        out_specs=VMEM,
+        enter_kernel,
+        out_shape=outs,
+        in_specs=[pl.BlockSpec(memory_space=pltpu.HBM)] * len(inputs),
+        out_specs=[VMEM] * len(outs),
         scratch_shapes=[
-            pltpu.VMEM(hidden_bias.shape, jnp.float32),
-            pltpu.SemaphoreType.DMA((1 + BLOCKS * (1 + D // units),)),
+            pltpu.VMEM(b_expand.shape, jnp.float32),
+            pltpu.SemaphoreType.DMA((5 + BLOCKS * (1 + D // units),)),
         ],
         compiler_params=pltpu.CompilerParams(vmem_limit_bytes=16 << 20),
-    )(*[pltpu.with_memory_space_constraint(array, pltpu.HBM) for array in (w_expand, w_reduce, hidden_bias)])
+    )(*[pltpu.with_memory_space_constraint(array, pltpu.HBM) for array in inputs])
 
 
 def conv_kernel(before_leads, before_ref, rows_ref, after_ref, wide_ref, out_ref):
@@ -226,9 +211,10 @@
         before = lax.ppermute(last, "space", down)
         after = lax.ppermute(first, "space", up)
         if block == 0:
-            wide, affine, stream, taps, layer_scale, b_reduce = entered(stream, taps, layer_scale, b_reduce)
-            layer_scale, own_bias = lax.optimization_barrier((layer_scale, b_expand))
-            pack = lax.ppermute(packed(w_expand, w_reduce, own_bias), "tensor", sibling)
+            wide, affine, stream, taps, layer_scale, b_reduce, pack = entered(
+                stream, taps, layer_scale, b_reduce, w_expand, w_reduce, b_expand
+            )
+            pack = lax.ppermute(pack, "tensor", sibling)
         else:
             stream, next_scale = lax.optimization_barrier((stream, layer_scale))
             wide, affine = call(

time: 91.9 us -> 91.8 us (level)
  waiting for transfers between devices: 1.33 us -> 2.87 us
  Pallas kernels: 8.5 us -> 6.97 us
    ppermute x2, starting transfers between devices: 12.9 us -> 11.4 us  [per_device(): after = lax.ppermute(first, 'space', up)]
    ppermute x2, waiting for transfers between devices: 1.32 us -> 2.87 us  [per_device(): after = lax.ppermute(first, 'space', up)]
    ppermute x2, starting transfers between devices: 9.55 us -> 11.1 us  [per_device(): before = lax.ppermute(last, 'space', down)]
    pallas_call x2 -> x1, Pallas kernels: 3.24 us -> 1.71 us  [entered(): pl.pallas_call(enter_kernel, out_shape=outs, in_specs=[pl.BlockSpec(memor...]
  transfers between devices with their start and end apart: 5 -> 5, of which waited for: 1 -> 1; matrix products, arithmetic and copies ran while one was open for 0% -> 0% of each run, Pallas kernels for 5% -> 3%
where the time goes in v8:
time: 91.8 us; the launch traced here: 91.1 us
  blocking collectives  56.7 us (62%)
  starting transfers between devices  24.4 us (27%)
  Pallas kernels  6.97 us (8%)
  waiting for transfers between devices  2.87 us (3%)
    all_to_all x2, blocking collectives, per_device(): lax.all_to_all(filtered.reshape(members, share, half), 'tensor', 0, 0, ti...  29.7 us
    all_to_all x2, blocking collectives, per_device(): lax.all_to_all(partial.reshape(members, share, half), 'tensor', 0, 0, til...  27 us
    ppermute x2, starting transfers between devices, per_device(): after = lax.ppermute(first, 'space', up)  11.4 us
    ppermute x2, starting transfers between devices, per_device(): before = lax.ppermute(last, 'space', down)  11.1 us
    pallas_call x7, Pallas kernels, call(): pl.pallas_call(body, out_shape=outs, in_specs=[VMEM] * len(args), out_spe...  5.26 us
    ppermute x2, waiting for transfers between devices, per_device(): after = lax.ppermute(first, 'space', up)  2.87 us
    ppermute x1, starting transfers between devices, per_device(): pack = lax.ppermute(pack, 'tensor', sibling)  1.92 us
  transfers between devices with their start and end apart: 5, of which 1 were waited for; matrix products, arithmetic and copies ran while one was open for 0% of the time, Pallas kernels for 3%

profile of v8, /device:TPU:56, one launch (start us, length us, event | category | flops | bytes accessed | tf_op | source)
XLA Modules:
  0.0 91.1 jit_solution(16847421882149297160)
XLA Ops:
  0.0 6.1 %collective-permute-start.1 = (bf16[4,64,128]{2,1,0:T(8,128)(2,1)}, bf16[4,64,128]{2,1,0:T(8,128)(2,1)S(1)}, u32[]{:S(2)}, u32[]{:S(2)}) collective-permute-start(bf16[4,64,128]{2,1,0:T(8,128)(2,1)} %bitcast.17), channel_id=1, source_target_pairs={{0,16},{16,32},{32,48},{48,64},{64,80},{80,96},{96,112},{112,128},... | collective-permute-start | bytes 196616 | tf_op jit(solution)/shard_map/ppermute | solution.py:211
  6.1 7.6 %collective-permute-start = (bf16[4,64,128]{2,1,0:T(8,128)(2,1)}, bf16[4,64,128]{2,1,0:T(8,128)(2,1)S(1)}, u32[]{:S(2)}, u32[]{:S(2)}) collective-permute-start(bf16[4,64,128]{2,1,0:T(8,128)(2,1)} %bitcast.18), channel_id=1, source_target_pairs={{16,0},{32,16},{48,32},{64,48},{80,64},{96,80},{112,96},{128,112},... | collective-permute-start | bytes 196616 | tf_op jit(solution)/shard_map/ppermute | solution.py:212
  13.6 1.7 %shard_map.91 = (f32[49,64,128]{2,1,0:T(8,128)S(1)}, f32[2,64,128]{2,1,0:T(8,128)S(1)}, bf16[4,64,128]{2,1,0:T(8,128)(2,1)S(1)}, bf16[49,2,64]{2,1,0:T(2,128)(2,...) custom-call(bf16[4,64,128]{2,1,0:T(8,128)(2,1)} %bitcast.19, ...), custom_call_target="tpu_custom_call" | custom-call | tf_op jit(solution)/shard_map/pallas_call | solution.py:84
  15.4 1.9 %collective-permute-start.2 = (bf16[2,2056,256]{2,1,0:T(8,128)(2,1)S(1)}, bf16[2,2056,256]{2,1,0:T(8,128)(2,1)S(1)}, u32[]{:S(2)}, u32[]{:S(2)}) collective-permute-start(bf16[2,2056,256]{2,1,0:T(8,128)(2,1)S(1)} %get-tuple-element.21), channel_id=1, source_target_pairs={{0,1},{1,0},{2,3},{3,2},{4,5},{5,4},{6,7},{7,6},{8,9},{9,8},{10,11... | collective-permute-start | bytes 6316040 | tf_op jit(solution)/shard_map/ppermute | solution.py:217
  17.3 0.0 collective-permute-done.1.refs_2_
  17.3 0.0 collective-permute-done.refs_0_
  17.3 0.0 copy-start
  17.3 0.0 copy-start.1
  17.3 0.0 copy-start.2
  17.4 0.0 copy-start.3
  17.4 0.0 copy-start.4
  17.4 0.5 shard_map.92
  17.9 16.2 %all_to_all.20.refs_0_ = bf16[16,64,256]{2,1,0:T(8,128)(2,1)S(1)} all-to-all(bf16[16,64,256]{2,1,0:T(8,128)(2,1)S(1)} %bitcast.16), channel_id=1, replica_groups=mesh['space'=32,'tensor'=16] {'tensor'}, dimensions={0} | all-to-all | bytes 1048576 | tf_op jit(solution)/shard_map/all_to_all | solution.py:230
  34.1 0.0 collective-permute-done.2.refs_6_
  34.1 0.0 copy-done
  34.1 0.0 copy-done.1
  34.1 0.0 copy-done.2
  34.1 0.0 copy-done.3
  34.1 0.0 copy-done.4
  34.2 1.4 %shard_map.93 = bf16[8,2,64,256]{3,2,1,0:T(8,128)(2,1)S(1)} custom-call(bf16[16,64,256]{2,1,0:T(8,128)(2,1)S(1)} %all_to_all.20.refs_0_, f32[2,1024]{1,0:T(2,128)S(1)} %copy-done.2, f32[2,1024]{1,0:T(2,128)S(1)} %copy-done.3, bf16[2,1024,256]{2,1,0:T(8,128)(2,1)S(1)} %copy-done, bf16[2,256,1024]{2,1,0:T(8,128)(2,1)S(1)} %copy-done.1, ...), custom_call_target="tpu_custom_call" | custom-call | tf_op jit(solution)/shard_map/pallas_call | solution.py:19
  35.5 13.5 %all_to_all.21 = bf16[16,64,256]{2,1,0:T(8,128)(2,1)S(1)} all-to-all(bf16[16,64,256]{2,1,0:T(8,128)(2,1)S(1)} %bitcast.12), channel_id=1, replica_groups=mesh['space'=32,'tensor'=16] {'tensor'}, dimensions={0} | all-to-all | bytes 1048576 | tf_op jit(solution)/shard_map/all_to_all | solution.py:237
  49.0 0.1 shard_map.94
  49.1 5.0 %collective-permute-start.3 = (bf16[3,64,128]{2,1,0:T(8,128)(2,1)S(1)}, bf16[3,64,128]{2,1,0:T(8,128)(2,1)S(1)}, u32[]{:S(2)}, u32[]{:S(2)}) collective-permute-start(bf16[3,64,128]{2,1,0:T(8,128)(2,1)S(1)} %get-tuple-element.23), channel_id=1, source_target_pairs={{0,16},{16,32},{32,48},{48,64},{64,80},{80,96},{96,112},{112,128},... | collective-permute-start | bytes 147464 | tf_op jit(solution)/shard_map/ppermute | solution.py:211
  54.1 3.8 %collective-permute-start.4 = (bf16[3,64,128]{2,1,0:T(8,128)(2,1)S(1)}, bf16[3,64,128]{2,1,0:T(8,128)(2,1)S(1)}, u32[]{:S(2)}, u32[]{:S(2)}) collective-permute-start(bf16[3,64,128]{2,1,0:T(8,128)(2,1)S(1)} %get-tuple-element.27), channel_id=1, source_target_pairs={{16,0},{32,16},{48,32},{64,48},{80,64},{96,80},{112,96},{128,112},... | collective-permute-start | bytes 147464 | tf_op jit(solution)/shard_map/ppermute | solution.py:212
  58.0 0.7 shard_map.95
  58.7 0.0 collective-permute-done.3.refs_0_
  58.7 2.9 %collective-permute-done.4.refs_2_ = bf16[3,64,128]{2,1,0:T(8,128)(2,1)S(1)} collective-permute-done((bf16[3,64,128]{2,1,0:T(8,128)(2,1)S(1)}, bf16[3,64,128]{2,1,0:T(8,128)(2,1)S(1)}, u32[]{:S(2)}, u32[]{:S(2)}) %collective-permute-start.4) | collective-permute-done | bytes 49184 | tf_op jit(solution)/shard_map/ppermute | solution.py:212
  61.5 0.5 shard_map.96
  62.1 13.5 %all_to_all.22.refs_0_ = bf16[16,64,256]{2,1,0:T(8,128)(2,1)S(1)} all-to-all(bf16[16,64,256]{2,1,0:T(8,128)(2,1)S(1)} %bitcast.15), channel_id=1, replica_groups=mesh['space'=32,'tensor'=16] {'tensor'}, dimensions={0} | all-to-all | bytes 1048576 | tf_op jit(solution)/shard_map/all_to_all | solution.py:230
  75.5 1.4 %shard_map.97 = bf16[8,2,64,256]{3,2,1,0:T(8,128)(2,1)S(1)} custom-call(bf16[16,64,256]{2,1,0:T(8,128)(2,1)S(1)} %all_to_all.22.refs_0_, f32[2,1024]{1,0:T(2,128)S(1)} %copy-done.2, f32[2,1024]{1,0:T(2,128)S(1)} %copy-done.3, bf16[2,1024,256]{2,1,0:T(8,128)(2,1)S(1)} %copy-done, bf16[2,256,1024]{2,1,0:T(8,128)(2,1)S(1)} %copy-done.1, ...), custom_call_target="tpu_custom_call" | custom-call | tf_op jit(solution)/shard_map/pallas_call | solution.py:19
  76.9 13.5 %all_to_all.23 = bf16[16,64,256]{2,1,0:T(8,128)(2,1)S(1)} all-to-all(bf16[16,64,256]{2,1,0:T(8,128)(2,1)S(1)} %bitcast.11), channel_id=1, replica_groups=mesh['space'=32,'tensor'=16] {'tensor'}, dimensions={0} | all-to-all | bytes 1048576 | tf_op jit(solution)/shard_map/all_to_all | solution.py:237
  90.4 0.7 shard_map.98
Async XLA Ops:
  0.0 17.3 %collective-permute-start.1 = (bf16[4,64,128]{2,1,0:T(8,128)(2,1)}, bf16[4,64,128]{2,1,0:T(8,128)(2,1)S(1)}, u32[]{:S(2)}, u32[]{:S(2)}) collective-permute-start(bf16[4,64,128]{2,1,0:T(8,128)(2,1)} %bitcast.17), channel_id=1, source_target_pairs={{0,16},{16,32},{32,48},{48,64},{64,80},{80,96},{96,112},{112,128},... | collective-permute-start | bytes 196616 | tf_op jit(solution)/shard_map/ppermute | solution.py:211
  6.1 11.2 %collective-permute-start = (bf16[4,64,128]{2,1,0:T(8,128)(2,1)}, bf16[4,64,128]{2,1,0:T(8,128)(2,1)S(1)}, u32[]{:S(2)}, u32[]{:S(2)}) collective-permute-start(bf16[4,64,128]{2,1,0:T(8,128)(2,1)} %bitcast.18), channel_id=1, source_target_pairs={{16,0},{32,16},{48,32},{64,48},{80,64},{96,80},{112,96},{128,112},... | collective-permute-start | bytes 196616 | tf_op jit(solution)/shard_map/ppermute | solution.py:212
  15.4 18.8 %collective-permute-start.2 = (bf16[2,2056,256]{2,1,0:T(8,128)(2,1)S(1)}, bf16[2,2056,256]{2,1,0:T(8,128)(2,1)S(1)}, u32[]{:S(2)}, u32[]{:S(2)}) collective-permute-start(bf16[2,2056,256]{2,1,0:T(8,128)(2,1)S(1)} %get-tuple-element.21), channel_id=1, source_target_pairs={{0,1},{1,0},{2,3},{3,2},{4,5},{5,4},{6,7},{7,6},{8,9},{9,8},{10,11... | collective-permute-start | bytes 6316040 | tf_op jit(solution)/shard_map/ppermute | solution.py:217
  17.3 16.8 %copy-start = (bf16[2,1024,256]{2,1,0:T(8,128)(2,1)S(1)}, bf16[2,1024,256]{2,1,0:T(8,128)(2,1)}, u32[]{:S(2)}) copy-start(bf16[2,1024,256]{2,1,0:T(8,128)(2,1)} %refs_3_.3) | copy-start | bytes 3145732
  17.3 16.8 %copy-start.1 = (bf16[2,256,1024]{2,1,0:T(8,128)(2,1)S(1)}, bf16[2,256,1024]{2,1,0:T(8,128)(2,1)}, u32[]{:S(2)}) copy-start(bf16[2,256,1024]{2,1,0:T(8,128)(2,1)} %refs_4_.3) | copy-start | bytes 3145732
  17.3 16.8 %copy-start.2 = (f32[2,1024]{1,0:T(2,128)S(1)}, f32[2,1024]{1,0:T(2,128)}, u32[]{:S(2)}) copy-start(f32[2,1024]{1,0:T(2,128)} %refs_1_.3) | copy-start | bytes 24580
  17.4 16.8 %copy-start.3 = (f32[2,1024]{1,0:T(2,128)S(1)}, f32[2,1024]{1,0:T(2,128)}, u32[]{:S(2)}) copy-start(f32[2,1024]{1,0:T(2,128)} %refs_2_.3) | copy-start | bytes 24580
  17.4 16.8 %copy-start.4 = (f32[2,256]{1,0:T(2,128)S(1)}, f32[2,256]{1,0:T(2,128)}, u32[]{:S(2)}) copy-start(f32[2,256]{1,0:T(2,128)} %refs_5_.3) | copy-start | bytes 6148
  49.1 9.6 %collective-permute-start.3 = (bf16[3,64,128]{2,1,0:T(8,128)(2,1)S(1)}, bf16[3,64,128]{2,1,0:T(8,128)(2,1)S(1)}, u32[]{:S(2)}, u32[]{:S(2)}) collective-permute-start(bf16[3,64,128]{2,1,0:T(8,128)(2,1)S(1)} %get-tuple-element.23), channel_id=1, source_target_pairs={{0,16},{16,32},{32,48},{48,64},{64,80},{80,96},{96,112},{112,128},... | collective-permute-start | bytes 147464 | tf_op jit(solution)/shard_map/ppermute | solution.py:211
  54.1 7.4 %collective-permute-start.4 = (bf16[3,64,128]{2,1,0:T(8,128)(2,1)S(1)}, bf16[3,64,128]{2,1,0:T(8,128)(2,1)S(1)}, u32[]{:S(2)}, u32[]{:S(2)}) collective-permute-start(bf16[3,64,128]{2,1,0:T(8,128)(2,1)S(1)} %get-tuple-element.27), channel_id=1, source_target_pairs={{16,0},{32,16},{48,32},{64,48},{80,64},{96,80},{112,96},{128,112},... | collective-permute-start | bytes 147464 | tf_op jit(solution)/shard_map/ppermute | solution.py:212

commit v9 on v8

--- a/solution.py
+++ b/solution.py
@@ -94,9 +94,14 @@
     )(*[pltpu.with_memory_space_constraint(array, pltpu.HBM) for array in inputs])
 
 
-def conv_kernel(before_leads, before_ref, rows_ref, after_ref, wide_ref, out_ref):
-    if not before_leads:
-        before_ref, after_ref = after_ref, before_ref
+def even_band():
+    return lax.rem(lax.axis_index("space"), 2) == 0
+
+
+def conv_kernel(out_first, near_ref, rows_ref, far_ref, wide_ref, out_ref):
+    if out_first:
+        near_ref, far_ref = far_ref, near_ref
+    even = even_band()
     height, share, width = rows_ref.shape
     copies = out_ref.shape[0]
     size = 16
@@ -107,9 +112,12 @@
     }
     for group in range(share // size):
         chans = slice(size * group, size * (group + 1))
-        rows = [before_ref[r, chans, :] for r in range(before_ref.shape[0] - HALF, before_ref.shape[0])]
+        start = near_ref.shape[0] - HALF
+        near = [near_ref[r, chans, :].astype(jnp.float32) for r in range(near_ref.shape[0])]
+        far = [far_ref[r, chans, :].astype(jnp.float32) for r in range(far_ref.shape[0])]
+        rows = [jnp.where(even, far[start + r], near[start + r]) for r in range(HALF)]
         rows += [rows_ref[r, chans, :] for r in range(height)]
-        rows += [after_ref[r, chans, :] for r in range(HALF)]
+        rows += [jnp.where(even, near[r], far[r]) for r in range(HALF)]
         rows = [row.astype(jnp.float32) for row in rows]
         totals = [None] * height
         for j in range(TAPS):
@@ -179,18 +187,22 @@
 def mix_kernel(parts_ref, stream_ref, affine_ref, out_ref, *edge_refs):
     height, share, width = stream_ref.shape
     scale, shift = affine_ref[0], affine_ref[1]
+    rows = []
     for r in range(height):
         half, at = divmod(r, height // CORES)
         lanes = slice(width * at, width * (at + 1))
         mixed = parts_ref[0, half, :, lanes].astype(jnp.float32)
         for copy in range(1, parts_ref.shape[0]):
             mixed = mixed + parts_ref[copy, half, :, lanes].astype(jnp.float32)
-        updated = stream_ref[r].astype(jnp.float32) + scale * (mixed + shift)
-        row = updated.astype(jnp.bfloat16)
-        out_ref[r] = row
-        for ref, start in zip(edge_refs, (height - HALF, 0)):
-            if start <= r < start + HALF:
-                ref[r - start] = row
+        rows.append(stream_ref[r].astype(jnp.float32) + scale * (mixed + shift))
+        out_ref[r] = rows[r].astype(jnp.bfloat16)
+    if edge_refs:
+        even = even_band()
+        near_ref, far_ref = edge_refs
+        for r in range(HALF):
+            top, bottom = rows[r], rows[height - HALF + r]
+            near_ref[r] = jnp.where(even, bottom, top).astype(jnp.bfloat16)
+            far_ref[r] = jnp.where(even, top, bottom).astype(jnp.bfloat16)
 
 
 def per_device(features, depth_kernel, norm_gain, norm_bias, w_expand, b_expand, w_reduce, b_reduce, layer_scale):
@@ -199,17 +211,17 @@
     copies = members // CORES
     half = height // CORES * width
     units = w_expand.shape[2]
-    down = [(i, i + 1) for i in range(bands - 1)]
-    up = [(j, i) for i, j in down]
+    pairs = [(i, i ^ 1) for i in range(bands)]
+    others = [(i, ((i + 1) ^ 1) - 1) for i in range(1, bands - 1)]
     sibling = [(i, i ^ 1) for i in range(members)]
 
     stream = jnp.transpose(features, (0, 2, 1))
     taps = jnp.transpose(depth_kernel, (1, 2, 0, 3)).reshape(TAPS * TAPS, BLOCKS, share)
 
-    last = first = stream
+    near = far = stream
     for block in range(BLOCKS):
-        before = lax.ppermute(last, "space", down)
-        after = lax.ppermute(first, "space", up)
+        far = lax.ppermute(far, "space", others)
+        near = lax.ppermute(near, "space", pairs)
         if block == 0:
             wide, affine, stream, taps, layer_scale, b_reduce, pack = entered(
                 stream, taps, layer_scale, b_reduce, w_expand, w_reduce, b_expand
@@ -220,7 +232,7 @@
             wide, affine = call(
                 lambda *refs: spread(1, *refs), spread_shapes(share, width), taps, next_scale, b_reduce
             )
-        edges = (after, before) if block == 0 else (before, after)
+        edges = (near, far) if block == 0 else (far, near)
         filtered = call(
             lambda *refs: conv_kernel(block > 0, *refs),
             jax.ShapeDtypeStruct((copies, CORES, share, half), jnp.bfloat16),
@@ -239,7 +251,7 @@
         whole = jax.ShapeDtypeStruct((height, share, width), jnp.bfloat16)
         if block + 1 < BLOCKS:
             edge = jax.ShapeDtypeStruct((HALF, share, width), jnp.bfloat16)
-            stream, last, first = call(mix_kernel, (whole, edge, edge), partial, stream, affine)
+            stream, near, far = call(mix_kernel, (whole, edge, edge), partial, stream, affine)
         else:
             stream = call(mix_kernel, whole, partial, stream, affine)
     return jnp.transpose(stream, (0, 2, 1))

time: 91.8 us -> 91 us (level)
  starting transfers between devices: 24.4 us -> 20.8 us
  waiting for transfers between devices: 2.87 us -> 6.27 us
    ppermute x4, starting transfers between devices: 22.5 us -> 18.8 us  [the longest x2 14.6 us: per_device(): far = lax.ppermute(far, 'space', others)]
    ppermute x4, waiting for transfers between devices: 2.87 us -> 6.27 us  [the longest x2 3.16 us: per_device(): near = lax.ppermute(near, 'space', pairs)]
  transfers between devices with their start and end apart: 5 -> 5, of which waited for: 1 -> 3; matrix products, arithmetic and copies ran while one was open for 0% -> 0% of each run, Pallas kernels for 3% -> 3%
where the time goes in v9:
time: 91 us; the launch traced here: 90.6 us
  blocking collectives  56.4 us (62%)
  starting transfers between devices  20.8 us (23%)
  Pallas kernels  7.01 us (8%)
  waiting for transfers between devices  6.27 us (7%)
    all_to_all x2, blocking collectives, per_device(): lax.all_to_all(filtered.reshape(members, share, half), 'tensor', 0, 0, ti...  29.4 us
    all_to_all x2, blocking collectives, per_device(): lax.all_to_all(partial.reshape(members, share, half), 'tensor', 0, 0, til...  27 us
    ppermute x2, starting transfers between devices, per_device(): far = lax.ppermute(far, 'space', others)  14.6 us
    pallas_call x7, Pallas kernels, call(): pl.pallas_call(body, out_shape=outs, in_specs=[VMEM] * len(args), out_spe...  5.3 us
    ppermute x2, starting transfers between devices, per_device(): near = lax.ppermute(near, 'space', pairs)  4.25 us
    ppermute x2, waiting for transfers between devices, per_device(): near = lax.ppermute(near, 'space', pairs)  3.16 us
    ppermute x2, waiting for transfers between devices, per_device(): far = lax.ppermute(far, 'space', others)  3.1 us
    ppermute x1, starting transfers between devices, per_device(): pack = lax.ppermute(pack, 'tensor', sibling)  1.92 us
  transfers between devices with their start and end apart: 5, of which 3 were waited for; matrix products, arithmetic and copies ran while one was open for 0% of the time, Pallas kernels for 3%

profile of v9, /device:TPU:56, one launch (start us, length us, event | category | flops | bytes accessed | tf_op | source)
XLA Modules:
  0.0 90.6 jit_solution(6481810279598072593)
XLA Ops:
  0.0 11.7 %collective-permute-start.1 = (bf16[4,64,128]{2,1,0:T(8,128)(2,1)}, bf16[4,64,128]{2,1,0:T(8,128)(2,1)S(1)}, u32[]{:S(2)}, u32[]{:S(2)}) collective-permute-start(bf16[4,64,128]{2,1,0:T(8,128)(2,1)} %bitcast.17), channel_id=1, source_target_pairs={{16,32},{32,16},{48,64},{64,48},{80,96},{96,80},{112,128},{128,112... | collective-permute-start | bytes 196616 | tf_op jit(solution)/shard_map/ppermute | solution.py:223
  11.7 1.9 %collective-permute-start = (bf16[4,64,128]{2,1,0:T(8,128)(2,1)}, bf16[4,64,128]{2,1,0:T(8,128)(2,1)S(1)}, u32[]{:S(2)}, u32[]{:S(2)}) collective-permute-start(bf16[4,64,128]{2,1,0:T(8,128)(2,1)} %bitcast.18), channel_id=1, source_target_pairs={{0,16},{16,0},{32,48},{48,32},{64,80},{80,64},{96,112},{112,96},{1... | collective-permute-start | bytes 196616 | tf_op jit(solution)/shard_map/ppermute | solution.py:224
  13.6 1.7 %shard_map.91 = (f32[49,64,128]{2,1,0:T(8,128)S(1)}, f32[2,64,128]{2,1,0:T(8,128)S(1)}, bf16[4,64,128]{2,1,0:T(8,128)(2,1)S(1)}, bf16[49,2,64]{2,1,0:T(2,128)(2,...) custom-call(bf16[4,64,128]{2,1,0:T(8,128)(2,1)} %bitcast.19, ...), custom_call_target="tpu_custom_call" | custom-call | tf_op jit(solution)/shard_map/pallas_call | solution.py:84
  15.4 1.9 %collective-permute-start.2 = (bf16[2,2056,256]{2,1,0:T(8,128)(2,1)S(1)}, bf16[2,2056,256]{2,1,0:T(8,128)(2,1)S(1)}, u32[]{:S(2)}, u32[]{:S(2)}) collective-permute-start(bf16[2,2056,256]{2,1,0:T(8,128)(2,1)S(1)} %get-tuple-element.21), channel_id=1, source_target_pairs={{0,1},{1,0},{2,3},{3,2},{4,5},{5,4},{6,7},{7,6},{8,9},{9,8},{10,11... | collective-permute-start | bytes 6316040 | tf_op jit(solution)/shard_map/ppermute | solution.py:229
  17.3 0.0 collective-permute-done.1.refs_2_
  17.3 1.9 %collective-permute-done.refs_0_ = bf16[4,64,128]{2,1,0:T(8,128)(2,1)S(1)} collective-permute-done((bf16[4,64,128]{2,1,0:T(8,128)(2,1)}, bf16[4,64,128]{2,1,0:T(8,128)(2,1)S(1)}, u32[]{:S(2)}, u32[]{:S(2)}) %collective-permute-start) | collective-permute-done | bytes 65568 | tf_op jit(solution)/shard_map/ppermute | solution.py:224
  19.2 0.0 copy-start
  19.2 0.0 copy-start.1
  19.2 0.0 copy-start.2
  19.2 0.0 copy-start.3
  19.2 0.0 copy-start.4
  19.2 0.5 shard_map.92
  19.8 15.9 %all_to_all.20.refs_0_ = bf16[16,64,256]{2,1,0:T(8,128)(2,1)S(1)} all-to-all(bf16[16,64,256]{2,1,0:T(8,128)(2,1)S(1)} %bitcast.16), channel_id=1, replica_groups=mesh['space'=32,'tensor'=16] {'tensor'}, dimensions={0} | all-to-all | bytes 1048576 | tf_op jit(solution)/shard_map/all_to_all | solution.py:242
  35.7 0.0 collective-permute-done.2.refs_6_
  35.7 0.0 copy-done
  35.7 0.0 copy-done.1
  35.7 0.0 copy-done.2
  35.7 0.0 copy-done.3
  35.7 0.0 copy-done.4
  35.7 1.4 %shard_map.93 = bf16[8,2,64,256]{3,2,1,0:T(8,128)(2,1)S(1)} custom-call(bf16[16,64,256]{2,1,0:T(8,128)(2,1)S(1)} %all_to_all.20.refs_0_, f32[2,1024]{1,0:T(2,128)S(1)} %copy-done.2, f32[2,1024]{1,0:T(2,128)S(1)} %copy-done.3, bf16[2,1024,256]{2,1,0:T(8,128)(2,1)S(1)} %copy-done, bf16[2,256,1024]{2,1,0:T(8,128)(2,1)S(1)} %copy-done.1, ...), custom_call_target="tpu_custom_call" | custom-call | tf_op jit(solution)/shard_map/pallas_call | solution.py:19
  37.1 13.5 %all_to_all.21 = bf16[16,64,256]{2,1,0:T(8,128)(2,1)S(1)} all-to-all(bf16[16,64,256]{2,1,0:T(8,128)(2,1)S(1)} %bitcast.12), channel_id=1, replica_groups=mesh['space'=32,'tensor'=16] {'tensor'}, dimensions={0} | all-to-all | bytes 1048576 | tf_op jit(solution)/shard_map/all_to_all | solution.py:249
  50.6 0.1 shard_map.94
  50.7 2.9 %collective-permute-start.3 = (bf16[3,64,128]{2,1,0:T(8,128)(2,1)S(1)}, bf16[3,64,128]{2,1,0:T(8,128)(2,1)S(1)}, u32[]{:S(2)}, u32[]{:S(2)}) collective-permute-start(bf16[3,64,128]{2,1,0:T(8,128)(2,1)S(1)} %get-tuple-element.23), channel_id=1, source_target_pairs={{16,32},{32,16},{48,64},{64,48},{80,96},{96,80},{112,128},{128,112... | collective-permute-start | bytes 147464 | tf_op jit(solution)/shard_map/ppermute | solution.py:223
  53.6 2.3 %collective-permute-start.4 = (bf16[3,64,128]{2,1,0:T(8,128)(2,1)S(1)}, bf16[3,64,128]{2,1,0:T(8,128)(2,1)S(1)}, u32[]{:S(2)}, u32[]{:S(2)}) collective-permute-start(bf16[3,64,128]{2,1,0:T(8,128)(2,1)S(1)} %get-tuple-element.27), channel_id=1, source_target_pairs={{0,16},{16,0},{32,48},{48,32},{64,80},{80,64},{96,112},{112,96},{1... | collective-permute-start | bytes 147464 | tf_op jit(solution)/shard_map/ppermute | solution.py:224
  55.9 0.7 shard_map.95
  56.6 3.1 %collective-permute-done.3.refs_0_ = bf16[3,64,128]{2,1,0:T(8,128)(2,1)S(1)} collective-permute-done((bf16[3,64,128]{2,1,0:T(8,128)(2,1)S(1)}, bf16[3,64,128]{2,1,0:T(8,128)(2,1)S(1)}, u32[]{:S(2)}, u32[]{:S(2)}) %collective-permute-start.3) | collective-permute-done | bytes 49184 | tf_op jit(solution)/shard_map/ppermute | solution.py:223
  59.7 1.3 %collective-permute-done.4.refs_2_ = bf16[3,64,128]{2,1,0:T(8,128)(2,1)S(1)} collective-permute-done((bf16[3,64,128]{2,1,0:T(8,128)(2,1)S(1)}, bf16[3,64,128]{2,1,0:T(8,128)(2,1)S(1)}, u32[]{:S(2)}, u32[]{:S(2)}) %collective-permute-start.4) | collective-permute-done | bytes 49184 | tf_op jit(solution)/shard_map/ppermute | solution.py:224
  61.0 0.5 shard_map.96
  61.5 13.5 %all_to_all.22.refs_0_ = bf16[16,64,256]{2,1,0:T(8,128)(2,1)S(1)} all-to-all(bf16[16,64,256]{2,1,0:T(8,128)(2,1)S(1)} %bitcast.15), channel_id=1, replica_groups=mesh['space'=32,'tensor'=16] {'tensor'}, dimensions={0} | all-to-all | bytes 1048576 | tf_op jit(solution)/shard_map/all_to_all | solution.py:242
  75.0 1.4 %shard_map.97 = bf16[8,2,64,256]{3,2,1,0:T(8,128)(2,1)S(1)} custom-call(bf16[16,64,256]{2,1,0:T(8,128)(2,1)S(1)} %all_to_all.22.refs_0_, f32[2,1024]{1,0:T(2,128)S(1)} %copy-done.2, f32[2,1024]{1,0:T(2,128)S(1)} %copy-done.3, bf16[2,1024,256]{2,1,0:T(8,128)(2,1)S(1)} %copy-done, bf16[2,256,1024]{2,1,0:T(8,128)(2,1)S(1)} %copy-done.1, ...), custom_call_target="tpu_custom_call" | custom-call | tf_op jit(solution)/shard_map/pallas_call | solution.py:19
  76.4 13.5 %all_to_all.23 = bf16[16,64,256]{2,1,0:T(8,128)(2,1)S(1)} all-to-all(bf16[16,64,256]{2,1,0:T(8,128)(2,1)S(1)} %bitcast.11), channel_id=1, replica_groups=mesh['space'=32,'tensor'=16] {'tensor'}, dimensions={0} | all-to-all | bytes 1048576 | tf_op jit(solution)/shard_map/all_to_all | solution.py:249
  89.9 0.7 shard_map.98
Async XLA Ops:
  0.0 17.3 %collective-permute-start.1 = (bf16[4,64,128]{2,1,0:T(8,128)(2,1)}, bf16[4,64,128]{2,1,0:T(8,128)(2,1)S(1)}, u32[]{:S(2)}, u32[]{:S(2)}) collective-permute-start(bf16[4,64,128]{2,1,0:T(8,128)(2,1)} %bitcast.17), channel_id=1, source_target_pairs={{16,32},{32,16},{48,64},{64,48},{80,96},{96,80},{112,128},{128,112... | collective-permute-start | bytes 196616 | tf_op jit(solution)/shard_map/ppermute | solution.py:223
  11.7 7.5 %collective-permute-start = (bf16[4,64,128]{2,1,0:T(8,128)(2,1)}, bf16[4,64,128]{2,1,0:T(8,128)(2,1)S(1)}, u32[]{:S(2)}, u32[]{:S(2)}) collective-permute-start(bf16[4,64,128]{2,1,0:T(8,128)(2,1)} %bitcast.18), channel_id=1, source_target_pairs={{0,16},{16,0},{32,48},{48,32},{64,80},{80,64},{96,112},{112,96},{1... | collective-permute-start | bytes 196616 | tf_op jit(solution)/shard_map/ppermute | solution.py:224
  15.4 20.3 %collective-permute-start.2 = (bf16[2,2056,256]{2,1,0:T(8,128)(2,1)S(1)}, bf16[2,2056,256]{2,1,0:T(8,128)(2,1)S(1)}, u32[]{:S(2)}, u32[]{:S(2)}) collective-permute-start(bf16[2,2056,256]{2,1,0:T(8,128)(2,1)S(1)} %get-tuple-element.21), channel_id=1, source_target_pairs={{0,1},{1,0},{2,3},{3,2},{4,5},{5,4},{6,7},{7,6},{8,9},{9,8},{10,11... | collective-permute-start | bytes 6316040 | tf_op jit(solution)/shard_map/ppermute | solution.py:229
  19.2 16.5 %copy-start = (bf16[2,1024,256]{2,1,0:T(8,128)(2,1)S(1)}, bf16[2,1024,256]{2,1,0:T(8,128)(2,1)}, u32[]{:S(2)}) copy-start(bf16[2,1024,256]{2,1,0:T(8,128)(2,1)} %refs_3_.3) | copy-start | bytes 3145732
  19.2 16.5 %copy-start.1 = (bf16[2,256,1024]{2,1,0:T(8,128)(2,1)S(1)}, bf16[2,256,1024]{2,1,0:T(8,128)(2,1)}, u32[]{:S(2)}) copy-start(bf16[2,256,1024]{2,1,0:T(8,128)(2,1)} %refs_4_.3) | copy-start | bytes 3145732
  19.2 16.5 %copy-start.2 = (f32[2,1024]{1,0:T(2,128)S(1)}, f32[2,1024]{1,0:T(2,128)}, u32[]{:S(2)}) copy-start(f32[2,1024]{1,0:T(2,128)} %refs_1_.3) | copy-start | bytes 24580
  19.2 16.5 %copy-start.3 = (f32[2,1024]{1,0:T(2,128)S(1)}, f32[2,1024]{1,0:T(2,128)}, u32[]{:S(2)}) copy-start(f32[2,1024]{1,0:T(2,128)} %refs_2_.3) | copy-start | bytes 24580
  19.2 16.5 %copy-start.4 = (f32[2,256]{1,0:T(2,128)S(1)}, f32[2,256]{1,0:T(2,128)}, u32[]{:S(2)}) copy-start(f32[2,256]{1,0:T(2,128)} %refs_5_.3) | copy-start | bytes 6148
  50.7 9.0 %collective-permute-start.3 = (bf16[3,64,128]{2,1,0:T(8,128)(2,1)S(1)}, bf16[3,64,128]{2,1,0:T(8,128)(2,1)S(1)}, u32[]{:S(2)}, u32[]{:S(2)}) collective-permute-start(bf16[3,64,128]{2,1,0:T(8,128)(2,1)S(1)} %get-tuple-element.23), channel_id=1, source_target_pairs={{16,32},{32,16},{48,64},{64,48},{80,96},{96,80},{112,128},{128,112... | collective-permute-start | bytes 147464 | tf_op jit(solution)/shard_map/ppermute | solution.py:223
  53.6 7.4 %collective-permute-start.4 = (bf16[3,64,128]{2,1,0:T(8,128)(2,1)S(1)}, bf16[3,64,128]{2,1,0:T(8,128)(2,1)S(1)}, u32[]{:S(2)}, u32[]{:S(2)}) collective-permute-start(bf16[3,64,128]{2,1,0:T(8,128)(2,1)S(1)} %get-tuple-element.27), channel_id=1, source_target_pairs={{0,16},{16,0},{32,48},{48,32},{64,80},{80,64},{96,112},{112,96},{1... | collective-permute-start | bytes 147464 | tf_op jit(solution)/shard_map/ppermute | solution.py:224

commit v10 on v9

--- a/solution.py
+++ b/solution.py
@@ -98,10 +98,8 @@
     return lax.rem(lax.axis_index("space"), 2) == 0
 
 
-def conv_kernel(out_first, near_ref, rows_ref, far_ref, wide_ref, out_ref):
-    if out_first:
-        near_ref, far_ref = far_ref, near_ref
-    even = even_band()
+def conv_kernel(paired, first_ref, rows_ref, second_ref, wide_ref, out_ref):
+    even = even_band() if paired else None
     height, share, width = rows_ref.shape
     copies = out_ref.shape[0]
     size = 16
@@ -112,12 +110,16 @@
     }
     for group in range(share // size):
         chans = slice(size * group, size * (group + 1))
-        start = near_ref.shape[0] - HALF
-        near = [near_ref[r, chans, :].astype(jnp.float32) for r in range(near_ref.shape[0])]
-        far = [far_ref[r, chans, :].astype(jnp.float32) for r in range(far_ref.shape[0])]
-        rows = [jnp.where(even, far[start + r], near[start + r]) for r in range(HALF)]
+        start = first_ref.shape[0] - HALF
+        first = [first_ref[r, chans, :].astype(jnp.float32) for r in range(first_ref.shape[0])]
+        second = [second_ref[r, chans, :].astype(jnp.float32) for r in range(second_ref.shape[0])]
+        if paired:
+            rows = [jnp.where(even, second[start + r], first[start + r]) for r in range(HALF)]
+            last = [jnp.where(even, first[r], second[r]) for r in range(HALF)]
+        else:
+            rows, last = first[start:], second[:HALF]
         rows += [rows_ref[r, chans, :] for r in range(height)]
-        rows += [jnp.where(even, near[r], far[r]) for r in range(HALF)]
+        rows += last
         rows = [row.astype(jnp.float32) for row in rows]
         totals = [None] * height
         for j in range(TAPS):
@@ -196,13 +198,9 @@
             mixed = mixed + parts_ref[copy, half, :, lanes].astype(jnp.float32)
         rows.append(stream_ref[r].astype(jnp.float32) + scale * (mixed + shift))
         out_ref[r] = rows[r].astype(jnp.bfloat16)
-    if edge_refs:
-        even = even_band()
-        near_ref, far_ref = edge_refs
+    for ref, start in zip(edge_refs, (height - HALF, 0)):
         for r in range(HALF):
-            top, bottom = rows[r], rows[height - HALF + r]
-            near_ref[r] = jnp.where(even, bottom, top).astype(jnp.bfloat16)
-            far_ref[r] = jnp.where(even, top, bottom).astype(jnp.bfloat16)
+            ref[r] = rows[start + r].astype(jnp.bfloat16)
 
 
 def per_device(features, depth_kernel, norm_gain, norm_bias, w_expand, b_expand, w_reduce, b_reduce, layer_scale):
@@ -211,6 +209,8 @@
     copies = members // CORES
     half = height // CORES * width
     units = w_expand.shape[2]
+    down = [(i, i + 1) for i in range(bands - 1)]
+    up = [(j, i) for i, j in down]
     pairs = [(i, i ^ 1) for i in range(bands)]
     others = [(i, ((i + 1) ^ 1) - 1) for i in range(1, bands - 1)]
     sibling = [(i, i ^ 1) for i in range(members)]
@@ -218,10 +218,13 @@
     stream = jnp.transpose(features, (0, 2, 1))
     taps = jnp.transpose(depth_kernel, (1, 2, 0, 3)).reshape(TAPS * TAPS, BLOCKS, share)
 
-    near = far = stream
     for block in range(BLOCKS):
-        far = lax.ppermute(far, "space", others)
-        near = lax.ppermute(near, "space", pairs)
+        if block == 0:
+            second = lax.ppermute(stream, "space", others)
+            first = lax.ppermute(stream, "space", pairs)
+        else:
+            first = lax.ppermute(last_rows, "space", down)
+            second = lax.ppermute(first_rows, "space", up)
         if block == 0:
             wide, affine, stream, taps, layer_scale, b_reduce, pack = entered(
                 stream, taps, layer_scale, b_reduce, w_expand, w_reduce, b_expand
@@ -232,11 +235,10 @@
             wide, affine = call(
                 lambda *refs: spread(1, *refs), spread_shapes(share, width), taps, next_scale, b_reduce
             )
-        edges = (near, far) if block == 0 else (far, near)
         filtered = call(
-            lambda *refs: conv_kernel(block > 0, *refs),
+            lambda *refs: conv_kernel(block == 0, *refs),
             jax.ShapeDtypeStruct((copies, CORES, share, half), jnp.bfloat16),
-            edges[0], stream, edges[1], wide,
+            first, stream, second, wide,
             cost=pl.CostEstimate(flops=10**11, transcendentals=0, bytes_accessed=10**6) if block == 0 else None,
         )
         filtered = lax.all_to_all(filtered.reshape(members, share, half), "tensor", 0, 0, tiled=True)
@@ -251,7 +253,7 @@
         whole = jax.ShapeDtypeStruct((height, share, width), jnp.bfloat16)
         if block + 1 < BLOCKS:
             edge = jax.ShapeDtypeStruct((HALF, share, width), jnp.bfloat16)
-            stream, near, far = call(mix_kernel, (whole, edge, edge), partial, stream, affine)
+            stream, last_rows, first_rows = call(mix_kernel, (whole, edge, edge), partial, stream, affine)
         else:
             stream = call(mix_kernel, whole, partial, stream, affine)
     return jnp.transpose(stream, (0, 2, 1))

time: 91 us -> 91.7 us (level)
  starting transfers between devices: 20.8 us -> 24.4 us
  waiting for transfers between devices: 6.27 us -> 3.11 us
    ppermute x4, starting transfers between devices: 18.8 us -> 22.5 us  [the longest x1 11.7 us: per_device(): second = lax.ppermute(stream, 'space', others)]
    ppermute x4, waiting for transfers between devices: 6.27 us -> 3.11 us  [the longest x1 1.88 us: per_device(): first = lax.ppermute(stream, 'space', pairs)]
  transfers between devices with their start and end apart: 5 -> 5, of which waited for: 3 -> 2; matrix products, arithmetic and copies ran while one was open for 0% -> 0% of each run, Pallas kernels for 3% -> 3%
where the time goes in v10:
time: 91.7 us; the launch traced here: 91 us
  blocking collectives  56.4 us (62%)
  starting transfers between devices  24.4 us (27%)
  Pallas kernels  6.99 us (8%)
  waiting for transfers between devices  3.11 us (3%)
    all_to_all x2, blocking collectives, per_device(): lax.all_to_all(filtered.reshape(members, share, half), 'tensor', 0, 0, ti...  29.4 us
    all_to_all x2, blocking collectives, per_device(): lax.all_to_all(partial.reshape(members, share, half), 'tensor', 0, 0, til...  27 us
    ppermute x1, starting transfers between devices, per_device(): second = lax.ppermute(stream, 'space', others)  11.7 us
    ppermute x1, starting transfers between devices, per_device(): second = lax.ppermute(first_rows, 'space', up)  5.56 us
    pallas_call x7, Pallas kernels, call(): pl.pallas_call(body, out_shape=outs, in_specs=[VMEM] * len(args), out_spe...  5.28 us
    ppermute x1, starting transfers between devices, per_device(): first = lax.ppermute(last_rows, 'space', down)  3.29 us
    ppermute x1, starting transfers between devices, per_device(): pack = lax.ppermute(pack, 'tensor', sibling)  1.92 us
    ppermute x1, starting transfers between devices, per_device(): first = lax.ppermute(stream, 'space', pairs)  1.92 us
  transfers between devices with their start and end apart: 5, of which 2 were waited for; matrix products, arithmetic and copies ran while one was open for 0% of the time, Pallas kernels for 3%

profile of v10, /device:TPU:56, one launch (start us, length us, event | category | flops | bytes accessed | tf_op | source)
XLA Modules:
  0.0 91.0 jit_solution(988383173413936532)
XLA Ops:
  0.0 11.7 %collective-permute-start.1 = (bf16[4,64,128]{2,1,0:T(8,128)(2,1)}, bf16[4,64,128]{2,1,0:T(8,128)(2,1)S(1)}, u32[]{:S(2)}, u32[]{:S(2)}) collective-permute-start(bf16[4,64,128]{2,1,0:T(8,128)(2,1)} %bitcast.17), channel_id=1, source_target_pairs={{16,32},{32,16},{48,64},{64,48},{80,96},{96,80},{112,128},{128,112... | collective-permute-start | bytes 196616 | tf_op jit(solution)/shard_map/ppermute | solution.py:223
  11.7 1.9 %collective-permute-start = (bf16[4,64,128]{2,1,0:T(8,128)(2,1)}, bf16[4,64,128]{2,1,0:T(8,128)(2,1)S(1)}, u32[]{:S(2)}, u32[]{:S(2)}) collective-permute-start(bf16[4,64,128]{2,1,0:T(8,128)(2,1)} %bitcast.18), channel_id=1, source_target_pairs={{0,16},{16,0},{32,48},{48,32},{64,80},{80,64},{96,112},{112,96},{1... | collective-permute-start | bytes 196616 | tf_op jit(solution)/shard_map/ppermute | solution.py:224
  13.6 1.7 %shard_map.91 = (f32[49,64,128]{2,1,0:T(8,128)S(1)}, f32[2,64,128]{2,1,0:T(8,128)S(1)}, bf16[4,64,128]{2,1,0:T(8,128)(2,1)S(1)}, bf16[49,2,64]{2,1,0:T(2,128)(2,...) custom-call(bf16[4,64,128]{2,1,0:T(8,128)(2,1)} %bitcast.19, ...), custom_call_target="tpu_custom_call" | custom-call | tf_op jit(solution)/shard_map/pallas_call | solution.py:84
  15.4 1.9 %collective-permute-start.2 = (bf16[2,2056,256]{2,1,0:T(8,128)(2,1)S(1)}, bf16[2,2056,256]{2,1,0:T(8,128)(2,1)S(1)}, u32[]{:S(2)}, u32[]{:S(2)}) collective-permute-start(bf16[2,2056,256]{2,1,0:T(8,128)(2,1)S(1)} %get-tuple-element.21), channel_id=1, source_target_pairs={{0,1},{1,0},{2,3},{3,2},{4,5},{5,4},{6,7},{7,6},{8,9},{9,8},{10,11... | collective-permute-start | bytes 6316040 | tf_op jit(solution)/shard_map/ppermute | solution.py:232
  17.3 0.0 collective-permute-done.1.refs_2_
  17.3 1.9 %collective-permute-done.refs_0_ = bf16[4,64,128]{2,1,0:T(8,128)(2,1)S(1)} collective-permute-done((bf16[4,64,128]{2,1,0:T(8,128)(2,1)}, bf16[4,64,128]{2,1,0:T(8,128)(2,1)S(1)}, u32[]{:S(2)}, u32[]{:S(2)}) %collective-permute-start) | collective-permute-done | bytes 65568 | tf_op jit(solution)/shard_map/ppermute | solution.py:224
  19.2 0.0 copy-start
  19.2 0.0 copy-start.1
  19.2 0.0 copy-start.2
  19.2 0.0 copy-start.3
  19.2 0.0 copy-start.4
  19.2 0.5 shard_map.92
  19.8 15.9 %all_to_all.20.refs_0_ = bf16[16,64,256]{2,1,0:T(8,128)(2,1)S(1)} all-to-all(bf16[16,64,256]{2,1,0:T(8,128)(2,1)S(1)} %bitcast.16), channel_id=1, replica_groups=mesh['space'=32,'tensor'=16] {'tensor'}, dimensions={0} | all-to-all | bytes 1048576 | tf_op jit(solution)/shard_map/all_to_all | solution.py:244
  35.7 0.0 collective-permute-done.2.refs_6_
  35.7 0.0 copy-done
  35.7 0.0 copy-done.1
  35.7 0.0 copy-done.2
  35.7 0.0 copy-done.3
  35.7 0.0 copy-done.4
  35.7 1.4 %shard_map.93 = bf16[8,2,64,256]{3,2,1,0:T(8,128)(2,1)S(1)} custom-call(bf16[16,64,256]{2,1,0:T(8,128)(2,1)S(1)} %all_to_all.20.refs_0_, f32[2,1024]{1,0:T(2,128)S(1)} %copy-done.2, f32[2,1024]{1,0:T(2,128)S(1)} %copy-done.3, bf16[2,1024,256]{2,1,0:T(8,128)(2,1)S(1)} %copy-done, bf16[2,256,1024]{2,1,0:T(8,128)(2,1)S(1)} %copy-done.1, ...), custom_call_target="tpu_custom_call" | custom-call | tf_op jit(solution)/shard_map/pallas_call | solution.py:19
  37.1 13.5 %all_to_all.21 = bf16[16,64,256]{2,1,0:T(8,128)(2,1)S(1)} all-to-all(bf16[16,64,256]{2,1,0:T(8,128)(2,1)S(1)} %bitcast.12), channel_id=1, replica_groups=mesh['space'=32,'tensor'=16] {'tensor'}, dimensions={0} | all-to-all | bytes 1048576 | tf_op jit(solution)/shard_map/all_to_all | solution.py:251
  50.6 0.1 shard_map.94
  50.7 3.3 %collective-permute-start.3 = (bf16[3,64,128]{2,1,0:T(8,128)(2,1)S(1)}, bf16[3,64,128]{2,1,0:T(8,128)(2,1)S(1)}, u32[]{:S(2)}, u32[]{:S(2)}) collective-permute-start(bf16[3,64,128]{2,1,0:T(8,128)(2,1)S(1)} %get-tuple-element.23), channel_id=1, source_target_pairs={{0,16},{16,32},{32,48},{48,64},{64,80},{80,96},{96,112},{112,128},... | collective-permute-start | bytes 147464 | tf_op jit(solution)/shard_map/ppermute | solution.py:226
  54.0 5.6 %collective-permute-start.4 = (bf16[3,64,128]{2,1,0:T(8,128)(2,1)S(1)}, bf16[3,64,128]{2,1,0:T(8,128)(2,1)S(1)}, u32[]{:S(2)}, u32[]{:S(2)}) collective-permute-start(bf16[3,64,128]{2,1,0:T(8,128)(2,1)S(1)} %get-tuple-element.27), channel_id=1, source_target_pairs={{16,0},{32,16},{48,32},{64,48},{80,64},{96,80},{112,96},{128,112},... | collective-permute-start | bytes 147464 | tf_op jit(solution)/shard_map/ppermute | solution.py:227
  59.5 0.7 shard_map.95
  60.2 0.0 collective-permute-done.3.refs_0_
  60.2 1.2 %collective-permute-done.4.refs_2_ = bf16[3,64,128]{2,1,0:T(8,128)(2,1)S(1)} collective-permute-done((bf16[3,64,128]{2,1,0:T(8,128)(2,1)S(1)}, bf16[3,64,128]{2,1,0:T(8,128)(2,1)S(1)}, u32[]{:S(2)}, u32[]{:S(2)}) %collective-permute-start.4) | collective-permute-done | bytes 49184 | tf_op jit(solution)/shard_map/ppermute | solution.py:227
  61.5 0.5 shard_map.96
  62.0 13.5 %all_to_all.22.refs_0_ = bf16[16,64,256]{2,1,0:T(8,128)(2,1)S(1)} all-to-all(bf16[16,64,256]{2,1,0:T(8,128)(2,1)S(1)} %bitcast.15), channel_id=1, replica_groups=mesh['space'=32,'tensor'=16] {'tensor'}, dimensions={0} | all-to-all | bytes 1048576 | tf_op jit(solution)/shard_map/all_to_all | solution.py:244
  75.5 1.4 %shard_map.97 = bf16[8,2,64,256]{3,2,1,0:T(8,128)(2,1)S(1)} custom-call(bf16[16,64,256]{2,1,0:T(8,128)(2,1)S(1)} %all_to_all.22.refs_0_, f32[2,1024]{1,0:T(2,128)S(1)} %copy-done.2, f32[2,1024]{1,0:T(2,128)S(1)} %copy-done.3, bf16[2,1024,256]{2,1,0:T(8,128)(2,1)S(1)} %copy-done, bf16[2,256,1024]{2,1,0:T(8,128)(2,1)S(1)} %copy-done.1, ...), custom_call_target="tpu_custom_call" | custom-call | tf_op jit(solution)/shard_map/pallas_call | solution.py:19
  76.8 13.5 %all_to_all.23 = bf16[16,64,256]{2,1,0:T(8,128)(2,1)S(1)} all-to-all(bf16[16,64,256]{2,1,0:T(8,128)(2,1)S(1)} %bitcast.11), channel_id=1, replica_groups=mesh['space'=32,'tensor'=16] {'tensor'}, dimensions={0} | all-to-all | bytes 1048576 | tf_op jit(solution)/shard_map/all_to_all | solution.py:251
  90.3 0.7 shard_map.98
Async XLA Ops:
  0.0 17.3 %collective-permute-start.1 = (bf16[4,64,128]{2,1,0:T(8,128)(2,1)}, bf16[4,64,128]{2,1,0:T(8,128)(2,1)S(1)}, u32[]{:S(2)}, u32[]{:S(2)}) collective-permute-start(bf16[4,64,128]{2,1,0:T(8,128)(2,1)} %bitcast.17), channel_id=1, source_target_pairs={{16,32},{32,16},{48,64},{64,48},{80,96},{96,80},{112,128},{128,112... | collective-permute-start | bytes 196616 | tf_op jit(solution)/shard_map/ppermute | solution.py:223
  11.7 7.5 %collective-permute-start = (bf16[4,64,128]{2,1,0:T(8,128)(2,1)}, bf16[4,64,128]{2,1,0:T(8,128)(2,1)S(1)}, u32[]{:S(2)}, u32[]{:S(2)}) collective-permute-start(bf16[4,64,128]{2,1,0:T(8,128)(2,1)} %bitcast.18), channel_id=1, source_target_pairs={{0,16},{16,0},{32,48},{48,32},{64,80},{80,64},{96,112},{112,96},{1... | collective-permute-start | bytes 196616 | tf_op jit(solution)/shard_map/ppermute | solution.py:224
  15.4 20.3 %collective-permute-start.2 = (bf16[2,2056,256]{2,1,0:T(8,128)(2,1)S(1)}, bf16[2,2056,256]{2,1,0:T(8,128)(2,1)S(1)}, u32[]{:S(2)}, u32[]{:S(2)}) collective-permute-start(bf16[2,2056,256]{2,1,0:T(8,128)(2,1)S(1)} %get-tuple-element.21), channel_id=1, source_target_pairs={{0,1},{1,0},{2,3},{3,2},{4,5},{5,4},{6,7},{7,6},{8,9},{9,8},{10,11... | collective-permute-start | bytes 6316040 | tf_op jit(solution)/shard_map/ppermute | solution.py:232
  19.2 16.5 %copy-start = (bf16[2,1024,256]{2,1,0:T(8,128)(2,1)S(1)}, bf16[2,1024,256]{2,1,0:T(8,128)(2,1)}, u32[]{:S(2)}) copy-start(bf16[2,1024,256]{2,1,0:T(8,128)(2,1)} %refs_3_.3) | copy-start | bytes 3145732
  19.2 16.5 %copy-start.1 = (bf16[2,256,1024]{2,1,0:T(8,128)(2,1)S(1)}, bf16[2,256,1024]{2,1,0:T(8,128)(2,1)}, u32[]{:S(2)}) copy-start(bf16[2,256,1024]{2,1,0:T(8,128)(2,1)} %refs_4_.3) | copy-start | bytes 3145732
  19.2 16.5 %copy-start.2 = (f32[2,1024]{1,0:T(2,128)S(1)}, f32[2,1024]{1,0:T(2,128)}, u32[]{:S(2)}) copy-start(f32[2,1024]{1,0:T(2,128)} %refs_1_.3) | copy-start | bytes 24580
  19.2 16.5 %copy-start.3 = (f32[2,1024]{1,0:T(2,128)S(1)}, f32[2,1024]{1,0:T(2,128)}, u32[]{:S(2)}) copy-start(f32[2,1024]{1,0:T(2,128)} %refs_2_.3) | copy-start | bytes 24580
  19.2 16.5 %copy-start.4 = (f32[2,256]{1,0:T(2,128)S(1)}, f32[2,256]{1,0:T(2,128)}, u32[]{:S(2)}) copy-start(f32[2,256]{1,0:T(2,128)} %refs_5_.3) | copy-start | bytes 6148
  50.7 9.6 %collective-permute-start.3 = (bf16[3,64,128]{2,1,0:T(8,128)(2,1)S(1)}, bf16[3,64,128]{2,1,0:T(8,128)(2,1)S(1)}, u32[]{:S(2)}, u32[]{:S(2)}) collective-permute-start(bf16[3,64,128]{2,1,0:T(8,128)(2,1)S(1)} %get-tuple-element.23), channel_id=1, source_target_pairs={{0,16},{16,32},{32,48},{48,64},{64,80},{80,96},{96,112},{112,128},... | collective-permute-start | bytes 147464 | tf_op jit(solution)/shard_map/ppermute | solution.py:226
  54.0 7.5 %collective-permute-start.4 = (bf16[3,64,128]{2,1,0:T(8,128)(2,1)S(1)}, bf16[3,64,128]{2,1,0:T(8,128)(2,1)S(1)}, u32[]{:S(2)}, u32[]{:S(2)}) collective-permute-start(bf16[3,64,128]{2,1,0:T(8,128)(2,1)S(1)} %get-tuple-element.27), channel_id=1, source_target_pairs={{16,0},{32,16},{48,32},{64,48},{80,64},{96,80},{112,96},{128,112},... | collective-permute-start | bytes 147464 | tf_op jit(solution)/shard_map/ppermute | solution.py:227

commit v11 on v9

--- a/solution.py
+++ b/solution.py
@@ -184,25 +184,47 @@
         scatter(part, total, out_ref)
 
 
-def mix_kernel(parts_ref, stream_ref, affine_ref, out_ref, *edge_refs):
-    height, share, width = stream_ref.shape
-    scale, shift = affine_ref[0], affine_ref[1]
-    rows = []
+def mixed_row(r, parts_ref, stream_ref, affine_ref):
+    height, _, width = stream_ref.shape
+    half, at = divmod(r, height // CORES)
+    lanes = slice(width * at, width * (at + 1))
+    mixed = parts_ref[0, half, :, lanes].astype(jnp.float32)
+    for copy in range(1, parts_ref.shape[0]):
+        mixed = mixed + parts_ref[copy, half, :, lanes].astype(jnp.float32)
+    return stream_ref[r].astype(jnp.float32) + affine_ref[0] * (mixed + affine_ref[1])
+
+
+def mix_kernel(parts_ref, stream_ref, affine_ref, out_ref, near_ref, far_ref):
+    height = stream_ref.shape[0]
+    rows = [mixed_row(r, parts_ref, stream_ref, affine_ref) for r in range(height)]
     for r in range(height):
-        half, at = divmod(r, height // CORES)
-        lanes = slice(width * at, width * (at + 1))
-        mixed = parts_ref[0, half, :, lanes].astype(jnp.float32)
-        for copy in range(1, parts_ref.shape[0]):
-            mixed = mixed + parts_ref[copy, half, :, lanes].astype(jnp.float32)
-        rows.append(stream_ref[r].astype(jnp.float32) + scale * (mixed + shift))
         out_ref[r] = rows[r].astype(jnp.bfloat16)
-    if edge_refs:
-        even = even_band()
-        near_ref, far_ref = edge_refs
-        for r in range(HALF):
-            top, bottom = rows[r], rows[height - HALF + r]
-            near_ref[r] = jnp.where(even, bottom, top).astype(jnp.bfloat16)
-            far_ref[r] = jnp.where(even, top, bottom).astype(jnp.bfloat16)
+    even = even_band()
+    for r in range(HALF):
+        top, bottom = rows[r], rows[height - HALF + r]
+        near_ref[r] = jnp.where(even, bottom, top).astype(jnp.bfloat16)
+        far_ref[r] = jnp.where(even, top, bottom).astype(jnp.bfloat16)
+
+
+def last_kernel(parts_ref, stream_ref, affine_ref, out_ref, held_ref, sems):
+    copies = []
+    for r in range(stream_ref.shape[0]):
+        held_ref[r] = mixed_row(r, parts_ref, stream_ref, affine_ref).astype(jnp.bfloat16)
+        copies.append(pltpu.make_async_copy(held_ref.at[r], out_ref.at[r], sems.at[r]))
+        copies[-1].start()
+    for copy in copies:
+        copy.wait()
+
+
+def finish(parts, stream, affine):
+    return pl.pallas_call(
+        last_kernel,
+        out_shape=jax.ShapeDtypeStruct(stream.shape, stream.dtype),
+        in_specs=[VMEM] * 3,
+        out_specs=pl.BlockSpec(memory_space=pltpu.HBM),
+        scratch_shapes=[pltpu.VMEM(stream.shape, stream.dtype), pltpu.SemaphoreType.DMA((stream.shape[0],))],
+        compiler_params=pltpu.CompilerParams(vmem_limit_bytes=16 << 20),
+    )(parts, stream, affine)
 
 
 def per_device(features, depth_kernel, norm_gain, norm_bias, w_expand, b_expand, w_reduce, b_reduce, layer_scale):
@@ -253,7 +275,7 @@
             edge = jax.ShapeDtypeStruct((HALF, share, width), jnp.bfloat16)
             stream, near, far = call(mix_kernel, (whole, edge, edge), partial, stream, affine)
         else:
-            stream = call(mix_kernel, whole, partial, stream, affine)
+            stream = finish(partial, stream, affine)
     return jnp.transpose(stream, (0, 2, 1))
 
 

time: 91 us -> 91 us (level)
    pallas_call x7 -> x6, Pallas kernels: 5.3 us -> 4.6 us  [call(): pl.pallas_call(body, out_shape=outs, in_specs=[VMEM] * len(args), out_spe...]
where the time goes in v11:
time: 91 us; the launch traced here: 90.6 us
  blocking collectives  56.4 us (62%)
  starting transfers between devices  20.8 us (23%)
  Pallas kernels  7.04 us (8%)
  waiting for transfers between devices  6.27 us (7%)
    all_to_all x2, blocking collectives, per_device(): lax.all_to_all(filtered.reshape(members, share, half), 'tensor', 0, 0, ti...  29.4 us
    all_to_all x2, blocking collectives, per_device(): lax.all_to_all(partial.reshape(members, share, half), 'tensor', 0, 0, til...  27 us
    ppermute x2, starting transfers between devices, per_device(): far = lax.ppermute(far, 'space', others)  14.6 us
    pallas_call x6, Pallas kernels, call(): pl.pallas_call(body, out_shape=outs, in_specs=[VMEM] * len(args), out_spe...  4.6 us
    ppermute x2, starting transfers between devices, per_device(): near = lax.ppermute(near, 'space', pairs)  4.25 us
    ppermute x2, waiting for transfers between devices, per_device(): near = lax.ppermute(near, 'space', pairs)  3.16 us
    ppermute x2, waiting for transfers between devices, per_device(): far = lax.ppermute(far, 'space', others)  3.1 us
    ppermute x1, starting transfers between devices, per_device(): pack = lax.ppermute(pack, 'tensor', sibling)  1.92 us
  transfers between devices with their start and end apart: 5, of which 3 were waited for; matrix products, arithmetic and copies ran while one was open for 0% of the time, Pallas kernels for 3%

profile of v11, /device:TPU:56, one launch (start us, length us, event | category | flops | bytes accessed | tf_op | source)
XLA Modules:
  0.0 90.6 jit_solution(9724147328210083114)
XLA Ops:
  0.0 11.7 %collective-permute-start.1 = (bf16[4,64,128]{2,1,0:T(8,128)(2,1)}, bf16[4,64,128]{2,1,0:T(8,128)(2,1)S(1)}, u32[]{:S(2)}, u32[]{:S(2)}) collective-permute-start(bf16[4,64,128]{2,1,0:T(8,128)(2,1)} %bitcast.17), channel_id=1, source_target_pairs={{16,32},{32,16},{48,64},{64,48},{80,96},{96,80},{112,128},{128,112... | collective-permute-start | bytes 196616 | tf_op jit(solution)/shard_map/ppermute | solution.py:245
  11.7 1.9 %collective-permute-start = (bf16[4,64,128]{2,1,0:T(8,128)(2,1)}, bf16[4,64,128]{2,1,0:T(8,128)(2,1)S(1)}, u32[]{:S(2)}, u32[]{:S(2)}) collective-permute-start(bf16[4,64,128]{2,1,0:T(8,128)(2,1)} %bitcast.18), channel_id=1, source_target_pairs={{0,16},{16,0},{32,48},{48,32},{64,80},{80,64},{96,112},{112,96},{1... | collective-permute-start | bytes 196616 | tf_op jit(solution)/shard_map/ppermute | solution.py:246
  13.6 1.7 %shard_map.91 = (f32[49,64,128]{2,1,0:T(8,128)S(1)}, f32[2,64,128]{2,1,0:T(8,128)S(1)}, bf16[4,64,128]{2,1,0:T(8,128)(2,1)S(1)}, bf16[49,2,64]{2,1,0:T(2,128)(2,...) custom-call(bf16[4,64,128]{2,1,0:T(8,128)(2,1)} %bitcast.19, ...), custom_call_target="tpu_custom_call" | custom-call | tf_op jit(solution)/shard_map/pallas_call | solution.py:84
  15.4 1.9 %collective-permute-start.2 = (bf16[2,2056,256]{2,1,0:T(8,128)(2,1)S(1)}, bf16[2,2056,256]{2,1,0:T(8,128)(2,1)S(1)}, u32[]{:S(2)}, u32[]{:S(2)}) collective-permute-start(bf16[2,2056,256]{2,1,0:T(8,128)(2,1)S(1)} %get-tuple-element.21), channel_id=1, source_target_pairs={{0,1},{1,0},{2,3},{3,2},{4,5},{5,4},{6,7},{7,6},{8,9},{9,8},{10,11... | collective-permute-start | bytes 6316040 | tf_op jit(solution)/shard_map/ppermute | solution.py:251
  17.3 0.0 collective-permute-done.1.refs_2_
  17.3 1.9 %collective-permute-done.refs_0_ = bf16[4,64,128]{2,1,0:T(8,128)(2,1)S(1)} collective-permute-done((bf16[4,64,128]{2,1,0:T(8,128)(2,1)}, bf16[4,64,128]{2,1,0:T(8,128)(2,1)S(1)}, u32[]{:S(2)}, u32[]{:S(2)}) %collective-permute-start) | collective-permute-done | bytes 65568 | tf_op jit(solution)/shard_map/ppermute | solution.py:246
  19.2 0.0 copy-start
  19.2 0.0 copy-start.1
  19.2 0.0 copy-start.2
  19.2 0.0 copy-start.3
  19.2 0.0 copy-start.4
  19.2 0.5 shard_map.92
  19.8 15.9 %all_to_all.20.refs_0_ = bf16[16,64,256]{2,1,0:T(8,128)(2,1)S(1)} all-to-all(bf16[16,64,256]{2,1,0:T(8,128)(2,1)S(1)} %bitcast.16), channel_id=1, replica_groups=mesh['space'=32,'tensor'=16] {'tensor'}, dimensions={0} | all-to-all | bytes 1048576 | tf_op jit(solution)/shard_map/all_to_all | solution.py:264
  35.7 0.0 collective-permute-done.2.refs_6_
  35.7 0.0 copy-done
  35.7 0.0 copy-done.1
  35.7 0.0 copy-done.2
  35.7 0.0 copy-done.3
  35.7 0.0 copy-done.4
  35.7 1.4 %shard_map.93 = bf16[8,2,64,256]{3,2,1,0:T(8,128)(2,1)S(1)} custom-call(bf16[16,64,256]{2,1,0:T(8,128)(2,1)S(1)} %all_to_all.20.refs_0_, f32[2,1024]{1,0:T(2,128)S(1)} %copy-done.2, f32[2,1024]{1,0:T(2,128)S(1)} %copy-done.3, bf16[2,1024,256]{2,1,0:T(8,128)(2,1)S(1)} %copy-done, bf16[2,256,1024]{2,1,0:T(8,128)(2,1)S(1)} %copy-done.1, ...), custom_call_target="tpu_custom_call" | custom-call | tf_op jit(solution)/shard_map/pallas_call | solution.py:19
  37.1 13.5 %all_to_all.21 = bf16[16,64,256]{2,1,0:T(8,128)(2,1)S(1)} all-to-all(bf16[16,64,256]{2,1,0:T(8,128)(2,1)S(1)} %bitcast.12), channel_id=1, replica_groups=mesh['space'=32,'tensor'=16] {'tensor'}, dimensions={0} | all-to-all | bytes 1048576 | tf_op jit(solution)/shard_map/all_to_all | solution.py:271
  50.6 0.1 shard_map.94
  50.7 2.9 %collective-permute-start.3 = (bf16[3,64,128]{2,1,0:T(8,128)(2,1)S(1)}, bf16[3,64,128]{2,1,0:T(8,128)(2,1)S(1)}, u32[]{:S(2)}, u32[]{:S(2)}) collective-permute-start(bf16[3,64,128]{2,1,0:T(8,128)(2,1)S(1)} %get-tuple-element.23), channel_id=1, source_target_pairs={{16,32},{32,16},{48,64},{64,48},{80,96},{96,80},{112,128},{128,112... | collective-permute-start | bytes 147464 | tf_op jit(solution)/shard_map/ppermute | solution.py:245
  53.6 2.3 %collective-permute-start.4 = (bf16[3,64,128]{2,1,0:T(8,128)(2,1)S(1)}, bf16[3,64,128]{2,1,0:T(8,128)(2,1)S(1)}, u32[]{:S(2)}, u32[]{:S(2)}) collective-permute-start(bf16[3,64,128]{2,1,0:T(8,128)(2,1)S(1)} %get-tuple-element.27), channel_id=1, source_target_pairs={{0,16},{16,0},{32,48},{48,32},{64,80},{80,64},{96,112},{112,96},{1... | collective-permute-start | bytes 147464 | tf_op jit(solution)/shard_map/ppermute | solution.py:246
  55.9 0.7 shard_map.95
  56.6 3.1 %collective-permute-done.3.refs_0_ = bf16[3,64,128]{2,1,0:T(8,128)(2,1)S(1)} collective-permute-done((bf16[3,64,128]{2,1,0:T(8,128)(2,1)S(1)}, bf16[3,64,128]{2,1,0:T(8,128)(2,1)S(1)}, u32[]{:S(2)}, u32[]{:S(2)}) %collective-permute-start.3) | collective-permute-done | bytes 49184 | tf_op jit(solution)/shard_map/ppermute | solution.py:245
  59.7 1.3 %collective-permute-done.4.refs_2_ = bf16[3,64,128]{2,1,0:T(8,128)(2,1)S(1)} collective-permute-done((bf16[3,64,128]{2,1,0:T(8,128)(2,1)S(1)}, bf16[3,64,128]{2,1,0:T(8,128)(2,1)S(1)}, u32[]{:S(2)}, u32[]{:S(2)}) %collective-permute-start.4) | collective-permute-done | bytes 49184 | tf_op jit(solution)/shard_map/ppermute | solution.py:246
  61.0 0.5 shard_map.96
  61.5 13.5 %all_to_all.22.refs_0_ = bf16[16,64,256]{2,1,0:T(8,128)(2,1)S(1)} all-to-all(bf16[16,64,256]{2,1,0:T(8,128)(2,1)S(1)} %bitcast.15), channel_id=1, replica_groups=mesh['space'=32,'tensor'=16] {'tensor'}, dimensions={0} | all-to-all | bytes 1048576 | tf_op jit(solution)/shard_map/all_to_all | solution.py:264
  75.0 1.4 %shard_map.97 = bf16[8,2,64,256]{3,2,1,0:T(8,128)(2,1)S(1)} custom-call(bf16[16,64,256]{2,1,0:T(8,128)(2,1)S(1)} %all_to_all.22.refs_0_, f32[2,1024]{1,0:T(2,128)S(1)} %copy-done.2, f32[2,1024]{1,0:T(2,128)S(1)} %copy-done.3, bf16[2,1024,256]{2,1,0:T(8,128)(2,1)S(1)} %copy-done, bf16[2,256,1024]{2,1,0:T(8,128)(2,1)S(1)} %copy-done.1, ...), custom_call_target="tpu_custom_call" | custom-call | tf_op jit(solution)/shard_map/pallas_call | solution.py:19
  76.4 13.5 %all_to_all.23 = bf16[16,64,256]{2,1,0:T(8,128)(2,1)S(1)} all-to-all(bf16[16,64,256]{2,1,0:T(8,128)(2,1)S(1)} %bitcast.11), channel_id=1, replica_groups=mesh['space'=32,'tensor'=16] {'tensor'}, dimensions={0} | all-to-all | bytes 1048576 | tf_op jit(solution)/shard_map/all_to_all | solution.py:271
  89.9 0.7 shard_map.98
Async XLA Ops:
  0.0 17.3 %collective-permute-start.1 = (bf16[4,64,128]{2,1,0:T(8,128)(2,1)}, bf16[4,64,128]{2,1,0:T(8,128)(2,1)S(1)}, u32[]{:S(2)}, u32[]{:S(2)}) collective-permute-start(bf16[4,64,128]{2,1,0:T(8,128)(2,1)} %bitcast.17), channel_id=1, source_target_pairs={{16,32},{32,16},{48,64},{64,48},{80,96},{96,80},{112,128},{128,112... | collective-permute-start | bytes 196616 | tf_op jit(solution)/shard_map/ppermute | solution.py:245
  11.7 7.5 %collective-permute-start = (bf16[4,64,128]{2,1,0:T(8,128)(2,1)}, bf16[4,64,128]{2,1,0:T(8,128)(2,1)S(1)}, u32[]{:S(2)}, u32[]{:S(2)}) collective-permute-start(bf16[4,64,128]{2,1,0:T(8,128)(2,1)} %bitcast.18), channel_id=1, source_target_pairs={{0,16},{16,0},{32,48},{48,32},{64,80},{80,64},{96,112},{112,96},{1... | collective-permute-start | bytes 196616 | tf_op jit(solution)/shard_map/ppermute | solution.py:246
  15.4 20.3 %collective-permute-start.2 = (bf16[2,2056,256]{2,1,0:T(8,128)(2,1)S(1)}, bf16[2,2056,256]{2,1,0:T(8,128)(2,1)S(1)}, u32[]{:S(2)}, u32[]{:S(2)}) collective-permute-start(bf16[2,2056,256]{2,1,0:T(8,128)(2,1)S(1)} %get-tuple-element.21), channel_id=1, source_target_pairs={{0,1},{1,0},{2,3},{3,2},{4,5},{5,4},{6,7},{7,6},{8,9},{9,8},{10,11... | collective-permute-start | bytes 6316040 | tf_op jit(solution)/shard_map/ppermute | solution.py:251
  19.2 16.5 %copy-start = (bf16[2,1024,256]{2,1,0:T(8,128)(2,1)S(1)}, bf16[2,1024,256]{2,1,0:T(8,128)(2,1)}, u32[]{:S(2)}) copy-start(bf16[2,1024,256]{2,1,0:T(8,128)(2,1)} %refs_3_.3) | copy-start | bytes 3145732
  19.2 16.5 %copy-start.1 = (bf16[2,256,1024]{2,1,0:T(8,128)(2,1)S(1)}, bf16[2,256,1024]{2,1,0:T(8,128)(2,1)}, u32[]{:S(2)}) copy-start(bf16[2,256,1024]{2,1,0:T(8,128)(2,1)} %refs_4_.3) | copy-start | bytes 3145732
  19.2 16.5 %copy-start.2 = (f32[2,1024]{1,0:T(2,128)S(1)}, f32[2,1024]{1,0:T(2,128)}, u32[]{:S(2)}) copy-start(f32[2,1024]{1,0:T(2,128)} %refs_1_.3) | copy-start | bytes 24580
  19.2 16.5 %copy-start.3 = (f32[2,1024]{1,0:T(2,128)S(1)}, f32[2,1024]{1,0:T(2,128)}, u32[]{:S(2)}) copy-start(f32[2,1024]{1,0:T(2,128)} %refs_2_.3) | copy-start | bytes 24580
  19.2 16.5 %copy-start.4 = (f32[2,256]{1,0:T(2,128)S(1)}, f32[2,256]{1,0:T(2,128)}, u32[]{:S(2)}) copy-start(f32[2,256]{1,0:T(2,128)} %refs_5_.3) | copy-start | bytes 6148
  50.7 9.0 %collective-permute-start.3 = (bf16[3,64,128]{2,1,0:T(8,128)(2,1)S(1)}, bf16[3,64,128]{2,1,0:T(8,128)(2,1)S(1)}, u32[]{:S(2)}, u32[]{:S(2)}) collective-permute-start(bf16[3,64,128]{2,1,0:T(8,128)(2,1)S(1)} %get-tuple-element.23), channel_id=1, source_target_pairs={{16,32},{32,16},{48,64},{64,48},{80,96},{96,80},{112,128},{128,112... | collective-permute-start | bytes 147464 | tf_op jit(solution)/shard_map/ppermute | solution.py:245
  53.6 7.4 %collective-permute-start.4 = (bf16[3,64,128]{2,1,0:T(8,128)(2,1)S(1)}, bf16[3,64,128]{2,1,0:T(8,128)(2,1)S(1)}, u32[]{:S(2)}, u32[]{:S(2)}) collective-permute-start(bf16[3,64,128]{2,1,0:T(8,128)(2,1)S(1)} %get-tuple-element.27), channel_id=1, source_target_pairs={{0,16},{16,0},{32,48},{48,32},{64,80},{80,64},{96,112},{112,96},{1... | collective-permute-start | bytes 147464 | tf_op jit(solution)/shard_map/ppermute | solution.py:246

commit v12 on v9

--- a/solution.py
+++ b/solution.py
@@ -221,13 +221,14 @@
     near = far = stream
     for block in range(BLOCKS):
         far = lax.ppermute(far, "space", others)
-        near = lax.ppermute(near, "space", pairs)
         if block == 0:
             wide, affine, stream, taps, layer_scale, b_reduce, pack = entered(
                 stream, taps, layer_scale, b_reduce, w_expand, w_reduce, b_expand
             )
+            near = lax.ppermute(stream, "space", pairs)
             pack = lax.ppermute(pack, "tensor", sibling)
         else:
+            near = lax.ppermute(near, "space", pairs)
             stream, next_scale = lax.optimization_barrier((stream, layer_scale))
             wide, affine = call(
                 lambda *refs: spread(1, *refs), spread_shapes(share, width), taps, next_scale, b_reduce

time: 91 us -> 92.5 us (1.016)
  waiting for transfers between devices: 6.27 us -> 8.18 us
    ppermute x0 -> x1, waiting for transfers between devices: none -> 3.39 us  [per_device(): near = lax.ppermute(stream, 'space', pairs)]
    ppermute x2 -> x1, starting transfers between devices: 4.25 us -> 1.92 us  [per_device(): near = lax.ppermute(near, 'space', pairs)]
    ppermute x2 -> x1, waiting for transfers between devices: 3.16 us -> 1.14 us  [per_device(): near = lax.ppermute(near, 'space', pairs)]
    ppermute x0 -> x1, starting transfers between devices: none -> 1.92 us  [per_device(): near = lax.ppermute(stream, 'space', pairs)]
where the time goes in v12:
time: 92.5 us; the launch traced here: 92.1 us
  blocking collectives  56.4 us (61%)
  starting transfers between devices  20.4 us (22%)
  waiting for transfers between devices  8.18 us (9%)
  Pallas kernels  7.01 us (8%)
    all_to_all x2, blocking collectives, per_device(): lax.all_to_all(filtered.reshape(members, share, half), 'tensor', 0, 0, ti...  29.4 us
    all_to_all x2, blocking collectives, per_device(): lax.all_to_all(partial.reshape(members, share, half), 'tensor', 0, 0, til...  27 us
    ppermute x2, starting transfers between devices, per_device(): far = lax.ppermute(far, 'space', others)  14.6 us
    pallas_call x7, Pallas kernels, call(): pl.pallas_call(body, out_shape=outs, in_specs=[VMEM] * len(args), out_spe...  5.3 us
    ppermute x2, waiting for transfers between devices, per_device(): far = lax.ppermute(far, 'space', others)  3.65 us
    ppermute x1, waiting for transfers between devices, per_device(): near = lax.ppermute(stream, 'space', pairs)  3.39 us
    ppermute x1, starting transfers between devices, per_device(): near = lax.ppermute(stream, 'space', pairs)  1.92 us
    ppermute x1, starting transfers between devices, per_device(): pack = lax.ppermute(pack, 'tensor', sibling)  1.92 us
  transfers between devices with their start and end apart: 5, of which 3 were waited for; matrix products, arithmetic and copies ran while one was open for 0% of the time, Pallas kernels for 3%

profile of v12, /device:TPU:56, one launch (start us, length us, event | category | flops | bytes accessed | tf_op | source)
XLA Modules:
  0.0 92.1 jit_solution(4558191547230705938)
XLA Ops:
  0.0 11.7 %collective-permute-start.1 = (bf16[4,64,128]{2,1,0:T(8,128)(2,1)}, bf16[4,64,128]{2,1,0:T(8,128)(2,1)S(1)}, u32[]{:S(2)}, u32[]{:S(2)}) collective-permute-start(bf16[4,64,128]{2,1,0:T(8,128)(2,1)} %bitcast.17), channel_id=1, source_target_pairs={{16,32},{32,16},{48,64},{64,48},{80,96},{96,80},{112,128},{128,112... | collective-permute-start | bytes 196616 | tf_op jit(solution)/shard_map/ppermute | solution.py:223
  11.7 1.7 %shard_map.91 = (f32[49,64,128]{2,1,0:T(8,128)S(1)}, f32[2,64,128]{2,1,0:T(8,128)S(1)}, bf16[4,64,128]{2,1,0:T(8,128)(2,1)S(1)}, bf16[49,2,64]{2,1,0:T(2,128)(2,...) custom-call(bf16[4,64,128]{2,1,0:T(8,128)(2,1)} %bitcast.18, ...), custom_call_target="tpu_custom_call" | custom-call | tf_op jit(solution)/shard_map/pallas_call | solution.py:84
  13.4 1.9 %collective-permute-start = (bf16[4,64,128]{2,1,0:T(8,128)(2,1)S(1)}, bf16[4,64,128]{2,1,0:T(8,128)(2,1)S(1)}, u32[]{:S(2)}, u32[]{:S(2)}) collective-permute-start(bf16[4,64,128]{2,1,0:T(8,128)(2,1)S(1)} %get-tuple-element.19.refs_1_.stream_ref), channel_id=1, source_target_pairs={{0,16},{16,0},{32,48},{48,32},{64,80},{80,64},{96,112},{112,96},{1... | collective-permute-start | bytes 196616 | tf_op jit(solution)/shard_map/ppermute | solution.py:228
  15.4 1.9 %collective-permute-start.2 = (bf16[2,2056,256]{2,1,0:T(8,128)(2,1)S(1)}, bf16[2,2056,256]{2,1,0:T(8,128)(2,1)S(1)}, u32[]{:S(2)}, u32[]{:S(2)}) collective-permute-start(bf16[2,2056,256]{2,1,0:T(8,128)(2,1)S(1)} %get-tuple-element.21), channel_id=1, source_target_pairs={{0,1},{1,0},{2,3},{3,2},{4,5},{5,4},{6,7},{7,6},{8,9},{9,8},{10,11... | collective-permute-start | bytes 6316040 | tf_op jit(solution)/shard_map/ppermute | solution.py:229
  17.3 0.0 collective-permute-done.1.refs_2_
  17.3 3.4 %collective-permute-done.refs_0_ = bf16[4,64,128]{2,1,0:T(8,128)(2,1)S(1)} collective-permute-done((bf16[4,64,128]{2,1,0:T(8,128)(2,1)S(1)}, bf16[4,64,128]{2,1,0:T(8,128)(2,1)S(1)}, u32[]{:S(2)}, u32[]{:S(2)}) %collective-permute-start) | collective-permute-done | bytes 65568 | tf_op jit(solution)/shard_map/ppermute | solution.py:228
  20.7 0.0 copy-start
  20.7 0.0 copy-start.1
  20.7 0.0 copy-start.2
  20.7 0.0 copy-start.3
  20.7 0.0 copy-start.4
  20.7 0.5 shard_map.92
  21.3 15.9 %all_to_all.20.refs_0_ = bf16[16,64,256]{2,1,0:T(8,128)(2,1)S(1)} all-to-all(bf16[16,64,256]{2,1,0:T(8,128)(2,1)S(1)} %bitcast.16), channel_id=1, replica_groups=mesh['space'=32,'tensor'=16] {'tensor'}, dimensions={0} | all-to-all | bytes 1048576 | tf_op jit(solution)/shard_map/all_to_all | solution.py:243
  37.2 0.0 collective-permute-done.2.refs_6_
  37.2 0.0 copy-done
  37.2 0.0 copy-done.1
  37.2 0.0 copy-done.2
  37.2 0.0 copy-done.3
  37.2 0.0 copy-done.4
  37.2 1.4 %shard_map.93 = bf16[8,2,64,256]{3,2,1,0:T(8,128)(2,1)S(1)} custom-call(bf16[16,64,256]{2,1,0:T(8,128)(2,1)S(1)} %all_to_all.20.refs_0_, f32[2,1024]{1,0:T(2,128)S(1)} %copy-done.2, f32[2,1024]{1,0:T(2,128)S(1)} %copy-done.3, bf16[2,1024,256]{2,1,0:T(8,128)(2,1)S(1)} %copy-done, bf16[2,256,1024]{2,1,0:T(8,128)(2,1)S(1)} %copy-done.1, ...), custom_call_target="tpu_custom_call" | custom-call | tf_op jit(solution)/shard_map/pallas_call | solution.py:19
  38.6 13.5 %all_to_all.21 = bf16[16,64,256]{2,1,0:T(8,128)(2,1)S(1)} all-to-all(bf16[16,64,256]{2,1,0:T(8,128)(2,1)S(1)} %bitcast.12), channel_id=1, replica_groups=mesh['space'=32,'tensor'=16] {'tensor'}, dimensions={0} | all-to-all | bytes 1048576 | tf_op jit(solution)/shard_map/all_to_all | solution.py:250
  52.1 0.1 shard_map.94
  52.2 2.9 %collective-permute-start.3 = (bf16[3,64,128]{2,1,0:T(8,128)(2,1)S(1)}, bf16[3,64,128]{2,1,0:T(8,128)(2,1)S(1)}, u32[]{:S(2)}, u32[]{:S(2)}) collective-permute-start(bf16[3,64,128]{2,1,0:T(8,128)(2,1)S(1)} %get-tuple-element.23), channel_id=1, source_target_pairs={{16,32},{32,16},{48,64},{64,48},{80,96},{96,80},{112,128},{128,112... | collective-permute-start | bytes 147464 | tf_op jit(solution)/shard_map/ppermute | solution.py:223
  55.1 1.9 %collective-permute-start.4 = (bf16[3,64,128]{2,1,0:T(8,128)(2,1)S(1)}, bf16[3,64,128]{2,1,0:T(8,128)(2,1)S(1)}, u32[]{:S(2)}, u32[]{:S(2)}) collective-permute-start(bf16[3,64,128]{2,1,0:T(8,128)(2,1)S(1)} %get-tuple-element.27), channel_id=1, source_target_pairs={{0,16},{16,0},{32,48},{48,32},{64,80},{80,64},{96,112},{112,96},{1... | collective-permute-start | bytes 147464 | tf_op jit(solution)/shard_map/ppermute | solution.py:231
  57.0 0.7 shard_map.95
  57.7 3.6 %collective-permute-done.3.refs_0_ = bf16[3,64,128]{2,1,0:T(8,128)(2,1)S(1)} collective-permute-done((bf16[3,64,128]{2,1,0:T(8,128)(2,1)S(1)}, bf16[3,64,128]{2,1,0:T(8,128)(2,1)S(1)}, u32[]{:S(2)}, u32[]{:S(2)}) %collective-permute-start.3) | collective-permute-done | bytes 49184 | tf_op jit(solution)/shard_map/ppermute | solution.py:223
  61.3 1.1 %collective-permute-done.4.refs_2_ = bf16[3,64,128]{2,1,0:T(8,128)(2,1)S(1)} collective-permute-done((bf16[3,64,128]{2,1,0:T(8,128)(2,1)S(1)}, bf16[3,64,128]{2,1,0:T(8,128)(2,1)S(1)}, u32[]{:S(2)}, u32[]{:S(2)}) %collective-permute-start.4) | collective-permute-done | bytes 49184 | tf_op jit(solution)/shard_map/ppermute | solution.py:231
  62.5 0.5 shard_map.96
  63.0 13.5 %all_to_all.22.refs_0_ = bf16[16,64,256]{2,1,0:T(8,128)(2,1)S(1)} all-to-all(bf16[16,64,256]{2,1,0:T(8,128)(2,1)S(1)} %bitcast.15), channel_id=1, replica_groups=mesh['space'=32,'tensor'=16] {'tensor'}, dimensions={0} | all-to-all | bytes 1048576 | tf_op jit(solution)/shard_map/all_to_all | solution.py:243
  76.5 1.4 %shard_map.97 = bf16[8,2,64,256]{3,2,1,0:T(8,128)(2,1)S(1)} custom-call(bf16[16,64,256]{2,1,0:T(8,128)(2,1)S(1)} %all_to_all.22.refs_0_, f32[2,1024]{1,0:T(2,128)S(1)} %copy-done.2, f32[2,1024]{1,0:T(2,128)S(1)} %copy-done.3, bf16[2,1024,256]{2,1,0:T(8,128)(2,1)S(1)} %copy-done, bf16[2,256,1024]{2,1,0:T(8,128)(2,1)S(1)} %copy-done.1, ...), custom_call_target="tpu_custom_call" | custom-call | tf_op jit(solution)/shard_map/pallas_call | solution.py:19
  77.9 13.5 %all_to_all.23 = bf16[16,64,256]{2,1,0:T(8,128)(2,1)S(1)} all-to-all(bf16[16,64,256]{2,1,0:T(8,128)(2,1)S(1)} %bitcast.11), channel_id=1, replica_groups=mesh['space'=32,'tensor'=16] {'tensor'}, dimensions={0} | all-to-all | bytes 1048576 | tf_op jit(solution)/shard_map/all_to_all | solution.py:250
  91.4 0.7 shard_map.98
Async XLA Ops:
  0.0 17.3 %collective-permute-start.1 = (bf16[4,64,128]{2,1,0:T(8,128)(2,1)}, bf16[4,64,128]{2,1,0:T(8,128)(2,1)S(1)}, u32[]{:S(2)}, u32[]{:S(2)}) collective-permute-start(bf16[4,64,128]{2,1,0:T(8,128)(2,1)} %bitcast.17), channel_id=1, source_target_pairs={{16,32},{32,16},{48,64},{64,48},{80,96},{96,80},{112,128},{128,112... | collective-permute-start | bytes 196616 | tf_op jit(solution)/shard_map/ppermute | solution.py:223
  13.4 7.3 %collective-permute-start = (bf16[4,64,128]{2,1,0:T(8,128)(2,1)S(1)}, bf16[4,64,128]{2,1,0:T(8,128)(2,1)S(1)}, u32[]{:S(2)}, u32[]{:S(2)}) collective-permute-start(bf16[4,64,128]{2,1,0:T(8,128)(2,1)S(1)} %get-tuple-element.19.refs_1_.stream_ref), channel_id=1, source_target_pairs={{0,16},{16,0},{32,48},{48,32},{64,80},{80,64},{96,112},{112,96},{1... | collective-permute-start | bytes 196616 | tf_op jit(solution)/shard_map/ppermute | solution.py:228
  15.4 21.8 %collective-permute-start.2 = (bf16[2,2056,256]{2,1,0:T(8,128)(2,1)S(1)}, bf16[2,2056,256]{2,1,0:T(8,128)(2,1)S(1)}, u32[]{:S(2)}, u32[]{:S(2)}) collective-permute-start(bf16[2,2056,256]{2,1,0:T(8,128)(2,1)S(1)} %get-tuple-element.21), channel_id=1, source_target_pairs={{0,1},{1,0},{2,3},{3,2},{4,5},{5,4},{6,7},{7,6},{8,9},{9,8},{10,11... | collective-permute-start | bytes 6316040 | tf_op jit(solution)/shard_map/ppermute | solution.py:229
  20.7 16.5 %copy-start = (bf16[2,1024,256]{2,1,0:T(8,128)(2,1)S(1)}, bf16[2,1024,256]{2,1,0:T(8,128)(2,1)}, u32[]{:S(2)}) copy-start(bf16[2,1024,256]{2,1,0:T(8,128)(2,1)} %refs_3_.3) | copy-start | bytes 3145732
  20.7 16.5 %copy-start.1 = (bf16[2,256,1024]{2,1,0:T(8,128)(2,1)S(1)}, bf16[2,256,1024]{2,1,0:T(8,128)(2,1)}, u32[]{:S(2)}) copy-start(bf16[2,256,1024]{2,1,0:T(8,128)(2,1)} %refs_4_.3) | copy-start | bytes 3145732
  20.7 16.5 %copy-start.2 = (f32[2,1024]{1,0:T(2,128)S(1)}, f32[2,1024]{1,0:T(2,128)}, u32[]{:S(2)}) copy-start(f32[2,1024]{1,0:T(2,128)} %refs_1_.3) | copy-start | bytes 24580
  20.7 16.5 %copy-start.3 = (f32[2,1024]{1,0:T(2,128)S(1)}, f32[2,1024]{1,0:T(2,128)}, u32[]{:S(2)}) copy-start(f32[2,1024]{1,0:T(2,128)} %refs_2_.3) | copy-start | bytes 24580
  20.7 16.5 %copy-start.4 = (f32[2,256]{1,0:T(2,128)S(1)}, f32[2,256]{1,0:T(2,128)}, u32[]{:S(2)}) copy-start(f32[2,256]{1,0:T(2,128)} %refs_5_.3) | copy-start | bytes 6148
  52.2 9.2 %collective-permute-start.3 = (bf16[3,64,128]{2,1,0:T(8,128)(2,1)S(1)}, bf16[3,64,128]{2,1,0:T(8,128)(2,1)S(1)}, u32[]{:S(2)}, u32[]{:S(2)}) collective-permute-start(bf16[3,64,128]{2,1,0:T(8,128)(2,1)S(1)} %get-tuple-element.23), channel_id=1, source_target_pairs={{16,32},{32,16},{48,64},{64,48},{80,96},{96,80},{112,128},{128,112... | collective-permute-start | bytes 147464 | tf_op jit(solution)/shard_map/ppermute | solution.py:223
  55.1 7.4 %collective-permute-start.4 = (bf16[3,64,128]{2,1,0:T(8,128)(2,1)S(1)}, bf16[3,64,128]{2,1,0:T(8,128)(2,1)S(1)}, u32[]{:S(2)}, u32[]{:S(2)}) collective-permute-start(bf16[3,64,128]{2,1,0:T(8,128)(2,1)S(1)} %get-tuple-element.27), channel_id=1, source_target_pairs={{0,16},{16,0},{32,48},{48,32},{64,80},{80,64},{96,112},{112,96},{1... | collective-permute-start | bytes 147464 | tf_op jit(solution)/shard_map/ppermute | solution.py:231

commit v13 on v9

--- a/solution.py
+++ b/solution.py
@@ -148,14 +148,18 @@
 
 
 def normalized(block, x_ref, gain_ref, bias_ref):
-    x = x_ref[...].reshape(D, x_ref.shape[-1])
-    x = jnp.transpose(x).astype(jnp.float32)
-    mean = jnp.mean(x, axis=-1, keepdims=True)
-    centered = x - mean
-    var = jnp.mean(centered * centered, axis=-1, keepdims=True)
+    whole = jnp.transpose(x_ref[...].reshape(D, x_ref.shape[-1]))
     gain = gain_ref[block : block + 1, :]
     bias = bias_ref[block : block + 1, :]
-    return (centered * lax.rsqrt(var + 1e-06) * gain + bias).astype(jnp.bfloat16)
+    size = 16
+    groups = []
+    for at in range(0, whole.shape[0], size):
+        x = whole[at : at + size, :].astype(jnp.float32)
+        mean = jnp.mean(x, axis=-1, keepdims=True)
+        centered = x - mean
+        var = jnp.mean(centered * centered, axis=-1, keepdims=True)
+        groups.append((centered * lax.rsqrt(var + 1e-06) * gain + bias).astype(jnp.bfloat16))
+    return jnp.concatenate(groups, axis=0)
 
 
 def scatter(part, total, out_ref):

time: 91 us -> 91 us (level)
  no operation moved by 1% of the time
where the time goes in v13:
time: 91 us; the launch traced here: 90.6 us
  blocking collectives  56.4 us (62%)
  starting transfers between devices  20.8 us (23%)
  Pallas kernels  7.01 us (8%)
  waiting for transfers between devices  6.27 us (7%)
    all_to_all x2, blocking collectives, per_device(): lax.all_to_all(filtered.reshape(members, share, half), 'tensor', 0, 0, ti...  29.4 us
    all_to_all x2, blocking collectives, per_device(): lax.all_to_all(partial.reshape(members, share, half), 'tensor', 0, 0, til...  27 us
    ppermute x2, starting transfers between devices, per_device(): far = lax.ppermute(far, 'space', others)  14.6 us
    pallas_call x7, Pallas kernels, call(): pl.pallas_call(body, out_shape=outs, in_specs=[VMEM] * len(args), out_spe...  5.3 us
    ppermute x2, starting transfers between devices, per_device(): near = lax.ppermute(near, 'space', pairs)  4.25 us
    ppermute x2, waiting for transfers between devices, per_device(): near = lax.ppermute(near, 'space', pairs)  3.16 us
    ppermute x2, waiting for transfers between devices, per_device(): far = lax.ppermute(far, 'space', others)  3.1 us
    ppermute x1, starting transfers between devices, per_device(): pack = lax.ppermute(pack, 'tensor', sibling)  1.92 us
  transfers between devices with their start and end apart: 5, of which 3 were waited for; matrix products, arithmetic and copies ran while one was open for 0% of the time, Pallas kernels for 3%

profile of v13, /device:TPU:56, one launch (start us, length us, event | category | flops | bytes accessed | tf_op | source)
XLA Modules:
  0.0 90.6 jit_solution(6481810279598072593)
XLA Ops:
  0.0 11.7 %collective-permute-start.1 = (bf16[4,64,128]{2,1,0:T(8,128)(2,1)}, bf16[4,64,128]{2,1,0:T(8,128)(2,1)S(1)}, u32[]{:S(2)}, u32[]{:S(2)}) collective-permute-start(bf16[4,64,128]{2,1,0:T(8,128)(2,1)} %bitcast.17), channel_id=1, source_target_pairs={{16,32},{32,16},{48,64},{64,48},{80,96},{96,80},{112,128},{128,112... | collective-permute-start | bytes 196616 | tf_op jit(solution)/shard_map/ppermute | solution.py:227
  11.7 1.9 %collective-permute-start = (bf16[4,64,128]{2,1,0:T(8,128)(2,1)}, bf16[4,64,128]{2,1,0:T(8,128)(2,1)S(1)}, u32[]{:S(2)}, u32[]{:S(2)}) collective-permute-start(bf16[4,64,128]{2,1,0:T(8,128)(2,1)} %bitcast.18), channel_id=1, source_target_pairs={{0,16},{16,0},{32,48},{48,32},{64,80},{80,64},{96,112},{112,96},{1... | collective-permute-start | bytes 196616 | tf_op jit(solution)/shard_map/ppermute | solution.py:228
  13.6 1.7 %shard_map.91 = (f32[49,64,128]{2,1,0:T(8,128)S(1)}, f32[2,64,128]{2,1,0:T(8,128)S(1)}, bf16[4,64,128]{2,1,0:T(8,128)(2,1)S(1)}, bf16[49,2,64]{2,1,0:T(2,128)(2,...) custom-call(bf16[4,64,128]{2,1,0:T(8,128)(2,1)} %bitcast.19, ...), custom_call_target="tpu_custom_call" | custom-call | tf_op jit(solution)/shard_map/pallas_call | solution.py:84
  15.4 1.9 %collective-permute-start.2 = (bf16[2,2056,256]{2,1,0:T(8,128)(2,1)S(1)}, bf16[2,2056,256]{2,1,0:T(8,128)(2,1)S(1)}, u32[]{:S(2)}, u32[]{:S(2)}) collective-permute-start(bf16[2,2056,256]{2,1,0:T(8,128)(2,1)S(1)} %get-tuple-element.21), channel_id=1, source_target_pairs={{0,1},{1,0},{2,3},{3,2},{4,5},{5,4},{6,7},{7,6},{8,9},{9,8},{10,11... | collective-permute-start | bytes 6316040 | tf_op jit(solution)/shard_map/ppermute | solution.py:233
  17.3 0.0 collective-permute-done.1.refs_2_
  17.3 1.9 %collective-permute-done.refs_0_ = bf16[4,64,128]{2,1,0:T(8,128)(2,1)S(1)} collective-permute-done((bf16[4,64,128]{2,1,0:T(8,128)(2,1)}, bf16[4,64,128]{2,1,0:T(8,128)(2,1)S(1)}, u32[]{:S(2)}, u32[]{:S(2)}) %collective-permute-start) | collective-permute-done | bytes 65568 | tf_op jit(solution)/shard_map/ppermute | solution.py:228
  19.2 0.0 copy-start
  19.2 0.0 copy-start.1
  19.2 0.0 copy-start.2
  19.2 0.0 copy-start.3
  19.2 0.0 copy-start.4
  19.2 0.5 shard_map.92
  19.8 15.9 %all_to_all.20.refs_0_ = bf16[16,64,256]{2,1,0:T(8,128)(2,1)S(1)} all-to-all(bf16[16,64,256]{2,1,0:T(8,128)(2,1)S(1)} %bitcast.16), channel_id=1, replica_groups=mesh['space'=32,'tensor'=16] {'tensor'}, dimensions={0} | all-to-all | bytes 1048576 | tf_op jit(solution)/shard_map/all_to_all | solution.py:246
  35.7 0.0 collective-permute-done.2.refs_6_
  35.7 0.0 copy-done
  35.7 0.0 copy-done.1
  35.7 0.0 copy-done.2
  35.7 0.0 copy-done.3
  35.7 0.0 copy-done.4
  35.7 1.4 %shard_map.93 = bf16[8,2,64,256]{3,2,1,0:T(8,128)(2,1)S(1)} custom-call(bf16[16,64,256]{2,1,0:T(8,128)(2,1)S(1)} %all_to_all.20.refs_0_, f32[2,1024]{1,0:T(2,128)S(1)} %copy-done.2, f32[2,1024]{1,0:T(2,128)S(1)} %copy-done.3, bf16[2,1024,256]{2,1,0:T(8,128)(2,1)S(1)} %copy-done, bf16[2,256,1024]{2,1,0:T(8,128)(2,1)S(1)} %copy-done.1, ...), custom_call_target="tpu_custom_call" | custom-call | tf_op jit(solution)/shard_map/pallas_call | solution.py:19
  37.1 13.5 %all_to_all.21 = bf16[16,64,256]{2,1,0:T(8,128)(2,1)S(1)} all-to-all(bf16[16,64,256]{2,1,0:T(8,128)(2,1)S(1)} %bitcast.12), channel_id=1, replica_groups=mesh['space'=32,'tensor'=16] {'tensor'}, dimensions={0} | all-to-all | bytes 1048576 | tf_op jit(solution)/shard_map/all_to_all | solution.py:253
  50.6 0.1 shard_map.94
  50.7 2.9 %collective-permute-start.3 = (bf16[3,64,128]{2,1,0:T(8,128)(2,1)S(1)}, bf16[3,64,128]{2,1,0:T(8,128)(2,1)S(1)}, u32[]{:S(2)}, u32[]{:S(2)}) collective-permute-start(bf16[3,64,128]{2,1,0:T(8,128)(2,1)S(1)} %get-tuple-element.23), channel_id=1, source_target_pairs={{16,32},{32,16},{48,64},{64,48},{80,96},{96,80},{112,128},{128,112... | collective-permute-start | bytes 147464 | tf_op jit(solution)/shard_map/ppermute | solution.py:227
  53.6 2.3 %collective-permute-start.4 = (bf16[3,64,128]{2,1,0:T(8,128)(2,1)S(1)}, bf16[3,64,128]{2,1,0:T(8,128)(2,1)S(1)}, u32[]{:S(2)}, u32[]{:S(2)}) collective-permute-start(bf16[3,64,128]{2,1,0:T(8,128)(2,1)S(1)} %get-tuple-element.27), channel_id=1, source_target_pairs={{0,16},{16,0},{32,48},{48,32},{64,80},{80,64},{96,112},{112,96},{1... | collective-permute-start | bytes 147464 | tf_op jit(solution)/shard_map/ppermute | solution.py:228
  55.9 0.7 shard_map.95
  56.6 3.1 %collective-permute-done.3.refs_0_ = bf16[3,64,128]{2,1,0:T(8,128)(2,1)S(1)} collective-permute-done((bf16[3,64,128]{2,1,0:T(8,128)(2,1)S(1)}, bf16[3,64,128]{2,1,0:T(8,128)(2,1)S(1)}, u32[]{:S(2)}, u32[]{:S(2)}) %collective-permute-start.3) | collective-permute-done | bytes 49184 | tf_op jit(solution)/shard_map/ppermute | solution.py:227
  59.7 1.3 %collective-permute-done.4.refs_2_ = bf16[3,64,128]{2,1,0:T(8,128)(2,1)S(1)} collective-permute-done((bf16[3,64,128]{2,1,0:T(8,128)(2,1)S(1)}, bf16[3,64,128]{2,1,0:T(8,128)(2,1)S(1)}, u32[]{:S(2)}, u32[]{:S(2)}) %collective-permute-start.4) | collective-permute-done | bytes 49184 | tf_op jit(solution)/shard_map/ppermute | solution.py:228
  61.0 0.5 shard_map.96
  61.5 13.5 %all_to_all.22.refs_0_ = bf16[16,64,256]{2,1,0:T(8,128)(2,1)S(1)} all-to-all(bf16[16,64,256]{2,1,0:T(8,128)(2,1)S(1)} %bitcast.15), channel_id=1, replica_groups=mesh['space'=32,'tensor'=16] {'tensor'}, dimensions={0} | all-to-all | bytes 1048576 | tf_op jit(solution)/shard_map/all_to_all | solution.py:246
  75.0 1.4 %shard_map.97 = bf16[8,2,64,256]{3,2,1,0:T(8,128)(2,1)S(1)} custom-call(bf16[16,64,256]{2,1,0:T(8,128)(2,1)S(1)} %all_to_all.22.refs_0_, f32[2,1024]{1,0:T(2,128)S(1)} %copy-done.2, f32[2,1024]{1,0:T(2,128)S(1)} %copy-done.3, bf16[2,1024,256]{2,1,0:T(8,128)(2,1)S(1)} %copy-done, bf16[2,256,1024]{2,1,0:T(8,128)(2,1)S(1)} %copy-done.1, ...), custom_call_target="tpu_custom_call" | custom-call | tf_op jit(solution)/shard_map/pallas_call | solution.py:19
  76.4 13.5 %all_to_all.23 = bf16[16,64,256]{2,1,0:T(8,128)(2,1)S(1)} all-to-all(bf16[16,64,256]{2,1,0:T(8,128)(2,1)S(1)} %bitcast.11), channel_id=1, replica_groups=mesh['space'=32,'tensor'=16] {'tensor'}, dimensions={0} | all-to-all | bytes 1048576 | tf_op jit(solution)/shard_map/all_to_all | solution.py:253
  89.9 0.7 shard_map.98
Async XLA Ops:
  0.0 17.3 %collective-permute-start.1 = (bf16[4,64,128]{2,1,0:T(8,128)(2,1)}, bf16[4,64,128]{2,1,0:T(8,128)(2,1)S(1)}, u32[]{:S(2)}, u32[]{:S(2)}) collective-permute-start(bf16[4,64,128]{2,1,0:T(8,128)(2,1)} %bitcast.17), channel_id=1, source_target_pairs={{16,32},{32,16},{48,64},{64,48},{80,96},{96,80},{112,128},{128,112... | collective-permute-start | bytes 196616 | tf_op jit(solution)/shard_map/ppermute | solution.py:227
  11.7 7.5 %collective-permute-start = (bf16[4,64,128]{2,1,0:T(8,128)(2,1)}, bf16[4,64,128]{2,1,0:T(8,128)(2,1)S(1)}, u32[]{:S(2)}, u32[]{:S(2)}) collective-permute-start(bf16[4,64,128]{2,1,0:T(8,128)(2,1)} %bitcast.18), channel_id=1, source_target_pairs={{0,16},{16,0},{32,48},{48,32},{64,80},{80,64},{96,112},{112,96},{1... | collective-permute-start | bytes 196616 | tf_op jit(solution)/shard_map/ppermute | solution.py:228
  15.4 20.3 %collective-permute-start.2 = (bf16[2,2056,256]{2,1,0:T(8,128)(2,1)S(1)}, bf16[2,2056,256]{2,1,0:T(8,128)(2,1)S(1)}, u32[]{:S(2)}, u32[]{:S(2)}) collective-permute-start(bf16[2,2056,256]{2,1,0:T(8,128)(2,1)S(1)} %get-tuple-element.21), channel_id=1, source_target_pairs={{0,1},{1,0},{2,3},{3,2},{4,5},{5,4},{6,7},{7,6},{8,9},{9,8},{10,11... | collective-permute-start | bytes 6316040 | tf_op jit(solution)/shard_map/ppermute | solution.py:233
  19.2 16.5 %copy-start = (bf16[2,1024,256]{2,1,0:T(8,128)(2,1)S(1)}, bf16[2,1024,256]{2,1,0:T(8,128)(2,1)}, u32[]{:S(2)}) copy-start(bf16[2,1024,256]{2,1,0:T(8,128)(2,1)} %refs_3_.3) | copy-start | bytes 3145732
  19.2 16.5 %copy-start.1 = (bf16[2,256,1024]{2,1,0:T(8,128)(2,1)S(1)}, bf16[2,256,1024]{2,1,0:T(8,128)(2,1)}, u32[]{:S(2)}) copy-start(bf16[2,256,1024]{2,1,0:T(8,128)(2,1)} %refs_4_.3) | copy-start | bytes 3145732
  19.2 16.5 %copy-start.2 = (f32[2,1024]{1,0:T(2,128)S(1)}, f32[2,1024]{1,0:T(2,128)}, u32[]{:S(2)}) copy-start(f32[2,1024]{1,0:T(2,128)} %refs_1_.3) | copy-start | bytes 24580
  19.2 16.5 %copy-start.3 = (f32[2,1024]{1,0:T(2,128)S(1)}, f32[2,1024]{1,0:T(2,128)}, u32[]{:S(2)}) copy-start(f32[2,1024]{1,0:T(2,128)} %refs_2_.3) | copy-start | bytes 24580
  19.2 16.5 %copy-start.4 = (f32[2,256]{1,0:T(2,128)S(1)}, f32[2,256]{1,0:T(2,128)}, u32[]{:S(2)}) copy-start(f32[2,256]{1,0:T(2,128)} %refs_5_.3) | copy-start | bytes 6148
  50.7 9.0 %collective-permute-start.3 = (bf16[3,64,128]{2,1,0:T(8,128)(2,1)S(1)}, bf16[3,64,128]{2,1,0:T(8,128)(2,1)S(1)}, u32[]{:S(2)}, u32[]{:S(2)}) collective-permute-start(bf16[3,64,128]{2,1,0:T(8,128)(2,1)S(1)} %get-tuple-element.23), channel_id=1, source_target_pairs={{16,32},{32,16},{48,64},{64,48},{80,96},{96,80},{112,128},{128,112... | collective-permute-start | bytes 147464 | tf_op jit(solution)/shard_map/ppermute | solution.py:227
  53.6 7.4 %collective-permute-start.4 = (bf16[3,64,128]{2,1,0:T(8,128)(2,1)S(1)}, bf16[3,64,128]{2,1,0:T(8,128)(2,1)S(1)}, u32[]{:S(2)}, u32[]{:S(2)}) collective-permute-start(bf16[3,64,128]{2,1,0:T(8,128)(2,1)S(1)} %get-tuple-element.27), channel_id=1, source_target_pairs={{0,16},{16,0},{32,48},{48,32},{64,80},{80,64},{96,112},{112,96},{1... | collective-permute-start | bytes 147464 | tf_op jit(solution)/shard_map/ppermute | solution.py:228
